TPU v7x, 32 devices: a whole 2x2x4 slice. The times are simulated.
32 devices in a mesh: dp: 4 (over y, x), ctx: 2 (over core), tensor: 4 (over z).
Axes of the slice: x: 2, y: 2, z: 4, core: 2. Of those that a mesh axis runs over, the one named last changes fastest.
Arguments:
- hidden: bfloat16 [4, 1024, 1408], P('dp', 'ctx'), may hold values from -6 to 6
- long_skip_input: bfloat16 [4, 1024, 1408], P('dp', 'ctx'), may hold values from -6 to 6
- condition: bfloat16 [4, 1408], P('dp'), may hold values from -6 to 6
- projected_text_tokens: bfloat16 [4, 333, 1024], P('dp'), may hold values from -6 to 6
- sequence_adapter_index: int32 [4], P('dp'), may hold values from 0 to 7
- skip_projection_weight: bfloat16 [2816, 1408], P('tensor', 'dp'), may hold values from -0.109375 to 0.109375
- shift_modulation_weight: bfloat16 [1408, 1408], P('dp'), may hold values from -0.15625 to 0.15625
- self_query_weight: bfloat16 [1408, 1408], P('dp', 'tensor'), may hold values from -0.15625 to 0.15625
- self_key_weight: bfloat16 [1408, 1408], P('dp', 'tensor'), may hold values from -0.15625 to 0.15625
- self_value_weight: bfloat16 [1408, 1408], P('dp', 'tensor'), may hold values from -0.15625 to 0.15625
- attention_output_weight: bfloat16 [1408, 1408], P('tensor', 'dp'), may hold values from -0.625 to 0.625
- cross_query_weight: bfloat16 [1408, 1408], P('dp', 'tensor'), may hold values from -0.15625 to 0.15625
- cross_key_weight: bfloat16 [1024, 1408], P('dp', 'tensor'), may hold values from -0.1875 to 0.1875
- cross_value_weight: bfloat16 [1024, 1408], P('dp', 'tensor'), may hold values from -0.1875 to 0.1875
- cross_output_weight: bfloat16 [1408, 1408], P('tensor', 'dp'), may hold values from -0.4375 to 0.4375
- feedforward_up_weight: bfloat16 [1408, 6144], P('dp', 'tensor'), may hold values from -0.15625 to 0.15625
- feedforward_down_weight: bfloat16 [6144, 1408], P('tensor', 'dp'), may hold values from -0.078125 to 0.078125
- skip_norm_gain: float32 [2816], replicated, may hold values from 0.1 to 1.9
- norm_gain_rows: float32 [3, 1408], replicated, may hold values from 0.1 to 1.9
- adapter_down_factor: bfloat16 [8, 16, 22272], replicated, may hold values from -0.15625 to 0.15625
- adapter_up_factor: bfloat16 [8, 16, 21632], replicated, may hold values from -0.75 to 0.75
- cotangent: bfloat16 [4, 1024, 1408], P('dp', 'ctx'), may hold values from -6 to 6
Outputs:
- block_out: bfloat16 [4, 1024, 1408], P('dp', 'ctx')
- hidden_grad: float32 [4, 1024, 1408], P('dp', 'ctx')
- skip_grad: float32 [4, 1024, 1408], P('dp', 'ctx')
- condition_gradient: float32 [5632], P(('dp', 'ctx', 'tensor'))
- adapter_down_gradient: float32 [2850816], P(('dp', 'ctx', 'tensor'))
- adapter_up_gradient: float32 [2768896], P(('dp', 'ctx', 'tensor'))
Inputs may be any that keep to these rules, and one draw needn't show every extreme that they name: `sequence_adapter_index`: the adapter of each sequence, one of 8.
All inputs are finite; a program needn't handle non-finite values.
Results may differ from a plain program's by a relative error of at most 0.024.
Values may be sent and summed in bfloat16 or wider, within the bound.
A program may use at most 192 MiB of HBM per device.

v0:
```python
from functools import partial

import jax
import jax.numpy as jnp
from jax import lax
from jax.sharding import PartitionSpec as P

MODEL_WIDTH = 1408
HD = 88
FF = 6144
TW = 1024


PRECISE = lax.Precision.HIGHEST
NORM_EPS = 1e-06


def row_norm(values):
    centered = values - jnp.mean(values, axis=-1, keepdims=True)
    inverse = lax.rsqrt(jnp.mean(centered * centered, axis=-1, keepdims=True) + NORM_EPS)
    return (centered * inverse, inverse)


def head_norm(values, head_width):
    shaped = values.reshape(values.shape[:-1] + (values.shape[-1] // head_width, head_width))
    centered = shaped - jnp.mean(shaped, axis=-1, keepdims=True)
    inverse = lax.rsqrt(jnp.mean(centered * centered, axis=-1, keepdims=True) + NORM_EPS)
    return (centered * inverse, inverse)


def norm_back(normal, inverse, grad_normal):
    return inverse * (
        grad_normal
        - jnp.mean(grad_normal, axis=-1, keepdims=True)
        - normal * jnp.mean(grad_normal * normal, axis=-1, keepdims=True)
    )


def split_parts(values):
    if values.dtype == jnp.bfloat16:
        return [values]
    upper_half = values.astype(jnp.bfloat16)
    lower_half = (values - upper_half.astype(jnp.float32)).astype(jnp.bfloat16)
    return [upper_half, lower_half]


def paired_product(form, left, right):
    total = None
    for left_number, left_part in enumerate(split_parts(left)):
        for right_number, right_part in enumerate(split_parts(right)):
            if left_number + right_number < 2:
                term = jnp.einsum(form, left_part, right_part, preferred_element_type=jnp.float32)
                total = term if total is None else total + term
    return total


def lowrank_out(input_list, weight_matrix, down_piece, up_factor_piece):
    frozen_term = jnp.einsum(
        "gtb,bx->gtx", input_list, weight_matrix, preferred_element_type=jnp.float32
    )
    rank_activation = jnp.einsum(
        "snd,srd->snr", input_list, down_piece, preferred_element_type=jnp.float32
    )
    adapter_term = paired_product("dti,dip->dtp", rank_activation, up_factor_piece)
    return (frozen_term + adapter_term, rank_activation)


def lowrank_back(
    input_list,
    weight_matrix,
    down_piece,
    up_factor_piece,
    rank_activation,
    output_gradient,
    want_input,
):
    upper_gradient = paired_product("pmf,pmz->pfz", rank_activation, output_gradient)
    rank_gradient = paired_product("hzu,hlu->hzl", output_gradient, up_factor_piece)
    grad_lower = paired_product("snr,snd->srd", rank_gradient, input_list)
    if want_input:
        input_gradients = paired_product("lga,wa->lgw", output_gradient, weight_matrix)
        input_gradients = input_gradients + paired_product(
            "snr,srd->snd", rank_gradient, down_piece
        )
        return (input_gradients, grad_lower, upper_gradient)
    return (None, grad_lower, upper_gradient)


def attend_forward(query, key_rows, values_in, scale_factor):
    scores = (
        jnp.einsum("snhe,smhe->shnm", query, key_rows, preferred_element_type=jnp.float32)
        * scale_factor
    )
    row_top = jnp.max(scores, axis=-1, keepdims=True)
    exp_scores = jnp.exp(scores - row_top)
    row_total = jnp.sum(exp_scores, axis=-1, keepdims=True)
    attn_probs = (exp_scores / row_total).astype(jnp.bfloat16)
    result = jnp.einsum(
        "shnm,smhe->snhe", attn_probs, values_in, preferred_element_type=jnp.float32
    )
    return (result, row_top + jnp.log(row_total))


def attend_back(query, key_rows, values_in, log_total, grad_result, scale_factor):
    scores = (
        jnp.einsum("snhe,smhe->shnm", query, key_rows, preferred_element_type=jnp.float32)
        * scale_factor
    )
    attn_probs = jnp.exp(scores - log_total)
    grad_probs = jnp.einsum(
        "snhe,smhe->shnm", grad_result, values_in, preferred_element_type=jnp.float32
    )
    row_inner = jnp.sum(attn_probs * grad_probs, axis=-1, keepdims=True)
    grad_scores = (attn_probs * (grad_probs - row_inner)).astype(jnp.bfloat16)
    grad_query = (
        jnp.einsum("shnm,smhe->snhe", grad_scores, key_rows, preferred_element_type=jnp.float32)
        * scale_factor
    )
    grad_keys = (
        jnp.einsum("shnm,snhe->smhe", grad_scores, query, preferred_element_type=jnp.float32)
        * scale_factor
    )
    grad_values = jnp.einsum(
        "shnm,snhe->smhe",
        attn_probs.astype(jnp.bfloat16),
        grad_result,
        preferred_element_type=jnp.float32,
    )
    return (grad_query, grad_keys, grad_values)


def body(
    hidden,
    long_skip_input,
    condition,
    projected_text_tokens,
    sequence_adapter_index,
    skip_projection_weight,
    shift_modulation_weight,
    self_query_weight,
    self_key_weight,
    self_value_weight,
    attention_output_weight,
    cross_query_weight,
    cross_key_weight,
    cross_value_weight,
    cross_output_weight,
    feedforward_up_weight,
    feedforward_down_weight,
    skip_norm_gain,
    norm_gain_rows,
    adapter_down_factor,
    adapter_up_factor,
    cotangent,
):
    (
        skip_projection_weight,
        shift_modulation_weight,
        self_query_weight,
        self_key_weight,
        self_value_weight,
        attention_output_weight,
        cross_query_weight,
        cross_key_weight,
        cross_value_weight,
        cross_output_weight,
        feedforward_up_weight,
        feedforward_down_weight,
    ) = (
        lax.all_gather(skip_projection_weight, "dp", axis=1, tiled=True),
        lax.all_gather(shift_modulation_weight, "dp", axis=0, tiled=True),
        lax.all_gather(self_query_weight, "dp", axis=0, tiled=True),
        lax.all_gather(self_key_weight, "dp", axis=0, tiled=True),
        lax.all_gather(self_value_weight, "dp", axis=0, tiled=True),
        lax.all_gather(attention_output_weight, "dp", axis=1, tiled=True),
        lax.all_gather(cross_query_weight, "dp", axis=0, tiled=True),
        lax.all_gather(cross_key_weight, "dp", axis=0, tiled=True),
        lax.all_gather(cross_value_weight, "dp", axis=0, tiled=True),
        lax.all_gather(cross_output_weight, "dp", axis=1, tiled=True),
        lax.all_gather(feedforward_up_weight, "dp", axis=0, tiled=True),
        lax.all_gather(feedforward_down_weight, "dp", axis=1, tiled=True),
    )
    tensor_rank = lax.axis_index("tensor")
    tensor_count = lax.axis_size("tensor")
    seqs_local = hidden.shape[0]
    tokens_local = hidden.shape[1]
    local_width = self_query_weight.shape[1]
    heads_local = local_width // HD
    ff_local = feedforward_up_weight.shape[1]
    skip_width = skip_projection_weight.shape[0]
    scale_factor = HD ** (-0.5)
    in_sizes = [
        2 * MODEL_WIDTH,
        MODEL_WIDTH,
        MODEL_WIDTH,
        MODEL_WIDTH,
        MODEL_WIDTH,
        MODEL_WIDTH,
        MODEL_WIDTH,
        TW,
        TW,
        MODEL_WIDTH,
        MODEL_WIDTH,
        FF,
    ]
    out_sizes = [MODEL_WIDTH] * 10 + [FF, MODEL_WIDTH]
    input_offsets = [sum(in_sizes[:number]) for number in range(12)]
    output_offsets = [sum(out_sizes[:number]) for number in range(12)]
    select_adapter = (
        sequence_adapter_index[:, None]
        == jnp.arange(adapter_down_factor.shape[0], dtype=jnp.int32)[None, :]
    )
    choose_wide = select_adapter.astype(jnp.float32)
    down_seq = jnp.einsum(
        "fn,nge->fge",
        select_adapter.astype(jnp.bfloat16),
        adapter_down_factor,
        preferred_element_type=jnp.float32,
    ).astype(jnp.bfloat16)
    up_seq = jnp.einsum(
        "fn,nge->fge",
        select_adapter.astype(jnp.bfloat16),
        adapter_up_factor,
        preferred_element_type=jnp.float32,
    ).astype(jnp.bfloat16)

    def down_full(number):
        return down_seq[:, :, input_offsets[number] : input_offsets[number] + in_sizes[number]]

    def up_full(number):
        return up_seq[:, :, output_offsets[number] : output_offsets[number] + out_sizes[number]]

    def down_local(number, span_width):
        return lax.dynamic_slice_in_dim(
            down_seq, input_offsets[number] + tensor_rank * span_width, span_width, 2
        )

    def up_local(number, span_width):
        return lax.dynamic_slice_in_dim(
            up_seq, output_offsets[number] + tensor_rank * span_width, span_width, 2
        )

    def to_slots(grad_piece):
        return jnp.einsum("si,srd->ird", choose_wide, grad_piece, precision=PRECISE)

    joined = jnp.concatenate([hidden, long_skip_input], axis=-1).astype(jnp.float32)
    joined_normal, joined_inverse = row_norm(joined)
    joined_low = (joined_normal * skip_norm_gain).astype(jnp.bfloat16)
    joined_part = lax.dynamic_slice_in_dim(joined_low, tensor_rank * skip_width, skip_width, 2)
    skip_partial, skip_rank = lowrank_out(
        joined_part, skip_projection_weight, down_local(0, skip_width), up_full(0)
    )
    skip_out = lax.psum(skip_partial.astype(jnp.bfloat16), "tensor").astype(jnp.float32)
    act_wide, silu_pull = jax.vjp(jax.nn.silu, condition.astype(jnp.float32))
    act_low = act_wide.astype(jnp.bfloat16)[:, None, :]
    shift_row, mod_rank = lowrank_out(act_low, shift_modulation_weight, down_full(1), up_full(1))
    first_normal, first_inverse = row_norm(skip_out)
    attn_in = (first_normal * norm_gain_rows[0] + shift_row).astype(jnp.bfloat16)
    query_proj, query_rank = lowrank_out(
        attn_in, self_query_weight, down_full(2), up_local(2, local_width)
    )
    key_proj, key_rank = lowrank_out(
        attn_in, self_key_weight, down_full(3), up_local(3, local_width)
    )
    value_proj, value_rank = lowrank_out(
        attn_in, self_value_weight, down_full(4), up_local(4, local_width)
    )
    query_normal, query_inverse = head_norm(query_proj, HD)
    key_normal, key_inverse = head_norm(key_proj, HD)
    query_low = query_normal.astype(jnp.bfloat16)
    key_low = key_normal.astype(jnp.bfloat16).reshape(seqs_local, tokens_local, local_width)
    value_low = value_proj.astype(jnp.bfloat16)
    keys_all, values_all = (
        lax.all_gather(key_low, "ctx", axis=1, tiled=True),
        lax.all_gather(value_low, "ctx", axis=1, tiled=True),
    )
    keys_four = keys_all.reshape(seqs_local, -1, heads_local, HD)
    values_four = values_all.reshape(seqs_local, -1, heads_local, HD)
    attn_result, attn_log = attend_forward(query_low, keys_four, values_four, scale_factor)
    attn_low = attn_result.reshape(seqs_local, tokens_local, local_width).astype(jnp.bfloat16)
    attn_partial, out_rank = lowrank_out(
        attn_low, attention_output_weight, down_local(5, local_width), up_full(5)
    )
    first_res = skip_out + lax.psum(attn_partial.astype(jnp.bfloat16), "tensor").astype(jnp.float32)
    second_normal, second_inverse = row_norm(first_res)
    cross_in = (second_normal * norm_gain_rows[1]).astype(jnp.bfloat16)
    cquery_proj, cquery_rank = lowrank_out(
        cross_in, cross_query_weight, down_full(6), up_local(6, local_width)
    )
    ckey_proj, ckey_rank = lowrank_out(
        projected_text_tokens, cross_key_weight, down_full(7), up_local(7, local_width)
    )
    cvalue_proj, cvalue_rank = lowrank_out(
        projected_text_tokens, cross_value_weight, down_full(8), up_local(8, local_width)
    )
    cquery_normal, cquery_inverse = head_norm(cquery_proj, HD)
    ckey_normal, ckey_inverse = head_norm(ckey_proj, HD)
    cquery_low = cquery_normal.astype(jnp.bfloat16)
    ckey_low = ckey_normal.astype(jnp.bfloat16)
    cvalue_low = cvalue_proj.astype(jnp.bfloat16).reshape(seqs_local, -1, heads_local, HD)
    cross_result, cross_log = attend_forward(cquery_low, ckey_low, cvalue_low, scale_factor)
    cross_low = cross_result.reshape(seqs_local, tokens_local, local_width).astype(jnp.bfloat16)
    cross_partial, cout_rank = lowrank_out(
        cross_low, cross_output_weight, down_local(9, local_width), up_full(9)
    )
    second_res = first_res + lax.psum(cross_partial.astype(jnp.bfloat16), "tensor").astype(
        jnp.float32
    )
    third_normal, third_inverse = row_norm(second_res)
    mlp_in = (third_normal * norm_gain_rows[2]).astype(jnp.bfloat16)
    up_proj, up_rank = lowrank_out(
        mlp_in, feedforward_up_weight, down_full(10), up_local(10, ff_local)
    )
    activated, gelu_pull = jax.vjp(partial(jax.nn.gelu, approximate=True), up_proj)
    activated_low = activated.astype(jnp.bfloat16)
    down_partial, down_rank = lowrank_out(
        activated_low, feedforward_down_weight, down_local(11, ff_local), up_full(11)
    )
    block_out = second_res + lax.psum(down_partial.astype(jnp.bfloat16), "tensor").astype(
        jnp.float32
    )
    grad_act, grad_down_lower, grad_down_upper = lowrank_back(
        activated_low,
        feedforward_down_weight,
        down_local(11, ff_local),
        up_full(11),
        down_rank,
        cotangent,
        True,
    )
    grad_pre = gelu_pull(grad_act)[0].astype(jnp.bfloat16)
    grad_mlp_in, grad_up_lower, grad_up_upper = lowrank_back(
        mlp_in,
        feedforward_up_weight,
        down_full(10),
        up_local(10, ff_local),
        up_rank,
        grad_pre,
        True,
    )
    grad_mlp_in = lax.psum(grad_mlp_in.astype(jnp.bfloat16), "tensor").astype(jnp.float32)
    grad_second = cotangent.astype(jnp.float32) + norm_back(
        third_normal, third_inverse, grad_mlp_in * norm_gain_rows[2]
    )
    grad_cross_low, grad_cout_lower, grad_cout_upper = lowrank_back(
        cross_low,
        cross_output_weight,
        down_local(9, local_width),
        up_full(9),
        cout_rank,
        grad_second.astype(jnp.bfloat16),
        True,
    )
    grad_cross_result = grad_cross_low.astype(jnp.bfloat16).reshape(
        seqs_local, tokens_local, heads_local, HD
    )
    grad_cquery, grad_ckey, grad_cvalue = attend_back(
        cquery_low, ckey_low, cvalue_low, cross_log, grad_cross_result, scale_factor
    )
    grad_cquery_proj = (
        norm_back(cquery_normal, cquery_inverse, grad_cquery)
        .reshape(seqs_local, tokens_local, local_width)
        .astype(jnp.bfloat16)
    )
    grad_ckey_proj = norm_back(ckey_normal, ckey_inverse, grad_ckey).reshape(
        seqs_local, -1, local_width
    )
    none_first, grad_ckey_lower, grad_ckey_upper = lowrank_back(
        projected_text_tokens,
        cross_key_weight,
        down_full(7),
        up_local(7, local_width),
        ckey_rank,
        grad_ckey_proj,
        False,
    )
    none_second, grad_cvalue_lower, grad_cvalue_upper = lowrank_back(
        projected_text_tokens,
        cross_value_weight,
        down_full(8),
        up_local(8, local_width),
        cvalue_rank,
        grad_cvalue.reshape(seqs_local, -1, local_width),
        False,
    )
    grad_cross_in, grad_cquery_lower, grad_cquery_upper = lowrank_back(
        cross_in,
        cross_query_weight,
        down_full(6),
        up_local(6, local_width),
        cquery_rank,
        grad_cquery_proj,
        True,
    )
    grad_cross_in = lax.psum(grad_cross_in.astype(jnp.bfloat16), "tensor").astype(jnp.float32)
    grad_first = grad_second + norm_back(
        second_normal, second_inverse, grad_cross_in * norm_gain_rows[1]
    )
    grad_attn_low, grad_aout_lower, grad_aout_upper = lowrank_back(
        attn_low,
        attention_output_weight,
        down_local(5, local_width),
        up_full(5),
        out_rank,
        grad_first.astype(jnp.bfloat16),
        True,
    )
    grad_attn_result = grad_attn_low.astype(jnp.bfloat16).reshape(
        seqs_local, tokens_local, heads_local, HD
    )
    grad_query, grad_keys_all, grad_values_all = attend_back(
        query_low, keys_four, values_four, attn_log, grad_attn_result, scale_factor
    )
    grad_keys, grad_values = (
        lax.psum_scatter(
            grad_keys_all.reshape(seqs_local, -1, local_width).astype(jnp.bfloat16),
            "ctx",
            scatter_dimension=1,
            tiled=True,
        ).astype(jnp.float32),
        lax.psum_scatter(
            grad_values_all.reshape(seqs_local, -1, local_width).astype(jnp.bfloat16),
            "ctx",
            scatter_dimension=1,
            tiled=True,
        ).astype(jnp.float32),
    )
    grad_query_proj = (
        norm_back(query_normal, query_inverse, grad_query)
        .reshape(seqs_local, tokens_local, local_width)
        .astype(jnp.bfloat16)
    )
    grad_key_proj = (
        norm_back(
            key_normal, key_inverse, grad_keys.reshape(seqs_local, tokens_local, heads_local, HD)
        )
        .reshape(seqs_local, tokens_local, local_width)
        .astype(jnp.bfloat16)
    )
    grad_value_proj = grad_values.astype(jnp.bfloat16)
    grad_in_query, grad_query_lower, grad_query_upper = lowrank_back(
        attn_in,
        self_query_weight,
        down_full(2),
        up_local(2, local_width),
        query_rank,
        grad_query_proj,
        True,
    )
    grad_in_key, grad_key_lower, grad_key_upper = lowrank_back(
        attn_in,
        self_key_weight,
        down_full(3),
        up_local(3, local_width),
        key_rank,
        grad_key_proj,
        True,
    )
    grad_in_value, grad_value_lower, grad_value_upper = lowrank_back(
        attn_in,
        self_value_weight,
        down_full(4),
        up_local(4, local_width),
        value_rank,
        grad_value_proj,
        True,
    )
    grad_attn_in = lax.psum(
        (grad_in_query + grad_in_key + grad_in_value).astype(jnp.bfloat16), "tensor"
    ).astype(jnp.float32)
    grad_shift = jnp.sum(grad_attn_in, axis=1, keepdims=True) / tensor_count
    grad_act_low, grad_mod_lower, grad_mod_upper = lowrank_back(
        act_low, shift_modulation_weight, down_full(1), up_full(1), mod_rank, grad_shift, True
    )
    grad_condition = silu_pull(grad_act_low[:, 0, :])[0]
    grad_skip_out = grad_first + norm_back(
        first_normal, first_inverse, grad_attn_in * norm_gain_rows[0]
    )
    grad_joined_part, grad_skip_lower, grad_skip_upper = lowrank_back(
        joined_part,
        skip_projection_weight,
        down_local(0, skip_width),
        up_full(0),
        skip_rank,
        grad_skip_out.astype(jnp.bfloat16),
        True,
    )
    grad_joined = lax.all_gather(
        grad_joined_part.astype(jnp.bfloat16), "tensor", axis=2, tiled=True
    ).astype(grad_joined_part.dtype)
    grad_joined_full = norm_back(joined_normal, joined_inverse, grad_joined * skip_norm_gain)
    hidden_grad = grad_joined_full[:, :, :MODEL_WIDTH]
    skip_grad = grad_joined_full[:, :, MODEL_WIDTH:]
    lower_factor_parts = [
        (0, grad_skip_lower, True),
        (1, grad_mod_lower, False),
        (2, grad_query_lower, False),
        (3, grad_key_lower, False),
        (4, grad_value_lower, False),
        (5, grad_aout_lower, True),
        (6, grad_cquery_lower, False),
        (7, grad_ckey_lower, False),
        (8, grad_cvalue_lower, False),
        (9, grad_cout_lower, True),
        (10, grad_up_lower, False),
        (11, grad_down_lower, True),
    ]
    upper_factor_parts = [
        (0, grad_skip_upper, False),
        (1, grad_mod_upper, False),
        (2, grad_query_upper, True),
        (3, grad_key_upper, True),
        (4, grad_value_upper, True),
        (5, grad_aout_upper, False),
        (6, grad_cquery_upper, True),
        (7, grad_ckey_upper, True),
        (8, grad_cvalue_upper, True),
        (9, grad_cout_upper, False),
        (10, grad_up_upper, True),
        (11, grad_down_upper, False),
    ]
    slot_total = adapter_down_factor.shape[0]
    rank_total = adapter_down_factor.shape[1]
    cond_buffer = jnp.zeros((lax.axis_size("dp") * seqs_local, MODEL_WIDTH), jnp.float32)
    cond_buffer = lax.dynamic_update_slice_in_dim(
        cond_buffer, grad_condition, lax.axis_index("dp") * seqs_local, 0
    )
    cond_flat = cond_buffer.reshape(-1)

    def dense_table(parts_list, starts, total_width, row_count, slot_pieces):
        table = jnp.zeros((row_count, total_width), jnp.float32)
        for position, (number, grad_piece, is_local) in enumerate(parts_list):
            span_width = grad_piece.shape[2]
            column_start = starts[number] + tensor_rank * span_width if is_local else starts[number]
            table = lax.dynamic_update_slice_in_dim(table, slot_pieces[position], column_start, 1)
        return table

    down_factor_slots = [
        to_slots(grad_piece).reshape(slot_total * rank_total, -1)
        for number, grad_piece, is_local in lower_factor_parts
    ]
    up_factor_slots = [
        to_slots(grad_piece).reshape(slot_total * rank_total, -1)
        for number, grad_piece, is_local in upper_factor_parts
    ]
    down_compact = jnp.concatenate(down_factor_slots, axis=1)
    up_compact = jnp.concatenate(up_factor_slots, axis=1)
    cond_rows, down_rows, up_rows = (
        lax.psum_scatter(
            cond_flat.astype(jnp.bfloat16), ("dp", "ctx"), scatter_dimension=0, tiled=True
        ).astype(jnp.float32),
        lax.psum_scatter(
            down_compact.astype(jnp.bfloat16), ("dp", "ctx"), scatter_dimension=0, tiled=True
        ).astype(jnp.float32),
        lax.psum_scatter(
            up_compact.astype(jnp.bfloat16), ("dp", "ctx"), scatter_dimension=0, tiled=True
        ).astype(jnp.float32),
    )
    row_count = down_rows.shape[0]
    down_widths = [grad_piece.shape[2] for number, grad_piece, is_local in lower_factor_parts]
    up_widths = [grad_piece.shape[2] for number, grad_piece, is_local in upper_factor_parts]
    down_pieces = [
        down_rows[:, sum(down_widths[:position]) : sum(down_widths[: position + 1])]
        for position in range(12)
    ]
    up_pieces = [
        up_rows[:, sum(up_widths[:position]) : sum(up_widths[: position + 1])]
        for position in range(12)
    ]
    down_block = dense_table(
        lower_factor_parts, input_offsets, adapter_down_factor.shape[2], row_count, down_pieces
    ).reshape(-1)
    up_block = dense_table(
        upper_factor_parts, output_offsets, adapter_up_factor.shape[2], row_count, up_pieces
    ).reshape(-1)
    condition_gradient, adapter_down_gradient, adapter_up_gradient = (
        lax.psum_scatter(
            cond_rows.astype(jnp.bfloat16), "tensor", scatter_dimension=0, tiled=True
        ).astype(jnp.float32),
        lax.psum_scatter(
            down_block.astype(jnp.bfloat16), "tensor", scatter_dimension=0, tiled=True
        ).astype(jnp.float32),
        lax.psum_scatter(
            up_block.astype(jnp.bfloat16), "tensor", scatter_dimension=0, tiled=True
        ).astype(jnp.float32),
    )
    return (
        block_out.astype(jnp.bfloat16),
        hidden_grad,
        skip_grad,
        condition_gradient,
        adapter_down_gradient,
        adapter_up_gradient,
    )


def solution(mesh):
    in_specs = (
        P("dp", "ctx", None),
        P("dp", "ctx", None),
        P("dp", None),
        P("dp", None, None),
        P("dp"),
        P("tensor", "dp"),
        P("dp", None),
        P("dp", "tensor"),
        P("dp", "tensor"),
        P("dp", "tensor"),
        P("tensor", "dp"),
        P("dp", "tensor"),
        P("dp", "tensor"),
        P("dp", "tensor"),
        P("tensor", "dp"),
        P("dp", "tensor"),
        P("tensor", "dp"),
        P(),
        P(),
        P(),
        P(),
        P("dp", "ctx", None),
    )
    out_specs = (
        P("dp", "ctx", None),
        P("dp", "ctx", None),
        P("dp", "ctx", None),
        P(("dp", "ctx", "tensor")),
        P(("dp", "ctx", "tensor")),
        P(("dp", "ctx", "tensor")),
    )
    return jax.shard_map(body, mesh=mesh, in_specs=in_specs, out_specs=out_specs, check_vma=False)
```

profile of v0, /device:TPU:0, one launch (start us, length us, event | category | flops | bytes accessed | tf_op | source)
XLA Modules:
  0.0 1049.0 jit_solution(11061848913004036909)
XLA Ops:
  10.1 4.8 fusion.12
  21.7 6.3 fusion.10
  37.6 10.8 %all-gather.9.cloned.1.call-done = bf16[704,1408]{0,1:T(8,128)(2,1)} async-done(((bf16[704,352]{0,1:T(8,128)(2,1)}), bf16[704,1408]{0,1:T(8,128)(2,1)}) %all-gather.9.cloned.1.call-update) | async-done | bytes 1982480 | tf_op jit(solution)/shard_map/all_gather | solution.py:170
  61.2 13.8 %all_gather.47 = bf16[1408,352]{1,0:T(8,128)(2,1)S(1)} all-gather(bf16[352,352]{1,0:T(8,128)(2,1)S(1)} %copy-done.126), channel_id=1, replica_groups=mesh['dp'=4,'ctx'=2,'tensor'=4] {'dp'}, dimensions={0}, use_global_device_ids=true | all-gather | bytes 1239040 | tf_op jit(solution)/shard_map/all_gather | solution.py:174
  75.0 13.3 %all_gather.50 = bf16[1408,352]{1,0:T(8,128)(2,1)} all-gather(bf16[352,352]{1,0:T(8,128)(2,1)} %param.30), channel_id=1, replica_groups=mesh['dp'=4,'ctx'=2,'tensor'=4] {'dp'}, dimensions={0}, use_global_device_ids=true | all-gather | bytes 1239040 | tf_op jit(solution)/shard_map/all_gather | solution.py:173
  88.4 13.4 %all_gather.49 = bf16[1408,352]{1,0:T(8,128)(2,1)} all-gather(bf16[352,352]{1,0:T(8,128)(2,1)S(1)} %copy-done.127), channel_id=1, replica_groups=mesh['dp'=4,'ctx'=2,'tensor'=4] {'dp'}, dimensions={0}, use_global_device_ids=true | all-gather | bytes 1239040 | tf_op jit(solution)/shard_map/all_gather | solution.py:172
  101.8 14.3 %all_gather.52 = bf16[352,1408]{0,1:T(8,128)(2,1)} all-gather(bf16[352,352]{0,1:T(8,128)(2,1)S(1)} %copy.46), channel_id=1, replica_groups=mesh['dp'=4,'ctx'=2,'tensor'=4] {'dp'}, dimensions={1}, use_global_device_ids=true | all-gather | bytes 1239040 | tf_op jit(solution)/shard_map/all_gather | solution.py:175
  122.3 48.8 %all-gather.11.cloned.1.call-done = bf16[1408,1408]{1,0:T(8,128)(2,1)} async-done(((bf16[352,1408]{1,0:T(8,128)(2,1)}), bf16[1408,1408]{1,0:T(8,128)(2,1)}) %all-gather.11.cloned.1.call-update) | async-done | bytes 3964944 | tf_op jit(solution)/shard_map/all_gather | solution.py:171
  212.1 17.5 %all_gather.53 = bf16[1024,352]{0,1:T(8,128)(2,1)S(1)} all-gather(bf16[256,352]{0,1:T(8,128)(2,1)S(1)} %copy-done.134), channel_id=1, replica_groups=mesh['dp'=4,'ctx'=2,'tensor'=4] {'dp'}, dimensions={0}, use_global_device_ids=true | all-gather | bytes 901120 | tf_op jit(solution)/shard_map/all_gather | solution.py:178
  233.1 14.1 %all_gather.55 = bf16[1024,352]{0,1:T(8,128)(2,1)S(1)} all-gather(bf16[256,352]{0,1:T(8,128)(2,1)S(1)} %copy-done.135), channel_id=1, replica_groups=mesh['dp'=4,'ctx'=2,'tensor'=4] {'dp'}, dimensions={0}, use_global_device_ids=true | all-gather | bytes 901120 | tf_op jit(solution)/shard_map/all_gather | solution.py:177
  251.8 13.5 %all_gather.54 = bf16[1408,352]{1,0:T(8,128)(2,1)} all-gather(bf16[352,352]{1,0:T(8,128)(2,1)} %param.33), channel_id=1, replica_groups=mesh['dp'=4,'ctx'=2,'tensor'=4] {'dp'}, dimensions={0}, use_global_device_ids=true | all-gather | bytes 1239040 | tf_op jit(solution)/shard_map/all_gather | solution.py:176
  265.3 15.5 %all_gather.56 = bf16[352,1408]{0,1:T(8,128)(2,1)} all-gather(bf16[352,352]{0,1:T(8,128)(2,1)} %copy.50), channel_id=1, replica_groups=mesh['dp'=4,'ctx'=2,'tensor'=4] {'dp'}, dimensions={1}, use_global_device_ids=true | all-gather | bytes 1239040 | tf_op jit(solution)/shard_map/all_gather | solution.py:179
  309.5 17.3 %all-gather.15.cloned.1.call-done = bf16[1536,1408]{0,1:T(8,128)(2,1)} async-done(((bf16[1536,352]{0,1:T(8,128)(2,1)}), bf16[1536,1408]{0,1:T(8,128)(2,1)}) %all-gather.15.cloned.1.call-update) | async-done | bytes 4325392 | tf_op jit(solution)/shard_map/all_gather | solution.py:181
  326.8 6.9 fusion.93
  334.4 59.5 %all-reduce.18.cloned.1.call-done = bf16[1,512,1408]{2,1,0:T(8,128)(2,1)} async-done(((bf16[1,512,1408]{2,1,0:T(8,128)(2,1)}), bf16[1,512,1408]{2,1,0:T(8,128)(2,1)}) %all-reduce.18.cloned.1.call-update) | async-done | bytes 1441808 | tf_op jit(solution)/shard_map/psum | solution.py:306
  402.5 46.7 %all-gather.13.cloned.1.call-done = bf16[1408,1536]{1,0:T(8,128)(2,1)} async-done(((bf16[352,1536]{1,0:T(8,128)(2,1)}), bf16[1408,1536]{1,0:T(8,128)(2,1)}) %all-gather.13.cloned.1.call-update) | async-done | bytes 4325392 | tf_op jit(solution)/shard_map/all_gather | solution.py:180
  449.3 5.0 fusion.366
  457.1 4.1 fusion.40
  480.2 56.7 %all-reduce.20.cloned.1.call-done = bf16[1,512,1408]{2,1,0:T(8,128)(2,1)} async-done(((bf16[1,512,1408]{2,1,0:T(8,128)(2,1)}), bf16[1,512,1408]{2,1,0:T(8,128)(2,1)}) %all-reduce.20.cloned.1.call-update) | async-done | bytes 1441808 | tf_op jit(solution)/shard_map/psum | solution.py:341
  540.5 4.2 fusion.356
  576.6 50.1 %all-reduce.22.cloned.1.call-done = bf16[1,512,1408]{2,1,0:T(8,128)(2,1)} async-done(((bf16[1,512,1408]{2,1,0:T(8,128)(2,1)}), bf16[1,512,1408]{2,1,0:T(8,128)(2,1)}) %all-reduce.22.cloned.1.call-update) | async-done | bytes 1441808 | tf_op jit(solution)/shard_map/psum | solution.py:395
  689.6 58.6 %all-reduce.24.cloned.1.call-done = bf16[1,512,1408]{2,1,0:T(8,128)(2,1)} async-done(((bf16[1,512,1408]{2,1,0:T(8,128)(2,1)}), bf16[1,512,1408]{2,1,0:T(8,128)(2,1)}) %all-reduce.24.cloned.1.call-update) | async-done | bytes 1441808 | tf_op jit(solution)/shard_map/psum | solution.py:468
  759.3 5.1 concatenate.37
  772.2 6.7 concatenate.36
  784.9 5.3 fusion.367
  804.4 4.3 reduce-scatter.11.cloned.1.call-done
  818.6 41.6 %reduce-scatter.9.cloned.1.call-done = bf16[16,13440]{1,0:T(8,128)(2,1)} async-done(((bf16[128,13440]{1,0:T(8,128)(2,1)}), bf16[16,13440]{1,0:T(8,128)(2,1)}) %reduce-scatter.9.cloned.1.call-update) | async-done | bytes 430096 | tf_op jit(solution)/shard_map/reduce_scatter | solution.py:552
  872.7 24.7 %all-reduce.1 = bf16[5632]{0:T(1024)(128)(2,1)S(1)} all-reduce(bf16[5632]{0:T(1024)(128)(2,1)S(1)} %convert_element_type.1041), channel_id=7, replica_groups=mesh['dp'=4,'ctx'=2,'tensor'=4] {'dp','ctx'}, use_global_device_ids=true, to_apply=%region_46.47.clone | all-reduce | flops 5632 | bytes 22528
  897.5 12.7 %all-reduce.2 = bf16[704]{0:T(1024)(128)(2,1)S(1)} all-reduce(bf16[704]{0:T(1024)(128)(2,1)S(1)} %dynamic-slice.45), channel_id=8, replica_groups=mesh['dp'=4,'ctx'=2,'tensor'=4] {'tensor'}, use_global_device_ids=true, to_apply=%region_47.48.clone | all-reduce | flops 704 | bytes 2816
  910.8 10.7 %all-gather.17.cloned.1.call-done = bf16[512,2816]{0,1:T(8,128)(2,1)} async-done(((bf16[512,704]{0,1:T(8,128)(2,1)}), bf16[512,2816]{0,1:T(8,128)(2,1)}) %all-gather.17.cloned.1.call-update) | async-done | bytes 2883600 | tf_op jit(solution)/shard_map/all_gather | solution.py:488
  921.6 5.1 fusion.6
  940.5 94.4 %all-reduce.26.cloned.1.call-done = (bf16[1,512,1408]{2,1,0:T(8,128)(2,1)}, bf16[356352]{0:T(1024)(128)(2,1)}, bf16[346112]{0:T(1024)(128)(2,1)}) async-done(((bf16[1,512,1408]{2,1,0:T(8,128)(2,1)}, bf16[356352]{0:T(1024)(128)(2,1)}, bf16[346112]{0:T(1024)(128)(2,1)}), (bf16[1,512,1408]{2,1,0:T(8,128)(2,1)}, bf16[356352]{0:T(1024)(128)(2,1)}, bf16[346112]{0:T(1024)(128)(2,1)})) %all-reduce.26.cloned.1.call-update) | async-done | bytes 2846736 | tf_op jit(solution)/shard_map/psum | solution.py:319
  (735 shorter events, 322.5 us)
Async XLA Ops:
  7.2 200.7 %copy-start = (bf16[1,333,1024]{2,1,0:T(8,128)(2,1)S(1)}, bf16[1,333,1024]{2,1,0:T(8,128)(2,1)}, u32[]{:S(2)}) copy-start(bf16[1,333,1024]{2,1,0:T(8,128)(2,1)} %param.25) | copy-start | bytes 2045956
  7.2 41.3 %all-gather.9.cloned.1.call-start = ((), (), s32[]{:S(2)}) async-start(), calls=%async_computation.4 | async-start | bytes 2703360 | tf_op jit(solution)/shard_map/all_gather | solution.py:170
  9.4 109.2 %all-reduce.14.cloned.1.call-start = ((), (), s32[]{:S(2)}) async-start(), calls=%async_computation.5 | async-start | bytes 2883584 | tf_op jit(solution)/shard_map/psum | solution.py:253
  54.2 116.8 %all-gather.11.cloned.1.call-start = ((), (), s32[]{:S(2)}) async-start(), calls=%async_computation.6 | async-start | bytes 4956160 | tf_op jit(solution)/shard_map/all_gather | solution.py:171
  54.9 225.9 %all-reduce.16.cloned.1.call-start = ((), (), s32[]{:S(2)}) async-start(), calls=%async_computation.7 | async-start | bytes 2883584 | tf_op jit(solution)/shard_map/psum | solution.py:284
  56.5 59.5 %copy-start.75 = (bf16[1,16,22272]{2,1,0:T(8,128)(2,1)}, bf16[1,16,22272]{2,1,0:T(8,128)(2,1)S(1)}, u32[]{:S(2)}) copy-start(bf16[1,16,22272]{2,1,0:T(8,128)(2,1)S(1)} %copy.69) | copy-start | bytes 2138116
  58.1 113.0 %copy-start.168 = (f32[1,1408]{1,0:T(1,128)}, f32[1,1408]{1,0:T(1,128)S(1)}, u32[]{:S(2)}) copy-start(f32[1,1408]{1,0:T(1,128)S(1)} %get-tuple-element.52) | copy-start | bytes 16900
  61.2 112.6 %copy-start.140 = (f32[1408]{0:T(1024)}, f32[1408]{0:T(1024)S(1)}, u32[]{:S(2)}) copy-start(f32[1408]{0:T(1024)S(1)} %get-tuple-element.40) | copy-start | bytes 16900
  61.2 222.3 %copy-start.146 = (f32[1408]{0:T(1024)}, f32[1408]{0:T(1024)S(1)}, u32[]{:S(2)}) copy-start(f32[1408]{0:T(1024)S(1)} %get-tuple-element.41) | copy-start | bytes 16900
  75.0 103.4 %copy-start.58 = (bf16[1408,352]{1,0:T(8,128)(2,1)}, bf16[1408,352]{1,0:T(8,128)(2,1)S(1)}, u32[]{:S(2)}) copy-start(bf16[1408,352]{1,0:T(8,128)(2,1)S(1)} %all_gather.47) | copy-start | bytes 2973700
  88.4 82.7 %copy-start.166 = (bf16[1,1408]{1,0:T(2,128)(2,1)S(1)}, bf16[1,1408]{1,0:T(2,128)(2,1)}, u32[]{:S(2)}) copy-start(bf16[1,1408]{1,0:T(2,128)(2,1)} %param.24) | copy-start | bytes 8452
  120.2 54.2 %copy-start.159 = (f32[512]{0:T(512)}, f32[512]{0:T(512)S(1)}, u32[]{:S(2)}) copy-start(f32[512]{0:T(512)S(1)} %broadcast_multiply_fusion.21) | copy-start | bytes 6148
  207.2 119.6 %all-gather.15.cloned.1.call-start = ((), (), s32[]{:S(2)}) async-start(), calls=%async_computation.10 | async-start | bytes 5406720 | tf_op jit(solution)/shard_map/all_gather | solution.py:181
  207.8 186.0 %all-reduce.18.cloned.1.call-start = ((), (), s32[]{:S(2)}) async-start(), calls=%async_computation.8 | async-start | bytes 2883584 | tf_op jit(solution)/shard_map/psum | solution.py:306
  301.1 148.2 %all-gather.13.cloned.1.call-start = ((), (), s32[]{:S(2)}) async-start(), calls=%async_computation.9 | async-start | bytes 5406720 | tf_op jit(solution)/shard_map/all_gather | solution.py:180
  301.8 235.1 %all-reduce.20.cloned.1.call-start = ((), (), s32[]{:S(2)}) async-start(), calls=%async_computation.11 | async-start | bytes 2883584 | tf_op jit(solution)/shard_map/psum | solution.py:341
  399.4 65.7 %copy-start.90 = (f32[512,16]{0,1:T(8,128)}, f32[512,16]{0,1:T(8,128)S(1)}, u32[]{:S(2)}) copy-start(f32[512,16]{0,1:T(8,128)S(1)} %fusion.179) | copy-start | bytes 98308
  472.6 154.2 %all-reduce.22.cloned.1.call-start = ((), (), s32[]{:S(2)}) async-start(), calls=%async_computation.12 | async-start | bytes 2883584 | tf_op jit(solution)/shard_map/psum | solution.py:395
  562.7 102.5 %reduce-scatter.5.cloned.1.call-start = ((), (), s32[]{:S(2)}) async-start(), calls=%async_computation.13 | async-start | bytes 1081344 | tf_op jit(solution)/shard_map/reduce_scatter | solution.py:415
  651.7 23.4 %reduce-scatter.7.cloned.1.call-start = ((), (), s32[]{:S(2)}) async-start(), calls=%async_computation.14 | async-start | bytes 1081344 | tf_op jit(solution)/shard_map/reduce_scatter | solution.py:421
  664.9 83.3 %all-reduce.24.cloned.1.call-start = ((), (), s32[]{:S(2)}) async-start(), calls=%async_computation.15 | async-start | bytes 2883584 | tf_op jit(solution)/shard_map/psum | solution.py:468
  684.0 124.6 %reduce-scatter.11.cloned.1.call-start = ((), (), s32[]{:S(2)}) async-start(), calls=%async_computation.17 | async-start | bytes 3096576 | tf_op jit(solution)/shard_map/reduce_scatter | solution.py:555
  685.7 62.6 %copy-start.141 = (f32[1408]{0:T(1024)S(1)}, f32[1408]{0:T(1024)}, u32[]{:S(2)}) copy-start(f32[1408]{0:T(1024)} %copy-done.140) | copy-start | bytes 16900
  685.7 62.6 %copy-start.160 = (f32[512]{0:T(512)S(1)}, f32[512]{0:T(512)}, u32[]{:S(2)}) copy-start(f32[512]{0:T(512)} %copy-done.159) | copy-start | bytes 6148
  685.7 62.6 %copy-start.176 = (f32[512]{0:T(512)S(1)}, f32[512]{0:T(512)}, u32[]{:S(2)}) copy-start(f32[512]{0:T(512)} %copy-done.175) | copy-start | bytes 6148
  764.4 95.8 %reduce-scatter.9.cloned.1.call-start = ((), (), s32[]{:S(2)}) async-start(), calls=%async_computation.16 | async-start | bytes 3870720 | tf_op jit(solution)/shard_map/reduce_scatter | solution.py:552
  778.9 142.6 %all-gather.17.cloned.1.call-start = ((), (), s32[]{:S(2)}) async-start(), calls=%async_computation.18 | async-start | bytes 3604480 | tf_op jit(solution)/shard_map/all_gather | solution.py:488
  799.6 235.3 %all-reduce.26.cloned.1.call-start = ((), (), s32[]{:S(2)}) async-start(), calls=%async_computation.19 | async-start | bytes 5693440 | tf_op jit(solution)/shard_map/psum | solution.py:319
  860.9 60.6 %copy-start.12 = (bf16[1,512,1408]{1,2,0:T(8,128)(2,1)S(1)}, bf16[1,512,1408]{1,2,0:T(8,128)(2,1)}, u32[]{:S(2)}) copy-start(bf16[1,512,1408]{1,2,0:T(8,128)(2,1)} %copy-done.11) | copy-start | bytes 4325380
  860.9 60.6 %copy-start.156 = (f32[2816]{0:T(1024)S(1)}, f32[2816]{0:T(1024)}, u32[]{:S(2)}) copy-start(f32[2816]{0:T(1024)} %param.39) | copy-start | bytes 33796
  860.9 60.6 %copy-start.164 = (f32[512]{0:T(512)S(1)}, f32[512]{0:T(512)}, u32[]{:S(2)}) copy-start(f32[512]{0:T(512)} %copy-done.163) | copy-start | bytes 6148
  860.9 60.6 %copy-start.181 = (f32[512]{0:T(512)S(1)}, f32[512]{0:T(512)}, u32[]{:S(2)}) copy-start(f32[512]{0:T(512)} %copy-done.180) | copy-start | bytes 6148
  (184 other events, 1150.1 us)
Sparse Core Ops, SparseCore 0:
  9.9 38.5 all-gather.8
  54.3 64.2 all-reduce.13
  120.5 50.5 all-gather.10
  207.4 64.1 all-reduce.15
  273.2 53.5 all-gather.14
  329.6 64.1 all-reduce.17
  395.7 53.5 all-gather.12
  472.7 64.1 all-reduce.19
  562.8 63.9 all-reduce.21
  651.8 7.9 reduce-scatter.4
  665.0 8.1 reduce-scatter.6
  684.1 64.1 all-reduce.23
  764.5 44.0 reduce-scatter.10
  812.4 47.7 reduce-scatter.8
  862.2 59.3 all-gather.16
  924.0 110.9 all-reduce.25
where the time goes:
time: 1060 us; the launch traced here: 1050 us
  waiting for transfers between devices  504 us (48%)
  matrix products  220 us (21%)
  blocking collectives  158 us (15%)
  other arithmetic  74 us (7%)
  local copies, waits for them, and re-layouts  70.8 us (7%)
  between operations  20.6 us (2%)
    dot_general x116, matrix products, paired_product(): jnp.einsum(form, left_part, right_part, preferred_element_type=jnp.float32)  149 us
    psum x1, waiting for transfers between devices, body(): lax.psum(down_partial.astype(jnp.bfloat16), 'tensor').astype(jnp.float32)  94.4 us
    psum x1, waiting for transfers between devices, body(): lax.psum(cross_partial.astype(jnp.bfloat16), 'tensor').astype(jnp.float32)  59.5 us
    psum x1, waiting for transfers between devices, body(): lax.psum((grad_in_query + grad_in_key + grad_in_value).astype(jnp.bfloat1...  58.6 us
    psum x1, waiting for transfers between devices, body(): lax.psum(grad_mlp_in.astype(jnp.bfloat16), 'tensor').astype(jnp.float32)  56.7 us
    psum x1, waiting for transfers between devices, body(): lax.psum(grad_cross_in.astype(jnp.bfloat16), 'tensor').astype(jnp.float32)  50.1 us
    all_gather x1, waiting for transfers between devices, body(): lax.all_gather(shift_modulation_weight, 'dp', axis=0, tiled=True)  48.8 us
    all_gather x1, waiting for transfers between devices, body(): lax.all_gather(feedforward_up_weight, 'dp', axis=0, tiled=True)  46.7 us
  transfers between devices with their start and end apart: 16, of which 13 were waited for; matrix products, arithmetic and copies ran while one was open for 21% of the time, Pallas kernels for 0%

commit v1 on v0

--- a/solution.py
+++ b/solution.py
@@ -3,6 +3,8 @@
 import jax
 import jax.numpy as jnp
 from jax import lax
+from jax.experimental import pallas as pl
+from jax.experimental.pallas import tpu as pltpu
 from jax.sharding import PartitionSpec as P
 
 MODEL_WIDTH = 1408
@@ -594,6 +596,1445 @@
     )
 
 
+BF = jnp.bfloat16
+F32 = jnp.float32
+MESH_ID = pl.DeviceIdType.MESH
+RANK = 16
+VMEM_BYTES = 60 << 20
+
+
+def dot_nn(left, right):
+    return jnp.dot(left, right, preferred_element_type=F32)
+
+
+def dot_nt(left, right):
+    return lax.dot_general(left, right, (((1,), (1,)), ((), ())), preferred_element_type=F32)
+
+
+def dot_tn(left, right):
+    return lax.dot_general(left, right, (((0,), (0,)), ((), ())), preferred_element_type=F32)
+
+
+def stats(values):
+    centered = values - jnp.mean(values, axis=-1, keepdims=True)
+    inverse = lax.rsqrt(jnp.mean(centered * centered, axis=-1, keepdims=True) + NORM_EPS)
+    return centered * inverse, inverse
+
+
+def greet(partners):
+    barrier = pltpu.get_barrier_semaphore()
+    for condition, device in partners:
+        @pl.when(condition)
+        def _(device=device):
+            pl.semaphore_signal(barrier, inc=1, device_id=device, device_id_type=MESH_ID)
+    expected = sum(jnp.where(condition, 1, 0) for condition, _ in partners)
+    pl.semaphore_wait(barrier, expected)
+
+
+def line_partners(me, count):
+    return [(me > 0, {"tensor": lax.max(me - 1, 0)}), (me < count - 1, {"tensor": lax.min(me + 1, count - 1)})]
+
+
+def push(source, target, send_sem, recv_sem, device):
+    return pltpu.make_async_remote_copy(
+        src_ref=source,
+        dst_ref=target,
+        send_sem=send_sem,
+        recv_sem=recv_sem,
+        device_id=device,
+        device_id_type=MESH_ID,
+    )
+
+
+class Line:
+    def __init__(self, me, count, send_right, recv_left, send_left, recv_right):
+        self.me, self.count = me, count
+        self.sems = (send_right, recv_left, send_left, recv_right)
+        self.left = {"tensor": lax.max(me - 1, 0)}
+        self.right = {"tensor": lax.min(me + 1, count - 1)}
+        self.has_left, self.has_right = me > 0, me < count - 1
+
+    def to_right(self, source, target, slot):
+        return push(source, target, self.sems[0].at[slot], self.sems[1].at[slot], self.right)
+
+    def to_left(self, source, target, slot):
+        return push(source, target, self.sems[2].at[slot], self.sems[3].at[slot], self.left)
+
+
+def line_reduce_all(line, steps, compute, partial_ref, from_left, from_right, stage_right, stage_left, finish):
+    me, count = line.me, line.count
+    far = count - 1 - me
+
+    def step(number, carry):
+        @pl.when(number < steps)
+        def _():
+            compute(number)
+
+        slot_r = number - me
+
+        @pl.when((slot_r >= 0) & (slot_r < steps))
+        def _():
+            slot = lax.clamp(0, slot_r, steps - 1)
+
+            @pl.when(line.has_left)
+            def _():
+                line.to_right(stage_right.at[slot], from_left.at[slot], slot).wait_recv()
+
+            @pl.when(line.has_right)
+            def _():
+                @pl.when(line.has_left)
+                def _():
+                    total = partial_ref[slot].astype(F32) + from_left[slot].astype(F32)
+                    stage_right[slot] = total.astype(BF)
+
+                @pl.when(jnp.logical_not(line.has_left))
+                def _():
+                    stage_right[slot] = partial_ref[slot]
+
+                line.to_right(stage_right.at[slot], from_left.at[slot], slot).start()
+
+        slot_l = number - far
+
+        @pl.when((slot_l >= 0) & (slot_l < steps))
+        def _():
+            slot = lax.clamp(0, slot_l, steps - 1)
+
+            @pl.when(line.has_right)
+            def _():
+                line.to_left(stage_left.at[slot], from_right.at[slot], slot).wait_recv()
+
+            @pl.when(line.has_left)
+            def _():
+                @pl.when(line.has_right)
+                def _():
+                    total = partial_ref[slot].astype(F32) + from_right[slot].astype(F32)
+                    stage_left[slot] = total.astype(BF)
+
+                @pl.when(jnp.logical_not(line.has_right))
+                def _():
+                    stage_left[slot] = partial_ref[slot]
+
+                line.to_left(stage_left.at[slot], from_right.at[slot], slot).start()
+
+        slot_f = number - lax.max(me, far)
+
+        @pl.when((slot_f >= 0) & (slot_f < steps))
+        def _():
+            slot = lax.clamp(0, slot_f, steps - 1)
+
+            @pl.when(jnp.logical_not(line.has_left))
+            def _():
+                finish(slot, partial_ref[slot].astype(F32) + from_right[slot].astype(F32))
+
+            @pl.when(line.has_left)
+            def _():
+                @pl.when(line.has_right)
+                def _():
+                    finish(
+                        slot,
+                        partial_ref[slot].astype(F32)
+                        + from_left[slot].astype(F32)
+                        + from_right[slot].astype(F32),
+                    )
+
+                @pl.when(jnp.logical_not(line.has_right))
+                def _():
+                    finish(slot, partial_ref[slot].astype(F32) + from_left[slot].astype(F32))
+
+        return carry
+
+    lax.fori_loop(0, steps + count - 1, step, 0)
+
+    def drain(slot, carry):
+        @pl.when(line.has_right)
+        def _():
+            line.to_right(stage_right.at[slot], from_left.at[slot], slot).wait_send()
+
+        @pl.when(line.has_left)
+        def _():
+            line.to_left(stage_left.at[slot], from_right.at[slot], slot).wait_send()
+
+        return carry
+
+    lax.fori_loop(0, steps, drain, 0)
+
+
+def scatter_order(me, count, place):
+    near = lax.min(me, count - 1 - me)
+    base = count - 1 - 2 * near
+    index = place - base
+    block = jnp.where(
+        place < base,
+        count - 1 - place,
+        jnp.where(index % 2 == 0, 2 * near - index // 2, index // 2),
+    )
+    return jnp.where(2 * me > count - 1, count - 1 - block, block)
+
+
+def line_scatter_step(line, number, partial_ref, from_left, from_right, stage_right, stage_left):
+    me, count = line.me, line.count
+    block_r = count - 1 - number + me
+
+    @pl.when((number >= me) & line.has_right & (block_r > me))
+    def _():
+        block = lax.clamp(0, block_r, count - 1)
+
+        @pl.when(line.has_left)
+        def _():
+            line.to_right(stage_right.at[block], from_left.at[block], block).wait_recv()
+            total = partial_ref[block].astype(F32) + from_left[block].astype(F32)
+            stage_right[block] = total.astype(BF)
+
+        @pl.when(jnp.logical_not(line.has_left))
+        def _():
+            stage_right[block] = partial_ref[block]
+
+        line.to_right(stage_right.at[block], from_left.at[block], block).start()
+
+    block_l = number - (count - 1 - me)
+
+    @pl.when((block_l >= 0) & line.has_left & (block_l < me))
+    def _():
+        block = lax.clamp(0, block_l, count - 1)
+
+        @pl.when(line.has_right)
+        def _():
+            line.to_left(stage_left.at[block], from_right.at[block], block).wait_recv()
+            total = partial_ref[block].astype(F32) + from_right[block].astype(F32)
+            stage_left[block] = total.astype(BF)
+
+        @pl.when(jnp.logical_not(line.has_right))
+        def _():
+            stage_left[block] = partial_ref[block]
+
+        line.to_left(stage_left.at[block], from_right.at[block], block).start()
+
+
+def line_scatter_finish(line, partial_ref, from_left, from_right, stage_right, stage_left, total_ref):
+    me, count = line.me, line.count
+    total_ref[...] = partial_ref[me].astype(F32)
+
+    @pl.when(line.has_left)
+    def _():
+        line.to_right(stage_right.at[me], from_left.at[me], me).wait_recv()
+        total_ref[...] += from_left[me].astype(F32)
+
+    @pl.when(line.has_right)
+    def _():
+        line.to_left(stage_left.at[me], from_right.at[me], me).wait_recv()
+        total_ref[...] += from_right[me].astype(F32)
+
+    def drain(block, carry):
+        @pl.when(block > me)
+        def _():
+            line.to_right(stage_right.at[block], from_left.at[block], block).wait_send()
+
+        @pl.when(block < me)
+        def _():
+            line.to_left(stage_left.at[block], from_right.at[block], block).wait_send()
+
+        return carry
+
+    lax.fori_loop(0, count, drain, 0)
+
+
+def line_gather_step(line, number, slots):
+    me, count = line.me, line.count
+    block_l = lax.clamp(0, me - number, count - 1)
+    block_r = lax.clamp(0, me + number, count - 1)
+
+    @pl.when(number <= me)
+    def _():
+        @pl.when(number > 0)
+        def _():
+            line.to_right(slots.at[block_l], slots.at[block_l], block_l).wait_recv()
+
+        @pl.when(line.has_right)
+        def _():
+            line.to_right(slots.at[block_l], slots.at[block_l], block_l).start()
+
+    @pl.when(me + number <= count - 1)
+    def _():
+        @pl.when(number > 0)
+        def _():
+            line.to_left(slots.at[block_r], slots.at[block_r], block_r).wait_recv()
+
+        @pl.when(line.has_left)
+        def _():
+            line.to_left(slots.at[block_r], slots.at[block_r], block_r).start()
+
+
+def line_gather_drain(line, slots):
+    me, count = line.me, line.count
+
+    def drain(block, carry):
+        @pl.when((block <= me) & line.has_right)
+        def _():
+            line.to_right(slots.at[block], slots.at[block], block).wait_send()
+
+        @pl.when((block >= me) & line.has_left)
+        def _():
+            line.to_left(slots.at[block], slots.at[block], block).wait_send()
+
+        return carry
+
+    lax.fori_loop(0, count, drain, 0)
+
+
+def line_gather(line, slots, compute):
+    me, count = line.me, line.count
+
+    def step(number, carry):
+        line_gather_step(line, number, slots)
+
+        def side(which, inner):
+            block = me + (2 * which - 1) * number
+
+            @pl.when((block >= 0) & (block < count) & ((number > 0) | (which == 0)))
+            def _():
+                compute(lax.clamp(0, block, count - 1))
+
+            return inner
+
+        return lax.fori_loop(0, 2, side, carry)
+
+    lax.fori_loop(0, count, step, 0)
+    line_gather_drain(line, slots)
+
+
+def xor_place(place, number):
+    if number == 0:
+        return place
+    if number == 1:
+        return place + 1 - 2 * (place % 2)
+    if number == 2:
+        return place + 2 - 4 * (place // 2)
+    return 3 - place
+
+
+def assemble(target, own, pieces, offset, sem, lead=None):
+    dp = lax.axis_index("dp")
+    core = lax.axis_index("ctx")
+    rows = own.shape[-2]
+    half = rows // 2
+    copies = []
+
+    def view(ref, start, size, place):
+        if lead is None:
+            return ref.at[pl.ds(start, size), :]
+        return ref.at[lead[place], pl.ds(start, size), :]
+
+    copies.append(
+        pltpu.make_async_copy(
+            view(own, 0, rows, 0), view(target, pl.multiple_of(dp * rows, 16), rows, 1), sem
+        )
+    )
+    first = jnp.where(core == 0, xor_place(dp, 1), xor_place(dp, 2))
+    second = jnp.where(core == 0, xor_place(dp, 2), xor_place(dp, 1))
+    third = xor_place(dp, 3)
+    blocks = (first, second, third, second, first, third)
+    halves = (core, core, core, 1 - core, 1 - core, 1 - core)
+    for piece, block, which in zip(pieces, blocks, halves):
+        start = pl.multiple_of(block * rows + which * half, 16)
+        copies.append(
+            pltpu.make_async_copy(view(piece, offset, half, 0), view(target, start, half, 1), sem)
+        )
+    return copies
+
+
+def call(kernel, inputs, outs, scratch, collective=None, cost=None):
+    space = {True: pltpu.VMEM, False: pl.ANY}
+    return pl.pallas_call(
+        kernel,
+        out_shape=[jax.ShapeDtypeStruct(shape, dtype) for shape, dtype, _ in outs],
+        in_specs=[pl.BlockSpec(memory_space=space[where]) for _, where in inputs],
+        out_specs=[pl.BlockSpec(memory_space=space[where]) for _, _, where in outs],
+        scratch_shapes=scratch,
+        cost_estimate=cost,
+        compiler_params=pltpu.CompilerParams(
+            collective_id=collective,
+            has_side_effects=collective is not None,
+            vmem_limit_bytes=VMEM_BYTES,
+        ),
+    )(*[array for array, _ in inputs])
+
+
+def cost_of(flops, moved):
+    return pl.CostEstimate(flops=int(flops), bytes_accessed=int(moved), transcendentals=0)
+
+
+def vmem(*shape, dtype=BF):
+    return pltpu.VMEM(shape, dtype)
+
+
+def dma(*shape):
+    return pltpu.SemaphoreType.DMA(shape)
+
+
+def whole_wait(target, sem):
+    pltpu.make_async_copy(target, target, sem).wait()
+
+
+def rows_of(index, size):
+    return pl.ds(pl.multiple_of(index * size, size), size)
+
+
+def skip_forward(count, own, pieces, hidden, long_skip, part, part_gain, down, up, gain_row, shift_row):
+    tokens, width = hidden.shape
+    span = part.shape[1]
+    block = min(128, tokens)
+    chunk = min(64, tokens)
+    steps = tokens // chunk
+    each = block // chunk
+
+    def kernel(own_ref, *refs):
+        piece_refs = refs[:6]
+        (hid, lsk, par, pgain, a_ref, b_ref, gain, shift, skip_out, attn_in, w, partial_ref, from_left, from_right,
+         stage_right, stage_left, wsem, *sems) = refs[6:]
+        me = lax.axis_index("tensor")
+        line = Line(me, count, *sems)
+        for copy in assemble(w, own_ref, piece_refs, 0, wsem):
+            copy.start()
+        greet(line_partners(me, count))
+        whole_wait(w, wsem)
+
+        def compute(number):
+            @pl.when(number % each == 0)
+            def _():
+                rows = rows_of(number // each, block)
+                left = hid[rows, :].astype(F32)
+                right = lsk[rows, :].astype(F32)
+                mean = (jnp.sum(left, axis=-1, keepdims=True) + jnp.sum(right, axis=-1, keepdims=True)) / (2 * width)
+                spread = jnp.sum((left - mean) ** 2, axis=-1, keepdims=True)
+                spread += jnp.sum((right - mean) ** 2, axis=-1, keepdims=True)
+                inverse = lax.rsqrt(spread / (2 * width) + NORM_EPS)
+                x = ((par[rows, :].astype(F32) - mean) * inverse * pgain[...]).astype(BF)
+                u = dot_nt(x, a_ref[...]).astype(BF)
+                y = (dot_nt(x, w[...]) + dot_nn(u, b_ref[...])).astype(BF)
+                for piece in range(each):
+                    partial_ref[number + piece] = y[piece * chunk : (piece + 1) * chunk]
+
+        def finish(slot, total):
+            rows = rows_of(slot, chunk)
+            skip_out[rows, :] = total
+            normal, _ = stats(total)
+            attn_in[rows, :] = (normal * gain[...] + shift[...]).astype(BF)
+
+        line_reduce_all(line, steps, compute, partial_ref, from_left, from_right, stage_right, stage_left, finish)
+
+    buffers = [vmem(steps, chunk, width) for _ in range(5)]
+    return call(
+        kernel,
+        [(own, False)] + [(piece, False) for piece in pieces]
+        + [(array, True) for array in (hidden, long_skip, part, part_gain, down, up, gain_row, shift_row)],
+        [((tokens, width), F32, True), ((tokens, width), BF, True)],
+        [vmem(width, span)] + buffers + [dma()] + [dma(steps) for _ in range(4)],
+        collective=1,
+        cost=cost_of(2 * tokens * width * span, 40e6),
+    )
+
+
+def text_forward(heads, text, own_key, own_value, pieces, key_row, value_row, down, up_key, up_value):
+    tokens, width = text.shape
+    local = own_key.shape[1]
+
+    def kernel(own_k, own_v, *refs):
+        piece_refs = refs[:6]
+        t_ref, a_ref, bk, bv, out, w, wsem = refs[6:]
+        core = lax.axis_index("ctx")
+
+        @pl.when(core == 0)
+        def _():
+            for copy in assemble(w, own_k, piece_refs, key_row, wsem):
+                copy.start()
+
+        @pl.when(core == 1)
+        def _():
+            for copy in assemble(w, own_v, piece_refs, value_row, wsem):
+                copy.start()
+
+        whole_wait(w, wsem)
+        x = t_ref[...]
+        u = dot_nt(x, a_ref[...]).astype(BF)
+        y = dot_nn(x, w[...])
+
+        @pl.when(core == 0)
+        def _():
+            z = y + dot_nn(u[:, :RANK], bk[...])
+            for head in range(heads):
+                normal, inverse = stats(z[:, head * HD : (head + 1) * HD])
+                upper = inverse.astype(BF)
+                lower = (inverse - upper.astype(F32)).astype(BF)
+                out[head] = jnp.concatenate([normal.astype(BF), upper, lower], axis=1)
+
+        @pl.when(core == 1)
+        def _():
+            z = (y + dot_nn(u[:, RANK:], bv[...])).astype(BF)
+            filler = jnp.zeros((tokens, 2), BF)
+            for head in range(heads):
+                out[head] = jnp.concatenate([z[:, head * HD : (head + 1) * HD], filler], axis=1)
+
+    return call(
+        kernel,
+        [(own_key, False), (own_value, False)] + [(piece, False) for piece in pieces]
+        + [(array, True) for array in (text, down, up_key, up_value)],
+        [((heads, tokens, HD + 2), BF, True)],
+        [vmem(width, local), dma()],
+        cost=cost_of(2 * tokens * width * local, 3e6),
+    )[0]
+
+
+def attention_forward(count, heads, attn_in, own_list, pieces, offsets, down, ups, out_down, out_up):
+    tokens, width = attn_in.shape
+    local = own_list[0].shape[1]
+    share = tokens // count
+    block = min(128, tokens)
+    scale = HD ** (-0.5)
+
+    def kernel(x_ref, *refs):
+        owns = refs[:4]
+        piece_refs = refs[4:10]
+        (a_ref, bq, bk, bv, ao, bo, q_out, keys, values, low_out, log_out, inv_q, inv_k, summed, wq, wk, wv, wo,
+         partial_ref, from_left, from_right, stage_right, stage_left, wsem, xsend, xrecv, *sems) = refs[10:]
+        me = lax.axis_index("tensor")
+        core = lax.axis_index("ctx")
+        line = Line(me, count, *sems)
+        for number, (w, own) in enumerate(zip((wq, wk, wv, wo), owns)):
+            for copy in assemble(w, own, piece_refs, offsets[number], wsem.at[number]):
+                copy.start()
+        peer = {"ctx": 1 - core}
+        greet(line_partners(me, count) + [(core >= 0, peer)])
+        for number, w in enumerate((wq, wk, wv)):
+            whole_wait(w, wsem.at[number])
+
+        def project(number, carry):
+            rows = rows_of(number, block)
+            x = x_ref[rows, :]
+            u = dot_nt(x, a_ref[...]).astype(BF)
+            yq = dot_nn(x, wq[...]) + dot_nn(u[:, :RANK], bq[...])
+            yk = dot_nn(x, wk[...]) + dot_nn(u[:, RANK : 2 * RANK], bk[...])
+            yv = (dot_nn(x, wv[...]) + dot_nn(u[:, 2 * RANK :], bv[...])).astype(BF)
+            for head in range(heads):
+                span = slice(head * HD, (head + 1) * HD)
+                normal, inverse = stats(yq[:, span])
+                q_out[head, rows, :] = normal.astype(BF)
+                inv_q[head, rows, :] = inverse
+                normal, inverse = stats(yk[:, span])
+                keys[core, head, rows, :] = normal.astype(BF)
+                inv_k[head, rows, :] = inverse
+                values[core, head, rows, :] = yv[:, span]
+            return carry
+
+        lax.fori_loop(0, tokens // block, project, 0)
+        swaps = [
+            push(ref.at[core], ref.at[core], xsend.at[number], xrecv.at[number], peer)
+            for number, ref in enumerate((keys, values))
+        ]
+        for swap in swaps:
+            swap.start()
+        whole_wait(wo, wsem.at[3])
+        for number, ref in enumerate((keys, values)):
+            push(ref.at[1 - core], ref.at[1 - core], xsend.at[number], xrecv.at[number], peer).wait_recv()
+
+        def attend(place, carry):
+            dest = scatter_order(me, count, place)
+            rows = rows_of(dest, share)
+            outs = []
+            for head in range(heads):
+                q = q_out[head, rows, :]
+                s0 = dot_nt(q, keys[0, head]) * scale
+                s1 = dot_nt(q, keys[1, head]) * scale
+                top = jnp.maximum(jnp.max(s0, axis=-1, keepdims=True), jnp.max(s1, axis=-1, keepdims=True))
+                e0 = jnp.exp(s0 - top)
+                e1 = jnp.exp(s1 - top)
+                total = jnp.sum(e0, axis=-1, keepdims=True) + jnp.sum(e1, axis=-1, keepdims=True)
+                share_of = 1.0 / total
+                p0 = (e0 * share_of).astype(BF)
+                p1 = (e1 * share_of).astype(BF)
+                outs.append(dot_nn(p0, values[0, head]) + dot_nn(p1, values[1, head]))
+                log_out[head, rows, :] = top + jnp.log(total)
+            low = jnp.concatenate(outs, axis=1).astype(BF)
+            low_out[rows, :] = low
+            u = dot_nt(low, ao[...]).astype(BF)
+            partial_ref[dest] = (dot_nt(low, wo[...]) + dot_nn(u, bo[...])).astype(BF)
+
+            @pl.when(place < count - 1)
+            def _():
+                line_scatter_step(line, place, partial_ref, from_left, from_right, stage_right, stage_left)
+
+            return carry
+
+        lax.fori_loop(0, count, attend, 0)
+        line_scatter_finish(line, partial_ref, from_left, from_right, stage_right, stage_left, summed)
+        for swap in swaps:
+            swap.wait_send()
+
+    buffers = [vmem(count, share, width) for _ in range(5)]
+    return call(
+        kernel,
+        [(attn_in, True)] + [(own, False) for own in own_list] + [(piece, False) for piece in pieces]
+        + [(array, True) for array in (down, *ups, out_down, out_up)],
+        [
+            ((heads, tokens, HD), BF, True),
+            ((2, heads, tokens, HD), BF, True),
+            ((2, heads, tokens, HD), BF, True),
+            ((tokens, local), BF, True),
+            ((heads, tokens, 1), F32, True),
+            ((heads, tokens, 1), F32, True),
+            ((heads, tokens, 1), F32, True),
+            ((share, width), F32, True),
+        ],
+        [vmem(width, local) for _ in range(4)] + buffers + [dma(4), dma(2), dma(2)] + [dma(count) for _ in range(4)],
+        collective=2,
+        cost=cost_of(8 * tokens * width * local, 60e6),
+    )
+
+
+def cross_forward(count, heads, summed, skip_out, query_stack, out_stack, keys, values, gains, down, up, out_down,
+                  out_up, offsets):
+    share, width = summed.shape
+    local = query_stack[0].shape[-1]
+    scale = HD ** (-0.5)
+    text = keys.shape[2]
+
+    def kernel(sum_ref, skip_ref, *refs):
+        own_q, own_o = refs[:2]
+        piece_refs = refs[2:8]
+        (kc, vc, gain, a_ref, b_ref, ao, bo, first_out, second_out, in_out, mlp_out, q_out, inv_out, log_out, low_out,
+         uo_out, wq, wo, wsem) = refs[8:]
+        me = lax.axis_index("tensor")
+        for number, (w, own) in enumerate(((wq, own_q), (wo, own_o))):
+            for far in range(count):
+                lead = (far, xor_place(me, far))
+                for copy in assemble(w, own, piece_refs, offsets[number], wsem.at[number], lead):
+                    copy.start()
+        first = skip_ref[rows_of(me, share), :] + sum_ref[...]
+        first_out[...] = first
+        normal, _ = stats(first)
+        x = (normal * gain[1:2, :]).astype(BF)
+        in_out[...] = x
+        u = dot_nt(x, a_ref[...]).astype(BF)
+        second_out[...] = first
+        whole_wait(wq, wsem.at[0])
+        whole_wait(wo, wsem.at[1])
+
+        def chunk(place, u_low):
+            y = dot_nn(x, wq[place]) + dot_nn(u, b_ref[place])
+            outs = []
+            for head in range(heads):
+                normal, inverse = stats(y[:, head * HD : (head + 1) * HD])
+                q = normal.astype(BF)
+                q_out[place, head] = q
+                inv_out[place, head] = inverse
+                s = dot_nt(q, kc[place, head, :, :HD]) * scale
+                top = jnp.max(s, axis=-1, keepdims=True)
+                e = jnp.exp(s - top)
+                total = jnp.sum(e, axis=-1, keepdims=True)
+                p = (e * (1.0 / total)).astype(BF)
+                outs.append(dot_nn(p, vc[place, head, :, :HD]))
+                log_out[place, head] = top + jnp.log(total)
+            low = jnp.concatenate(outs, axis=1).astype(BF)
+            low_out[place] = low
+            second_out[...] += dot_nt(low, wo[place])
+            return u_low + dot_nt(low, ao[place])
+
+        u_low = lax.fori_loop(0, count, chunk, jnp.zeros((share, RANK), F32)).astype(BF)
+        uo_out[...] = u_low
+        second = second_out[...] + dot_nn(u_low, bo[...])
+        second_out[...] = second
+        normal, _ = stats(second)
+        mlp_out[...] = (normal * gain[2:3, :]).astype(BF)
+
+    return call(
+        kernel,
+        [(summed, True), (skip_out, True), (query_stack[0], False), (out_stack[0], False)]
+        + [(piece, False) for piece in query_stack[1]]
+        + [(array, True) for array in (keys, values, gains, down, up, out_down, out_up)],
+        [
+            ((share, width), F32, True),
+            ((share, width), F32, True),
+            ((share, width), BF, True),
+            ((share, width), BF, True),
+            ((count, heads, share, HD), BF, True),
+            ((count, heads, share, 1), F32, True),
+            ((count, heads, share, 1), F32, True),
+            ((count, share, local), BF, True),
+            ((share, RANK), BF, True),
+        ],
+        [vmem(count, width, local), vmem(count, width, local), dma(2)],
+        cost=cost_of(4 * share * width * width, 20e6),
+    )
+
+
+def feed_forward(count, block_in, cotangent, second, own_up, own_down, pieces, offsets, up_a, up_b, down_a, down_b):
+    share, width = block_in.shape
+    tokens = cotangent.shape[0]
+    hidden_units = own_up.shape[1]
+
+    def kernel(x_ref, cot, sec, own_u, own_d, *refs):
+        piece_refs = refs[:6]
+        (ua, ub, da, db, summed, down_out, g_ua, g_ub, g_da, g_db, slots, wu, wd, partial_ref, from_left, from_right,
+         stage_right, stage_left, wsem, *sems) = refs[6:]
+        me = lax.axis_index("tensor")
+        gather_line = Line(me, count, *sems[:4])
+        scatter_line = Line(me, count, *sems[4:])
+        for number, (w, own) in enumerate(((wu, own_u), (wd, own_d))):
+            for copy in assemble(w, own, piece_refs, offsets[number], wsem.at[number]):
+                copy.start()
+        slots[me] = x_ref[...]
+        for ref in (g_ua, g_ub, g_da, g_db):
+            ref[...] = jnp.zeros_like(ref)
+        greet(line_partners(me, count))
+        line_gather_step(gather_line, 0, slots)
+        whole_wait(wu, wsem.at[0])
+        whole_wait(wd, wsem.at[1])
+
+        def compute(block):
+            rows = rows_of(block, share)
+            x = slots[block]
+            ct = cot[rows, :]
+            u = dot_nt(x, ua[...]).astype(BF)
+            up = dot_nn(x, wu[...]) + dot_nn(u, ub[...])
+            square = up * up
+            curve = jnp.tanh(0.7978845608028654 * (up + 0.044715 * square * up))
+            half = 0.5 * (1.0 + curve)
+            active = (up * half).astype(BF)
+            slope = half + 0.5 * up * (1.0 - curve * curve) * (0.7978845608028654 * (1.0 + 0.134145 * square))
+            ud = dot_nt(active, da[...]).astype(BF)
+            down = dot_nt(active, wd[...]) + dot_nn(ud, db[...])
+            down_out[rows, :] = down.astype(BF)
+
+            @pl.when(block == me)
+            def _():
+                down_out[rows, :] = (down + sec[...]).astype(BF)
+
+            gd = dot_nt(ct, db[...]).astype(BF)
+            g_active = dot_nn(ct, wd[...]) + dot_nn(gd, da[...])
+            g_up = (g_active * slope).astype(BF)
+            gu = dot_nt(g_up, ub[...]).astype(BF)
+            partial_ref[block] = (dot_nt(g_up, wu[...]) + dot_nn(gu, ua[...])).astype(BF)
+            g_ub[...] += dot_tn(u, g_up)
+            g_ua[...] += dot_tn(gu, x)
+            g_db[...] += dot_tn(ud, ct)
+            g_da[...] += dot_tn(gd, active)
+
+        compute(me)
+
+        def step(number, carry):
+            line_gather_step(gather_line, number, slots)
+
+            def side(which, inner):
+                block = me + (2 * which - 1) * number
+
+                @pl.when((block >= 0) & (block < count))
+                def _():
+                    compute(lax.clamp(0, block, count - 1))
+
+                return inner
+
+            return lax.fori_loop(0, 2, side, carry)
+
+        lax.fori_loop(1, count, step, 0)
+
+        def scatter(number, carry):
+            line_scatter_step(scatter_line, number, partial_ref, from_left, from_right, stage_right, stage_left)
+            return carry
+
+        lax.fori_loop(0, count - 1, scatter, 0)
+        line_gather_drain(gather_line, slots)
+        line_scatter_finish(scatter_line, partial_ref, from_left, from_right, stage_right, stage_left, summed)
+
+    buffers = [vmem(count, share, width) for _ in range(5)]
+    return call(
+        kernel,
+        [(block_in, True), (cotangent, True), (second, True), (own_up, False), (own_down, False)]
+        + [(piece, False) for piece in pieces]
+        + [(array, True) for array in (up_a, up_b, down_a, down_b)],
+        [
+            ((share, width), F32, True),
+            ((tokens, width), BF, True),
+            ((RANK, width), F32, True),
+            ((RANK, hidden_units), F32, True),
+            ((RANK, hidden_units), F32, True),
+            ((RANK, width), F32, True),
+        ],
+        [vmem(count, share, width), vmem(width, hidden_units), vmem(width, hidden_units)]
+        + buffers + [dma(2)] + [dma(count) for _ in range(8)],
+        collective=3,
+        cost=cost_of(8 * tokens * width * hidden_units, 60e6),
+    )
+
+
+def norm_backward(normal, inverse, grad):
+    return inverse * (
+        grad
+        - jnp.mean(grad, axis=-1, keepdims=True)
+        - normal * jnp.mean(grad * normal, axis=-1, keepdims=True)
+    )
+
+
+def cross_backward(count, heads, g_in, cotangent, first, second, block_in, query, inverses, logs, low, u_low, text,
+                   query_stack, out_stack, keys, values, gains, down, up, out_down, out_up, text_down, up_key,
+                   up_value, offsets):
+    share, width = g_in.shape
+    local = query_stack[0].shape[-1]
+    words, text_width = text.shape
+    scale = HD ** (-0.5)
+
+    def kernel(g_ref, cot, first_ref, second_ref, x_ref, q_ref, inv_ref, log_ref, low_ref, uo_ref, t_ref, *refs):
+        own_q, own_o = refs[:2]
+        piece_refs = refs[2:8]
+        (kc, vc, gain, a_ref, b_ref, ao, bo, at, bk, bv, g_first, ga_q, gb_q, ga_k, gb_k, ga_v, gb_v, ga_o, gb_o,
+         acc, wq, wo, wsem) = refs[8:]
+        me = lax.axis_index("tensor")
+        for number, (w, own) in enumerate(((wq, own_q), (wo, own_o))):
+            for far in range(count):
+                lead = (far, xor_place(me, far))
+                for copy in assemble(w, own, piece_refs, offsets[number], wsem.at[number], lead):
+                    copy.start()
+        normal, inverse = stats(second_ref[...])
+        g_second = cot[rows_of(me, share), :].astype(F32) + norm_backward(normal, inverse, g_ref[...] * gain[2:3, :])
+        g_low = g_second.astype(BF)
+        go = dot_nt(g_low, bo[...]).astype(BF)
+        gb_o[...] = dot_tn(uo_ref[...], g_low)
+        x = x_ref[...]
+        uq = dot_nt(x, a_ref[...]).astype(BF)
+        words_in = t_ref[...]
+        ut = dot_nt(words_in, at[...]).astype(BF)
+        uk, uv = ut[:, :RANK], ut[:, RANK:]
+        acc[...] = jnp.zeros_like(acc)
+        whole_wait(wq, wsem.at[0])
+        whole_wait(wo, wsem.at[1])
+
+        def chunk(place, carry):
+            gq_sum, gk_sum, gv_sum = carry
+            g_attn = (dot_nn(g_low, wo[place]) + dot_nn(go, ao[place])).astype(BF)
+            ga_o[place] = dot_tn(go, low_ref[place])
+            gq_parts, gk_parts, gv_parts = [], [], []
+            for head in range(heads):
+                gh = g_attn[:, head * HD : (head + 1) * HD]
+                q = q_ref[place, head]
+                kfull = kc[place, head]
+                k = kfull[:, :HD]
+                v = vc[place, head, :, :HD]
+                p = jnp.exp(dot_nt(q, k) * scale - log_ref[place, head])
+                dp = dot_nt(gh, v)
+                inner = jnp.sum(p * dp, axis=-1, keepdims=True)
+                ds = (p * (dp - inner)).astype(BF)
+                dq = dot_nn(ds, k) * scale
+                dk = dot_tn(ds, q) * scale
+                dv = dot_tn(p.astype(BF), gh)
+                gq_parts.append(norm_backward(q.astype(F32), inv_ref[place, head], dq))
+                inv_k = kfull[:, HD : HD + 1].astype(F32) + kfull[:, HD + 1 : HD + 2].astype(F32)
+                gk_parts.append(norm_backward(k.astype(F32), inv_k, dk))
+                gv_parts.append(dv)
+            gq = jnp.concatenate(gq_parts, axis=1).astype(BF)
+            gk = jnp.concatenate(gk_parts, axis=1).astype(BF)
+            gv = jnp.concatenate(gv_parts, axis=1).astype(BF)
+            acc[...] += dot_nt(gq, wq[place])
+            gb_q[place] = dot_tn(uq, gq)
+            gb_k[place] = dot_tn(uk, gk)
+            gb_v[place] = dot_tn(uv, gv)
+            return (
+                gq_sum + dot_nt(gq, b_ref[place]),
+                gk_sum + dot_nt(gk, bk[place]),
+                gv_sum + dot_nt(gv, bv[place]),
+            )
+
+        start = (jnp.zeros((share, RANK), F32), jnp.zeros((words, RANK), F32), jnp.zeros((words, RANK), F32))
+        gq_sum, gk_sum, gv_sum = lax.fori_loop(0, count, chunk, start)
+        gq_sum = gq_sum.astype(BF)
+        ga_q[...] = dot_tn(gq_sum, x)
+        ga_k[...] = dot_tn(gk_sum.astype(BF), words_in)
+        ga_v[...] = dot_tn(gv_sum.astype(BF), words_in)
+        g_x = acc[...] + dot_nn(gq_sum, a_ref[...])
+        normal, inverse = stats(first_ref[...])
+        g_first[...] = (g_second + norm_backward(normal, inverse, g_x * gain[1:2, :])).astype(BF)
+
+    return call(
+        kernel,
+        [(array, True) for array in (g_in, cotangent, first, second, block_in, query, inverses, logs, low, u_low, text)]
+        + [(query_stack[0], False), (out_stack[0], False)]
+        + [(piece, False) for piece in query_stack[1]]
+        + [(array, True) for array in (keys, values, gains, down, up, out_down, out_up, text_down, up_key, up_value)],
+        [
+            ((share, width), BF, True),
+            ((RANK, width), F32, True),
+            ((count, RANK, local), F32, True),
+            ((RANK, text_width), F32, True),
+            ((count, RANK, local), F32, True),
+            ((RANK, text_width), F32, True),
+            ((count, RANK, local), F32, True),
+            ((count, RANK, local), F32, True),
+            ((RANK, width), F32, True),
+        ],
+        [vmem(share, width, dtype=F32), vmem(count, width, local), vmem(count, width, local), dma(2)],
+        cost=cost_of(8 * share * width * width, 20e6),
+    )
+
+
+def attention_backward(count, heads, g_first, attn_in, query, keys, values, low, logs, inv_q, inv_k, own_list, pieces,
+                       offsets, down, ups, out_down, out_up):
+    share, width = g_first.shape
+    tokens = attn_in.shape[0]
+    local = own_list[0].shape[1]
+    block = min(128, tokens)
+    chunk = min(64, tokens)
+    steps = tokens // chunk
+    each = block // chunk
+    scale = HD ** (-0.5)
+
+    def kernel(g_ref, x_ref, q_ref, k_ref, v_ref, low_ref, log_ref, iq_ref, ik_ref, *refs):
+        owns = refs[:4]
+        piece_refs = refs[4:10]
+        (a_ref, bq, bk, bv, ao, bo, total_out, gall, ga_in, gb_q, gb_k, gb_v, ga_o, gb_o, wq, wk, wv, wo, gq_low, gk_acc,
+         gv_acc, swap_out, swap_in, partial_ref, from_left, from_right, stage_right, stage_left, wsem, xsend, xrecv,
+         *sems) = refs[10:]
+        me = lax.axis_index("tensor")
+        core = lax.axis_index("ctx")
+        peer = {"ctx": 1 - core}
+        gather_line = Line(me, count, *sems[:4])
+        reduce_line = Line(me, count, *sems[4:])
+        for number, (w, own) in enumerate(zip((wq, wk, wv, wo), owns)):
+            for copy in assemble(w, own, piece_refs, offsets[number], wsem.at[number]):
+                copy.start()
+        gall[me] = g_ref[...]
+        for ref in (ga_in, gb_q, gb_k, gb_v, ga_o, gb_o, gk_acc, gv_acc):
+            ref[...] = jnp.zeros_like(ref)
+        greet(line_partners(me, count) + [(core >= 0, peer)])
+        line_gather_step(gather_line, 0, gall)
+        for number, w in enumerate((wq, wk, wv, wo)):
+            whole_wait(w, wsem.at[number])
+
+        def attend(place):
+            rows = rows_of(place, share)
+            g = gall[place]
+            go = dot_nt(g, bo[...]).astype(BF)
+            g_attn = (dot_nn(g, wo[...]) + dot_nn(go, ao[...])).astype(BF)
+            low = low_ref[rows, :]
+            uo = dot_nt(low, ao[...]).astype(BF)
+            gb_o[...] += dot_tn(uo, g)
+            ga_o[...] += dot_tn(go, low)
+            parts = []
+            for head in range(heads):
+                gh = g_attn[:, head * HD : (head + 1) * HD]
+                q = q_ref[head, rows, :]
+                probs, grads = [], []
+                inner = 0.0
+                for half in range(2):
+                    p = jnp.exp(dot_nt(q, k_ref[half, head]) * scale - log_ref[head, rows, :])
+                    dp = dot_nt(gh, v_ref[half, head])
+                    inner = inner + jnp.sum(p * dp, axis=-1, keepdims=True)
+                    probs.append(p)
+                    grads.append(dp)
+                dq = 0.0
+                for half in range(2):
+                    ds = (probs[half] * (grads[half] - inner)).astype(BF)
+                    dq = dq + dot_nn(ds, k_ref[half, head])
+                    gk_acc[half, head] += dot_tn(ds, q)
+                    gv_acc[half, head] += dot_tn(probs[half].astype(BF), gh)
+                parts.append(norm_backward(q.astype(F32), iq_ref[head, rows, :], dq * scale))
+            gq_low[rows, :] = jnp.concatenate(parts, axis=1).astype(BF)
+
+        attend(me)
+
+        def gather(number, carry):
+            line_gather_step(gather_line, number, gall)
+
+            def side(which, inner):
+                place = me + (2 * which - 1) * number
+
+                @pl.when((place >= 0) & (place < count))
+                def _():
+                    attend(lax.clamp(0, place, count - 1))
+
+                return inner
+
+            return lax.fori_loop(0, 2, side, carry)
+
+        lax.fori_loop(1, count, gather, 0)
+        swap_out[0] = (gk_acc[1 - core] * scale).astype(BF)
+        swap_out[1] = gv_acc[1 - core].astype(BF)
+        swap = push(swap_out, swap_in, xsend, xrecv, peer)
+        swap.start()
+        line_gather_drain(gather_line, gall)
+        swap.wait()
+
+        def compute(number):
+            @pl.when(number % each == 0)
+            def _():
+                rows = rows_of(number // each, block)
+                x = x_ref[rows, :]
+                u = dot_nt(x, a_ref[...]).astype(BF)
+                parts_k, parts_v = [], []
+                for head in range(heads):
+                    dk = gk_acc[core, head, rows, :] * scale + swap_in[0, head, rows, :].astype(F32)
+                    normal = k_ref[core, head, rows, :].astype(F32)
+                    parts_k.append(norm_backward(normal, ik_ref[head, rows, :], dk))
+                    parts_v.append(gv_acc[core, head, rows, :] + swap_in[1, head, rows, :].astype(F32))
+                gq = gq_low[rows, :]
+                gk = jnp.concatenate(parts_k, axis=1).astype(BF)
+                gv = jnp.concatenate(parts_v, axis=1).astype(BF)
+                gu = jnp.concatenate([dot_nt(gq, bq[...]), dot_nt(gk, bk[...]), dot_nt(gv, bv[...])], axis=1).astype(BF)
+                y = dot_nt(gq, wq[...]) + dot_nt(gk, wk[...]) + dot_nt(gv, wv[...]) + dot_nn(gu, a_ref[...])
+                y = y.astype(BF)
+                for piece in range(each):
+                    partial_ref[number + piece] = y[piece * chunk : (piece + 1) * chunk]
+                ga_in[...] += dot_tn(gu, x)
+                gb_q[...] += dot_tn(u[:, :RANK], gq)
+                gb_k[...] += dot_tn(u[:, RANK : 2 * RANK], gk)
+                gb_v[...] += dot_tn(u[:, 2 * RANK :], gv)
+
+        def finish(slot, total):
+            total_out[rows_of(slot, chunk), :] = total
+
+        line_reduce_all(
+            reduce_line, steps, compute, partial_ref, from_left, from_right, stage_right, stage_left, finish
+        )
+
+    buffers = [vmem(steps, chunk, width) for _ in range(5)]
+    return call(
+        kernel,
+        [(array, True) for array in (g_first, attn_in, query, keys, values, low, logs, inv_q, inv_k)]
+        + [(own, False) for own in own_list] + [(piece, False) for piece in pieces]
+        + [(array, True) for array in (down, *ups, out_down, out_up)],
+        [
+            ((tokens, width), F32, True),
+            ((count, share, width), BF, True),
+            ((3 * RANK, width), F32, True),
+            ((RANK, local), F32, True),
+            ((RANK, local), F32, True),
+            ((RANK, local), F32, True),
+            ((RANK, local), F32, True),
+            ((RANK, width), F32, True),
+        ],
+        [vmem(width, local) for _ in range(4)]
+        + [vmem(tokens, local), vmem(2, heads, tokens, HD, dtype=F32), vmem(2, heads, tokens, HD, dtype=F32)]
+        + [vmem(2, heads, tokens, HD), vmem(2, heads, tokens, HD)]
+        + buffers + [dma(4), dma(), dma()] + [dma(count) for _ in range(4)] + [dma(steps) for _ in range(4)],
+        collective=4,
+        cost=cost_of(16 * tokens * width * local, 60e6),
+    )
+
+
+def skip_backward(count, g_attn, g_first, skip_out, hidden, long_skip, own, pieces, gain_halves, down, up, gain_row):
+    tokens, width = hidden.shape
+    span = own.shape[-1]
+    share = tokens // count
+    block = share
+
+    def kernel(g_ref, gf_ref, skip_ref, hid, lsk, own_ref, *refs):
+        piece_refs = refs[:6]
+        (gains, a_ref, b_ref, gain, out_h, out_l, g_shift, ga, gb, w, buf_h, buf_l, low, grads, wsem, osem) = refs[6:]
+        me = lax.axis_index("tensor")
+        for far in range(count):
+            lead = (far, xor_place(me, far))
+            for copy in assemble(w, own_ref, piece_refs, 0, wsem, lead):
+                copy.start()
+        g_shift[...] = jnp.zeros_like(g_shift)
+        whole_wait(w, wsem)
+
+        def step(number, carry):
+            rows = rows_of(number, block)
+            ga_in = g_ref[rows, :]
+            g_shift[...] += jnp.sum(ga_in, axis=0, keepdims=True)
+            normal, inverse = stats(skip_ref[rows, :])
+            g_low = (
+                gf_ref[number].astype(F32) + norm_backward(normal, inverse, ga_in * gain[...])
+            ).astype(BF)
+            left = hid[rows, :].astype(F32)
+            right = lsk[rows, :].astype(F32)
+            mean = (jnp.sum(left, axis=-1, keepdims=True) + jnp.sum(right, axis=-1, keepdims=True)) / (2 * width)
+            left = left - mean
+            right = right - mean
+            spread = jnp.sum(left * left, axis=-1, keepdims=True) + jnp.sum(right * right, axis=-1, keepdims=True)
+            inverse = lax.rsqrt(spread / (2 * width) + NORM_EPS)
+            left = left * inverse
+            right = right * inverse
+            gu = dot_nt(g_low, b_ref[...]).astype(BF)
+
+            @pl.when(number == me)
+            def _():
+                low_l = (left * gains[0:1, :]).astype(BF)
+                low_r = (right * gains[1:2, :]).astype(BF)
+                u = (dot_nt(low_l, a_ref[0]) + dot_nt(low_r, a_ref[1])).astype(BF)
+                ga[0] = dot_tn(gu, low_l)
+                ga[1] = dot_tn(gu, low_r)
+                gb[...] = dot_tn(u, g_low)
+
+            for place in range(count):
+                low[:, place * span : (place + 1) * span] = dot_nn(g_low, w[place])
+            gl = (low[:, :width] + dot_nn(gu, a_ref[0])) * gains[0:1, :]
+            gr = (low[:, width:] + dot_nn(gu, a_ref[1])) * gains[1:2, :]
+            mean = (jnp.sum(gl, axis=-1, keepdims=True) + jnp.sum(gr, axis=-1, keepdims=True)) / (2 * width)
+            inner = (
+                jnp.sum(gl * left, axis=-1, keepdims=True) + jnp.sum(gr * right, axis=-1, keepdims=True)
+            ) / (2 * width)
+            buf_h[number] = inverse * (gl - mean - left * inner)
+            buf_l[number] = inverse * (gr - mean - right * inner)
+            pltpu.make_async_copy(buf_h.at[number], out_h.at[rows, :], osem.at[0, number]).start()
+            pltpu.make_async_copy(buf_l.at[number], out_l.at[rows, :], osem.at[1, number]).start()
+            return carry
+
+        lax.fori_loop(0, tokens // block, step, 0)
+
+        def drain(number, carry):
+            rows = rows_of(number, block)
+            pltpu.make_async_copy(buf_h.at[number], out_h.at[rows, :], osem.at[0, number]).wait()
+            pltpu.make_async_copy(buf_l.at[number], out_l.at[rows, :], osem.at[1, number]).wait()
+            return carry
+
+        lax.fori_loop(0, tokens // block, drain, 0)
+
+    blocks = tokens // block
+    return call(
+        kernel,
+        [(array, True) for array in (g_attn, g_first, skip_out, hidden, long_skip)]
+        + [(own, False)] + [(piece, False) for piece in pieces]
+        + [(array, True) for array in (gain_halves, down, up, gain_row)],
+        [
+            ((tokens, width), F32, False),
+            ((tokens, width), F32, False),
+            ((1, width), F32, True),
+            ((2, RANK, width), F32, True),
+            ((RANK, width), F32, True),
+        ],
+        [
+            vmem(count, width, span),
+            vmem(blocks, block, width, dtype=F32),
+            vmem(blocks, block, width, dtype=F32),
+            vmem(block, 2 * width, dtype=F32),
+            vmem(8, 128, dtype=F32),
+            dma(),
+            dma(2, blocks),
+        ],
+        cost=cost_of(4 * tokens * width * width, 30e6),
+    )
+
+
+def adapter_reduce(count, table, chosen):
+    ranks, tiles, lanes = table.shape
+    half = tiles // 2
+    own_rows = ranks // count
+
+    def kernel(t_ref, sel, out, swap_out, swap_in, partial_ref, from_left, from_right, stage_right, stage_left, summed,
+               slots, other_out, other_in, ssem, rsem, dsend, drecv, *sems):
+        me = lax.axis_index("tensor")
+        core = lax.axis_index("ctx")
+        dp = lax.axis_index("dp")
+        peer = {"ctx": 1 - core}
+        line = Line(me, count, *sems)
+        peers = [{"dp": xor_place(dp, number)} for number in (1, 2, 3)]
+        greet(line_partners(me, count) + [(core >= 0, peer)] + [(core >= 0, device) for device in peers])
+        swap_out[...] = t_ref[:, pl.ds(pl.multiple_of((1 - core) * half, 16), half), :].astype(BF)
+        swap = push(swap_out, swap_in, ssem.at[0], rsem.at[0], peer)
+        swap.start()
+        swap.wait()
+        for number in range(count):
+            part = slice(number * own_rows, (number + 1) * own_rows)
+            mine = t_ref[part, pl.ds(pl.multiple_of(core * half, 16), half), :]
+            partial_ref[number] = (mine + swap_in[part].astype(F32)).astype(BF)
+
+        def scatter(number, carry):
+            line_scatter_step(line, number, partial_ref, from_left, from_right, stage_right, stage_left)
+            return carry
+
+        lax.fori_loop(0, count - 1, scatter, 0)
+        line_scatter_finish(line, partial_ref, from_left, from_right, stage_right, stage_left, summed)
+        slots[dp] = summed[...].astype(BF)
+        sends = [
+            push(slots.at[dp], slots.at[dp], dsend.at[number], drecv.at[number], device)
+            for number, device in enumerate(peers)
+        ]
+        for send in sends:
+            send.start()
+        for number in (1, 2, 3):
+            source = slots.at[xor_place(dp, number)]
+            push(source, source, dsend.at[number - 1], drecv.at[number - 1], peers[number - 1]).wait_recv()
+
+        def total(which):
+            result = jnp.zeros((own_rows, half, lanes), F32)
+            for sequence in range(4):
+                result = result + slots[sequence].astype(F32) * sel[which, sequence]
+            return result
+
+        other_out[...] = total(1 - core).astype(BF)
+        swap = push(other_out, other_in, ssem.at[1], rsem.at[1], peer)
+        swap.start()
+        out[core] = total(core)
+        for send in sends:
+            send.wait_send()
+        swap.wait()
+        out[1 - core] = other_in[...].astype(F32)
+
+    block = (own_rows, half, lanes)
+    return call(
+        kernel,
+        [(table, True), (chosen, True)],
+        [((2, *block), F32, True)],
+        [vmem(ranks, half, lanes), vmem(ranks, half, lanes)]
+        + [vmem(count, *block) for _ in range(5)]
+        + [vmem(*block, dtype=F32), vmem(4, *block), vmem(*block), vmem(*block)]
+        + [dma(2), dma(2), dma(3), dma(3)] + [dma(count) for _ in range(4)],
+        collective=5,
+        cost=cost_of(1e6, 10e6),
+    )[0]
+
+
+PAIR = ("dp", "ctx")
+
+
+def pair_permutation(core0, core1):
+    pairs = []
+    for dp in range(4):
+        for core in range(2):
+            pairs.append((dp * 2 + core, (dp ^ (core0 if core == 0 else core1)) * 2 + core))
+    return pairs
+
+
+def swap_cores(value):
+    return lax.ppermute(value, "ctx", [(0, 1), (1, 0)])
+
+
+def share_pieces(half):
+    first, second = pair_permutation(1, 2), pair_permutation(2, 1)
+    a = lax.ppermute(half, PAIR, first)
+    b = lax.ppermute(half, PAIR, second)
+    c = lax.ppermute(a, PAIR, second)
+    return [a, b, c, swap_cores(a), swap_cores(b), swap_cores(c)]
+
+
+def core_half(value, axis=0):
+    size = value.shape[axis] // 2
+    return lax.dynamic_slice_in_dim(value, lax.axis_index("ctx") * size, size, axis)
+
+
+def exchange_dp(rows):
+    dp = lax.axis_index("dp")
+    got = [lax.dynamic_slice_in_dim(rows, dp, 1, 0)]
+    for number in (1, 2, 3):
+        row = lax.dynamic_slice_in_dim(rows, dp ^ number, 1, 0)
+        got.append(lax.ppermute(row, "dp", [(place, place ^ number) for place in range(4)]))
+    return got
+
+
+def gather_dp(row):
+    dp = lax.axis_index("dp")
+    table = jnp.zeros((4, row.shape[1]), row.dtype)
+    table = lax.dynamic_update_slice_in_dim(table, row, dp, 0)
+    for number in (1, 2, 3):
+        got = lax.ppermute(row, "dp", [(place, place ^ number) for place in range(4)])
+        table = lax.dynamic_update_slice_in_dim(table, got, dp ^ number, 0)
+    return table
+
+
+def fused_body(
+    hidden,
+    long_skip_input,
+    condition,
+    projected_text_tokens,
+    sequence_adapter_index,
+    skip_projection_weight,
+    shift_modulation_weight,
+    self_query_weight,
+    self_key_weight,
+    self_value_weight,
+    attention_output_weight,
+    cross_query_weight,
+    cross_key_weight,
+    cross_value_weight,
+    cross_output_weight,
+    feedforward_up_weight,
+    feedforward_down_weight,
+    skip_norm_gain,
+    norm_gain_rows,
+    adapter_down_factor,
+    adapter_up_factor,
+    cotangent,
+):
+    rank = lax.axis_index("tensor")
+    count = lax.axis_size("tensor")
+    core = lax.axis_index("ctx")
+    dp = lax.axis_index("dp")
+    hidden, long_skip, text, cot = hidden[0], long_skip_input[0], projected_text_tokens[0], cotangent[0]
+    tokens, width = hidden.shape
+    local = self_query_weight.shape[1]
+    heads = local // HD
+    ff = feedforward_up_weight.shape[1]
+    span = skip_projection_weight.shape[0]
+    share = tokens // count
+    in_sizes = [2 * MODEL_WIDTH] + [MODEL_WIDTH] * 6 + [TW, TW, MODEL_WIDTH, MODEL_WIDTH, FF]
+    out_sizes = [MODEL_WIDTH] * 10 + [FF, MODEL_WIDTH]
+    in_at = [sum(in_sizes[:number]) for number in range(12)]
+    out_at = [sum(out_sizes[:number]) for number in range(12)]
+    index = sequence_adapter_index[0]
+    down_table = lax.dynamic_index_in_dim(adapter_down_factor, index, 0, keepdims=False)
+    up_table = lax.dynamic_index_in_dim(adapter_up_factor, index, 0, keepdims=False)
+
+    def down_full(number):
+        return down_table[:, in_at[number] : in_at[number] + in_sizes[number]]
+
+    def up_full(number):
+        return up_table[:, out_at[number] : out_at[number] + out_sizes[number]]
+
+    def down_local(number, size):
+        return lax.dynamic_slice_in_dim(down_table, in_at[number] + rank * size, size, 1)
+
+    def up_local(number, size):
+        return lax.dynamic_slice_in_dim(up_table, out_at[number] + rank * size, size, 1)
+
+    def stack(table):
+        return jnp.transpose(table.reshape(RANK, count, -1), (1, 0, 2))
+
+    skip_t = skip_projection_weight.T
+    attn_out_t = attention_output_weight.T
+    cross_out_t = cross_output_weight.T
+    ff_down_t = feedforward_down_weight.T
+
+    skip_half = core_half(skip_t)
+    skip_pieces = share_pieces(skip_half)
+
+    narrow = [self_query_weight, self_key_weight, self_value_weight, attn_out_t, cross_key_weight, cross_value_weight]
+    narrow_at = [sum(weight.shape[0] for weight in narrow[:number]) // 2 for number in range(6)]
+    narrow_pieces = share_pieces(jnp.concatenate([core_half(weight) for weight in narrow], axis=0))
+
+    def along_tensor(value):
+        others = [
+            lax.ppermute(value, "tensor", [(place, place ^ number) for place in range(count)])
+            for number in range(1, count)
+        ]
+        return jnp.stack([value] + others)
+
+    cross_own = along_tensor(jnp.concatenate([cross_query_weight, cross_out_t], axis=0))
+    rows_q = cross_query_weight.shape[0]
+    cross_half = jnp.concatenate(
+        [core_half(cross_own[:, :rows_q], 1), core_half(cross_own[:, rows_q:], 1)], axis=1
+    )
+    cross_pieces = share_pieces(cross_half)
+    cross_at = [0, rows_q // 2]
+    query_stack = (cross_own[:, :rows_q], cross_pieces)
+    out_stack = (cross_own[:, rows_q:], cross_pieces)
+
+    wide_pieces = share_pieces(jnp.concatenate([core_half(feedforward_up_weight), core_half(ff_down_t)], axis=0))
+    wide_at = [0, feedforward_up_weight.shape[0] // 2]
+
+    skip_own = along_tensor(skip_t)
+    skip_all_pieces = share_pieces(core_half(skip_own, 1))
+
+    act_wide, silu_pull = jax.vjp(jax.nn.silu, condition.astype(F32))
+    act_low = act_wide.astype(BF)
+    tag = jnp.full((1, 128), index, jnp.int32).astype(BF)
+    gathered = gather_dp(jnp.concatenate([act_low, tag], axis=1))
+    indices = gathered[:, MODEL_WIDTH].astype(jnp.int32)
+    mod_rows = shift_modulation_weight.shape[0]
+    act_slice = lax.dynamic_slice_in_dim(gathered, dp * mod_rows, mod_rows, 1)
+    shift_parts = exchange_dp(dot_nn(act_slice, shift_modulation_weight))
+    mod_u = dot_nt(act_low, down_full(1))
+    shift_row = sum(shift_parts) + jnp.dot(mod_u, up_full(1).astype(F32), precision=PRECISE)
+
+    both = jnp.concatenate([hidden, long_skip], axis=1)
+    part = lax.dynamic_slice_in_dim(both, rank * span, span, 1)
+    part_gain = lax.dynamic_slice_in_dim(skip_norm_gain, rank * span, span, 0)[None, :]
+    skip_out, attn_in = skip_forward(
+        count, skip_t, skip_pieces, hidden, long_skip, part, part_gain, down_local(0, span), up_full(0),
+        norm_gain_rows[0:1], shift_row,
+    )
+    own_text = text_forward(
+        heads, text, cross_key_weight, cross_value_weight, narrow_pieces, narrow_at[4], narrow_at[5],
+        jnp.concatenate([down_full(7), down_full(8)], axis=0), up_local(7, local), up_local(8, local),
+    )
+    text_all = jnp.zeros((count, *own_text.shape), BF)
+    for number in range(count):
+        got = own_text
+        if number:
+            got = lax.ppermute(own_text, "tensor", [(place, place ^ number) for place in range(count)])
+        text_all = lax.dynamic_update_slice_in_dim(text_all, got[None], rank ^ number, 0)
+    text_other = swap_cores(text_all)
+    text_keys = jnp.where(core == 0, text_all, text_other)
+    text_values = jnp.where(core == 0, text_other, text_all)
+
+    qkv_down = jnp.concatenate([down_full(2), down_full(3), down_full(4)], axis=0)
+    qkv_up = [up_local(number, local) for number in (2, 3, 4)]
+    attn_own = [self_query_weight, self_key_weight, self_value_weight, attn_out_t]
+    out_down, out_up = down_local(5, local), up_full(5)
+    query, keys, values, low, logs, inv_q, inv_k, summed = attention_forward(
+        count, heads, attn_in, attn_own, narrow_pieces, narrow_at[:4], qkv_down, qkv_up, out_down, out_up
+    )
+    cross_down, cross_up = down_full(6), stack(up_full(6))
+    cout_down, cout_up = stack(down_full(9)), up_full(9)
+    first, second, cross_in, mlp_in, cquery, cinv, clogs, clow, cu = cross_forward(
+        count, heads, summed, skip_out, query_stack, out_stack, text_keys, text_values, norm_gain_rows, cross_down,
+        cross_up, cout_down, cout_up, cross_at,
+    )
+    g_mlp_in, down_part, g_up_a, g_up_b, g_down_a, g_down_b = feed_forward(
+        count, mlp_in, cot, second, feedforward_up_weight, ff_down_t, wide_pieces, wide_at, down_full(10),
+        up_local(10, ff), down_local(11, ff), up_full(11),
+    )
+    block_out = lax.psum(down_part, "tensor")
+    g_first, g_cq_a, g_cq_b, g_ck_a, g_ck_b, g_cv_a, g_cv_b, g_co_a, g_co_b = cross_backward(
+        count, heads, g_mlp_in, cot, first, second, cross_in, cquery, cinv, clogs, clow, cu, text, query_stack,
+        out_stack, text_keys, text_values, norm_gain_rows, cross_down, cross_up, cout_down, cout_up,
+        jnp.concatenate([down_full(7), down_full(8)], axis=0), stack(up_full(7)), stack(up_full(8)), cross_at,
+    )
+    g_attn, g_first_all, g_qkv_a, g_q_b, g_k_b, g_v_b, g_o_a, g_o_b = attention_backward(
+        count, heads, g_first, attn_in, query, keys, values, low, logs, inv_q, inv_k, attn_own, narrow_pieces,
+        narrow_at[:4], qkv_down, qkv_up, out_down, out_up,
+    )
+    skip_down = jnp.transpose(down_full(0).reshape(RANK, 2, MODEL_WIDTH), (1, 0, 2))
+    hidden_grad, skip_grad, g_shift, g_skip_a, g_skip_b = skip_backward(
+        count, g_attn, g_first_all, skip_out, hidden, long_skip, skip_own, skip_all_pieces,
+        skip_norm_gain.reshape(2, MODEL_WIDTH), skip_down, up_full(0), norm_gain_rows[0:1],
+    )
+
+    g_mod_u = dot_nt(g_shift.astype(BF), up_full(1))
+    once = (rank == 0).astype(F32)
+    g_mod_a = jnp.dot(g_mod_u.T, act_low.astype(F32), precision=PRECISE) * once
+    g_mod_b = jnp.dot(mod_u.T, g_shift, precision=PRECISE) * once
+    shift_sum = g_shift + swap_cores(g_shift)
+    shift_all = gather_dp(shift_sum).astype(BF)
+    act_parts = exchange_dp(dot_nt(shift_all, shift_modulation_weight))
+    g_act = jnp.zeros((1, MODEL_WIDTH), F32)
+    for number, piece in enumerate(act_parts):
+        g_act = lax.dynamic_update_slice_in_dim(g_act, piece, (dp ^ number) * mod_rows, 1)
+    shift_u = jnp.dot(shift_sum, up_full(1).astype(F32).T, precision=PRECISE)
+    g_act = g_act + jnp.dot(shift_u, down_full(1).astype(F32), precision=PRECISE)
+    g_condition = silu_pull(g_act)[0][0]
+    size = MODEL_WIDTH // (2 * count)
+    condition_gradient = lax.dynamic_slice_in_dim(g_condition, (core * count + rank) * size, size, 0)
+
+    def unstack(value):
+        return jnp.transpose(value, (1, 0, 2)).reshape(RANK, -1)
+
+    def place_local(value, total):
+        return lax.dynamic_update_slice_in_dim(jnp.zeros((RANK, total), F32), value, rank * value.shape[1], 1)
+
+    table = jnp.concatenate(
+        [
+            g_skip_a[0], g_skip_a[1], g_mod_a, g_qkv_a[:RANK], g_qkv_a[RANK : 2 * RANK], g_qkv_a[2 * RANK :],
+            place_local(g_o_a, MODEL_WIDTH), g_cq_a, g_ck_a, g_cv_a, unstack(g_co_a), g_up_a, place_local(g_down_a, FF),
+            g_skip_b, g_mod_b, place_local(g_q_b, MODEL_WIDTH), place_local(g_k_b, MODEL_WIDTH),
+            place_local(g_v_b, MODEL_WIDTH), g_o_b, unstack(g_cq_b), unstack(g_ck_b), unstack(g_cv_b), g_co_b,
+            place_local(g_up_b, FF), g_down_b,
+        ],
+        axis=1,
+    )
+    wide_a, wide_b = sum(in_sizes) // 128, sum(out_sizes) // 128
+    tiles = -(-(wide_a + wide_b) // 32) * 32
+    table = jnp.pad(table.reshape(RANK, wide_a + wide_b, 128), ((0, 0), (0, tiles - wide_a - wide_b), (0, 0)))
+    chosen = (indices[None, :] == (dp * 2 + jnp.arange(2, dtype=jnp.int32))[:, None]).astype(F32)
+    chosen = jnp.broadcast_to(chosen[:, :, None, None], (2, 4, 1, 128))
+    reduced = adapter_reduce(count, table, chosen)
+    reduced = jnp.transpose(reduced, (1, 0, 2, 3)).reshape(RANK // count, tiles, 128)
+    return (
+        block_out[None],
+        hidden_grad[None],
+        skip_grad[None],
+        condition_gradient,
+        reduced[:, :wide_a].reshape(-1),
+        reduced[:, wide_a : wide_a + wide_b].reshape(-1),
+    )
+
+
 def solution(mesh):
     in_specs = (
         P("dp", "ctx", None),
@@ -627,4 +2068,6 @@
         P(("dp", "ctx", "tensor")),
         P(("dp", "ctx", "tensor")),
     )
-    return jax.shard_map(body, mesh=mesh, in_specs=in_specs, out_specs=out_specs, check_vma=False)
+    shape = mesh.shape
+    fused = shape["dp"] == 4 and shape["ctx"] == 2 and shape["tensor"] == 4
+    return jax.shard_map(fused_body if fused else body, mesh=mesh, in_specs=in_specs, out_specs=out_specs, check_vma=False)

time: 1060 us -> 704 us (0.66)
  the two profiles are of different devices: /device:TPU:0 before, /device:TPU:9 now
where the time goes in v1:
time: 704 us; the launch traced here: 693 us
  Pallas kernels  390 us (55%)
  local copies, waits for them, and re-layouts  118 us (17%)
  starting transfers between devices  76.1 us (11%)
  waiting for transfers between devices  63.5 us (9%)
  other arithmetic  23.4 us (3%)
  between operations  16.1 us (2%)
    pallas_call x9, Pallas kernels, call(): pl.pallas_call(kernel, out_shape=[jax.ShapeDtypeStruct(shape, dtype) for...  390 us
    ppermute x17, starting transfers between devices, swap_cores(): return lax.ppermute(value, 'ctx', [(0, 1), (1, 0)])  45 us
    ppermute x6, waiting for transfers between devices, along_tensor(): lax.ppermute(value, 'tensor', [(place, place ^ number) for place in range...  39.9 us
    unnamed x141, local copies, waits for them, and re-layouts  30.4 us
    ppermute x3, waiting for transfers between devices, fused_body(): lax.ppermute(own_text, 'tensor', [(place, place ^ number) for place in ra...  20.7 us
  transfers between devices with their start and end apart: 54, of which 7 were waited for; matrix products, arithmetic and copies ran while one was open for 20% of the time, Pallas kernels for 53%

profile of v1, /device:TPU:9, one launch (start us, length us, event | category | flops | bytes accessed | tf_op | source)
XLA Modules:
  0.0 692.5 jit_solution(10282764858511136634)
XLA Ops:
  15.8 2.3 collective-permute-start.19
  30.1 2.8 dynamic_update_slice.66
  35.4 3.2 dynamic_update_slice.67
  39.6 3.2 dynamic_update_slice.68
  43.8 3.2 dynamic_update_slice.69
  64.0 2.7 collective-permute-done.1.refs_1_
  67.5 7.9 %collective-permute-start.3 = (bf16[176,704]{1,0:T(8,128)(2,1)}, bf16[176,704]{1,0:T(8,128)(2,1)S(1)}, u32[]{:S(2)}, u32[]{:S(2)}) collective-permute-start(bf16[176,704]{1,0:T(8,128)(2,1)} %collective-permute-done.refs_0_), channel_id=1, source_target_pairs={{0,4},{4,0},{1,5},{5,1},{2,6},{6,2},{3,7},{7,3},{8,12},{12,8},{9,1... | collective-permute-start | bytes 743432 | tf_op jit(solution)/shard_map/ppermute | solution.py:1796
  83.6 13.0 %collective-permute-done.37 = bf16[352,704]{1,0:T(8,128)(2,1)S(1)} collective-permute-done((bf16[352,704]{1,0:T(8,128)(2,1)S(1)}, bf16[352,704]{1,0:T(8,128)(2,1)S(1)}, u32[]{:S(2)}, u32[]{:S(2)}) %collective-permute-start.37) | collective-permute-done | bytes 495648 | tf_op jit(solution)/shard_map/ppermute | solution.py:1903
  99.5 3.3 collective-permute-done.38
  103.9 23.6 %collective-permute-done.39 = bf16[352,704]{1,0:T(8,128)(2,1)S(1)} collective-permute-done((bf16[352,704]{1,0:T(8,128)(2,1)S(1)}, bf16[352,704]{1,0:T(8,128)(2,1)S(1)}, u32[]{:S(2)}, u32[]{:S(2)}) %collective-permute-start.39) | collective-permute-done | bytes 495648 | tf_op jit(solution)/shard_map/ppermute | solution.py:1903
  129.8 2.6 fusion.refs_8_
  132.3 3.1 collective-permute-start.15
  149.3 2.3 copy.78.refs_4_.refs_0_
  163.0 4.3 shard_map.255
  168.6 5.5 collective-permute-done.27
  174.9 8.1 %collective-permute-done.28 = bf16[4,333,90]{2,1,0:T(8,128)(2,1)S(1)} collective-permute-done((bf16[4,333,90]{2,1,0:T(8,128)(2,1)}, bf16[4,333,90]{2,1,0:T(8,128)(2,1)S(1)}, u32[]{:S(2)}, u32[]{:S(2)}) %collective-permute-start.28) | collective-permute-done | bytes 239792 | tf_op jit(solution)/shard_map/ppermute | solution.py:1950
  183.5 7.1 %collective-permute-done.29 = bf16[4,333,90]{2,1,0:T(8,128)(2,1)S(1)} collective-permute-done((bf16[4,333,90]{2,1,0:T(8,128)(2,1)S(1)}, bf16[4,333,90]{2,1,0:T(8,128)(2,1)S(1)}, u32[]{:S(2)}, u32[]{:S(2)}) %collective-permute-start.29) | collective-permute-done | bytes 239792 | tf_op jit(solution)/shard_map/ppermute | solution.py:1950
  193.6 25.1 %collective-permute-start.24 = (bf16[4,352,352]{2,1,0:T(8,128)(2,1)}, bf16[4,352,352]{2,1,0:T(8,128)(2,1)S(1)}, u32[]{:S(2)}, u32[]{:S(2)}) collective-permute-start(bf16[4,352,352]{2,1,0:T(8,128)(2,1)} %collective-permute-done.21.refs_2_), channel_id=1, source_target_pairs={{0,4},{4,0},{1,5},{5,1},{2,6},{6,2},{3,7},{7,3},{8,12},{12,8},{9,1... | collective-permute-start | bytes 2973704 | tf_op jit(solution)/shard_map/ppermute | solution.py:1796
  241.8 54.1 %shard_map.253 = (f32[512,1408]{1,0:T(8,128)}, bf16[512,1408]{1,0:T(8,128)(2,1)}) custom-call(bf16[352,704]{1,0:T(8,128)(2,1)} %bitcast.127, bf16[176,704]{1,0:T(8,128)(2,1)} %collective-permute-done.refs_0_, bf16[176,704]{1,0:T(8,128)(2,1)} %collective-permute-done.1.refs_1_, bf16[176,704]{1,0:T(8,128)(2,1)} %collective-permute-done.2.refs_2_, ...), custom_call_target="tpu_custom_call" | custom-call | flops 1015021568 | bytes 40000000 | tf_op jit(solution)/shard_map/pallas_call | solution.py:947
  296.0 54.4 %shard_map.254 = (bf16[4,512,88]{2,1,0:T(8,128)(2,1)}, bf16[2,4,512,88]{3,2,1,0:T(8,128)(2,1)}, bf16[2,4,512,88]{3,2,1,0:T(8,128)(2,1)}, bf16[512,352]{1,0:T(8,1...) custom-call(bf16[512,1408]{1,0:T(8,128)(2,1)} %get-tuple-element.53.x_ref, ...), custom_call_target="tpu_custom_call" | custom-call | flops 2030043136 | bytes 60000000 | tf_op jit(solution)/shard_map/pallas_call | solution.py:947
  350.4 3.5 copy.94
  353.9 3.1 broadcast_select_fusion
  356.9 20.5 %shard_map.256 = (f32[128,1408]{1,0:T(8,128)}, f32[128,1408]{1,0:T(8,128)}, bf16[128,1408]{1,0:T(8,128)(2,1)}, bf16[128,1408]{1,0:T(8,128)(2,1)}, bf16[4,4,128,8...) custom-call(f32[128,1408]{1,0:T(8,128)} %get-tuple-element.54.sum_re, ...), custom_call_target="tpu_custom_call" | custom-call | flops 1015021568 | bytes 20000000 | tf_op jit(solution)/shard_map/pallas_call | solution.py:947
  378.1 68.8 %shard_map.257 = (f32[128,1408]{1,0:T(8,128)}, bf16[512,1408]{1,0:T(8,128)(2,1)}, f32[16,1408]{1,0:T(8,128)}, f32[16,1536]{1,0:T(8,128)}, f32[16,1536]{1,0:T(8,128)}, /*index=5*/f32[16,1408]{1,0:T(8,128)}) custom-call(bf16[128,1408]{1,0:T(8,128)(2,1)} %get-tuple-element.56.x_ref, bf16[512,1408]{1,0:T(8,128)(2,1)} %bitcast.135, ...), custom_call_target="tpu_custom_call" | custom-call | flops 8858370048 | bytes 60000000 | tf_op jit(solution)/shard_map/pallas_call | solution.py:947
  446.9 24.4 %shard_map.258 = (bf16[128,1408]{1,0:T(8,128)(2,1)}, f32[16,1408]{1,0:T(8,128)}, f32[4,16,352]{2,1,0:T(8,128)}, f32[16,1024]{1,0:T(8,128)}, f32[4,16,352]{2,1,0:...) custom-call(f32[128,1408]{1,0:T(8,128)} %get-tuple-element.59.g_ref, ...), custom_call_target="tpu_custom_call" | custom-call | flops 2030043136 | bytes 20000000 | tf_op jit(solution)/shard_map/pallas_call | solution.py:947
  471.3 87.8 %shard_map.259 = (f32[512,1408]{1,0:T(8,128)}, bf16[4,128,1408]{2,1,0:T(8,128)(2,1)}, f32[48,1408]{1,0:T(8,128)}, f32[16,352]{1,0:T(8,128)}, f32[16,352]{1,0:T(8...) custom-call(bf16[128,1408]{1,0:T(8,128)(2,1)} %get-tuple-element.67.g_ref, ...), custom_call_target="tpu_custom_call" | custom-call | flops 4060086272 | bytes 60000000 | tf_op jit(solution)/shard_map/pallas_call | solution.py:947
  560.5 22.0 %shard_map.260 = (f32[512,1408]{1,0:T(8,128)}, f32[512,1408]{1,0:T(8,128)}, f32[1,1408]{1,0:T(1,128)}, f32[2,16,1408]{2,1,0:T(8,128)}, f32[16,1408]{1,0:T(8,128)}) custom-call(f32[512,1408]{1,0:T(8,128)} %get-tuple-element.75.g_ref, bf16[4,128,1408]{2,1,0:T(8,128)(2,1)} %get-tuple-element.76.gf_ref, f32[512,1408]{1,0:T(8,128)} %get-tuple-element.55.skip_ref, ...), custom_call_target="tpu_custom_call" | custom-call | flops 4060086272 | bytes 30000000 | tf_op jit(solution)/shard_map/pallas_call | solution.py:947
  583.5 4.2 collective-permute-start.46
  616.7 3.3 reshape.147
  620.1 3.7 pad.5.t_ref
  624.4 53.4 %shard_map.261 = f32[2,4,176,128]{3,2,1,0:T(8,128)} custom-call(f32[16,352,128]{2,1,0:T(8,128)} %pad.5.t_ref, f32[2,4,1,128]{3,2,1,0:T(1,128)} %broadcast_in_dim.57.sel), custom_call_target="tpu_custom_call" | custom-call | flops 1000000 | bytes 10000000 | tf_op jit(solution)/shard_map/pallas_call | solution.py:947
  682.9 2.6 copy.172
  (351 shorter events, 147.5 us)
Async XLA Ops:
  7.2 675.7 %all-reduce.4.cloned.1.call-start = ((), (), s32[]{:S(2)}) async-start(), calls=%async_computation | async-start | bytes 2883584 | tf_op jit(solution)/shard_map/psum | solution.py:1973
  9.9 23.0 %collective-permute-start.6 = (bf16[1,1536]{1,0:T(2,128)(2,1)S(1)}, bf16[1,1536]{1,0:T(2,128)(2,1)}, u32[]{:S(2)}, u32[]{:S(2)}) collective-permute-start(bf16[1,1536]{1,0:T(2,128)(2,1)S(1)} %concatenate.29), channel_id=1, source_target_pairs={{0,8},{8,0},{16,24},{24,16},{1,9},{9,1},{17,25},{25,17},{2,10},{10... | collective-permute-start | bytes 9224 | tf_op jit(solution)/shard_map/ppermute | solution.py:1826
  11.1 27.5 %collective-permute-start.7 = (bf16[1,1536]{1,0:T(2,128)(2,1)S(1)}, bf16[1,1536]{1,0:T(2,128)(2,1)}, u32[]{:S(2)}, u32[]{:S(2)}) collective-permute-start(bf16[1,1536]{1,0:T(2,128)(2,1)S(1)} %concatenate.29), channel_id=1, source_target_pairs={{0,16},{8,24},{16,0},{24,8},{1,17},{9,25},{17,1},{25,9},{2,18},{10... | collective-permute-start | bytes 9224 | tf_op jit(solution)/shard_map/ppermute | solution.py:1826
  12.4 30.4 %collective-permute-start.8 = (bf16[1,1536]{1,0:T(2,128)(2,1)S(1)}, bf16[1,1536]{1,0:T(2,128)(2,1)}, u32[]{:S(2)}, u32[]{:S(2)}) collective-permute-start(bf16[1,1536]{1,0:T(2,128)(2,1)S(1)} %concatenate.29), channel_id=1, source_target_pairs={{0,24},{8,16},{16,8},{24,0},{1,25},{9,17},{17,9},{25,1},{2,26},{10... | collective-permute-start | bytes 9224 | tf_op jit(solution)/shard_map/ppermute | solution.py:1826
  15.6 51.9 %collective-permute-start.18 = (bf16[704,352]{1,0:T(8,128)(2,1)}, bf16[704,352]{1,0:T(8,128)(2,1)}, u32[]{:S(2)}, u32[]{:S(2)}) collective-permute-start(bf16[704,352]{1,0:T(8,128)(2,1)} %get-tuple-element.130), channel_id=1, source_target_pairs={{0,1},{1,0},{2,3},{3,2},{4,5},{5,4},{6,7},{7,6},{8,9},{9,8},{10,11... | collective-permute-start | bytes 1486856 | tf_op jit(solution)/shard_map/ppermute | solution.py:1903
  15.8 59.6 %collective-permute-start.19 = (bf16[704,352]{1,0:T(8,128)(2,1)}, bf16[704,352]{1,0:T(8,128)(2,1)}, u32[]{:S(2)}, u32[]{:S(2)}) collective-permute-start(bf16[704,352]{1,0:T(8,128)(2,1)} %get-tuple-element.130), channel_id=1, source_target_pairs={{0,2},{1,3},{2,0},{3,1},{4,6},{5,7},{6,4},{7,5},{8,10},{9,11},{10,... | collective-permute-start | bytes 1486856 | tf_op jit(solution)/shard_map/ppermute | solution.py:1903
  32.9 29.1 %collective-permute-start = (bf16[176,704]{1,0:T(8,128)(2,1)}, bf16[176,704]{1,0:T(8,128)(2,1)}, u32[]{:S(2)}, u32[]{:S(2)}) collective-permute-start(bf16[176,704]{1,0:T(8,128)(2,1)} %dynamic-slice_bitcast_fusion.3), channel_id=1, source_target_pairs={{0,8},{4,20},{8,0},{12,28},{16,24},{20,4},{24,16},{28,12},{1,9},{5... | collective-permute-start | bytes 743432 | tf_op jit(solution)/shard_map/ppermute | solution.py:1801
  51.9 24.3 %collective-permute-start.20 = (bf16[704,352]{1,0:T(8,128)(2,1)}, bf16[704,352]{1,0:T(8,128)(2,1)}, u32[]{:S(2)}, u32[]{:S(2)}) collective-permute-start(bf16[704,352]{1,0:T(8,128)(2,1)} %get-tuple-element.130), channel_id=1, source_target_pairs={{0,3},{1,2},{2,1},{3,0},{4,7},{5,6},{6,5},{7,4},{8,11},{9,10},{10,... | collective-permute-start | bytes 1486856 | tf_op jit(solution)/shard_map/ppermute | solution.py:1903
  61.9 20.5 %collective-permute-start.12 = (bf16[960,352]{0,1:T(8,128)(2,1)}, bf16[960,352]{0,1:T(8,128)(2,1)}, u32[]{:S(2)}, u32[]{:S(2)}) collective-permute-start(bf16[960,352]{0,1:T(8,128)(2,1)} %concatenate.30), channel_id=1, source_target_pairs={{0,8},{4,20},{8,0},{12,28},{16,24},{20,4},{24,16},{28,12},{1,9},{5... | collective-permute-start | bytes 2027528 | tf_op jit(solution)/shard_map/ppermute | solution.py:1801
  79.2 53.2 %collective-permute-start.13 = (bf16[960,352]{0,1:T(8,128)(2,1)}, bf16[960,352]{0,1:T(8,128)(2,1)}, u32[]{:S(2)}, u32[]{:S(2)}) collective-permute-start(bf16[960,352]{0,1:T(8,128)(2,1)} %concatenate.30), channel_id=1, source_target_pairs={{0,16},{4,12},{8,24},{12,4},{16,0},{20,28},{24,8},{28,20},{1,17},{... | collective-permute-start | bytes 2027528 | tf_op jit(solution)/shard_map/ppermute | solution.py:1802
  81.0 21.8 %collective-permute-start.38 = (bf16[352,704]{1,0:T(8,128)(2,1)S(1)}, bf16[352,704]{1,0:T(8,128)(2,1)S(1)}, u32[]{:S(2)}, u32[]{:S(2)}) collective-permute-start(bf16[352,704]{1,0:T(8,128)(2,1)S(1)} %bitcast.124), channel_id=1, source_target_pairs={{0,2},{1,3},{2,0},{3,1},{4,6},{5,7},{6,4},{7,5},{8,10},{9,11},{10,... | collective-permute-start | bytes 1486856 | tf_op jit(solution)/shard_map/ppermute | solution.py:1903
  81.6 45.9 %collective-permute-start.39 = (bf16[352,704]{1,0:T(8,128)(2,1)S(1)}, bf16[352,704]{1,0:T(8,128)(2,1)S(1)}, u32[]{:S(2)}, u32[]{:S(2)}) collective-permute-start(bf16[352,704]{1,0:T(8,128)(2,1)S(1)} %bitcast.125), channel_id=1, source_target_pairs={{0,3},{1,2},{2,1},{3,0},{4,7},{5,6},{6,5},{7,4},{8,11},{9,10},{10,... | collective-permute-start | bytes 1486856 | tf_op jit(solution)/shard_map/ppermute | solution.py:1903
  82.4 53.1 %collective-permute-start.14 = (bf16[960,352]{0,1:T(8,128)(2,1)}, bf16[960,352]{0,1:T(8,128)(2,1)}, u32[]{:S(2)}, u32[]{:S(2)}) collective-permute-start(bf16[960,352]{0,1:T(8,128)(2,1)} %collective-permute-done.12), channel_id=1, source_target_pairs={{0,16},{4,12},{8,24},{12,4},{16,0},{20,28},{24,8},{28,20},{1,17},{... | collective-permute-start | bytes 2027528 | tf_op jit(solution)/shard_map/ppermute | solution.py:1803
  96.5 38.9 %collective-permute-start.5 = (bf16[176,704]{1,0:T(8,128)(2,1)}, bf16[176,704]{1,0:T(8,128)(2,1)}, u32[]{:S(2)}, u32[]{:S(2)}) collective-permute-start(bf16[176,704]{1,0:T(8,128)(2,1)} %collective-permute-done.2.refs_2_), channel_id=1, source_target_pairs={{0,4},{4,0},{1,5},{5,1},{2,6},{6,2},{3,7},{7,3},{8,12},{12,8},{9,1... | collective-permute-start | bytes 743432 | tf_op jit(solution)/shard_map/ppermute | solution.py:1796
  102.8 64.5 %collective-permute-start.31 = (bf16[352,1536]{1,0:T(8,128)(2,1)}, bf16[352,1536]{1,0:T(8,128)(2,1)}, u32[]{:S(2)}, u32[]{:S(2)}) collective-permute-start(bf16[352,1536]{1,0:T(8,128)(2,1)} %pad_maximum_fusion.3), channel_id=1, source_target_pairs={{0,8},{4,20},{8,0},{12,28},{16,24},{20,4},{24,16},{28,12},{1,9},{5... | collective-permute-start | bytes 3244040 | tf_op jit(solution)/shard_map/ppermute | solution.py:1801
  143.3 50.3 %collective-permute-start.32 = (bf16[352,1536]{1,0:T(8,128)(2,1)}, bf16[352,1536]{1,0:T(8,128)(2,1)}, u32[]{:S(2)}, u32[]{:S(2)}) collective-permute-start(bf16[352,1536]{1,0:T(8,128)(2,1)} %pad_maximum_fusion.3), channel_id=1, source_target_pairs={{0,16},{4,12},{8,24},{12,4},{16,0},{20,28},{24,8},{28,20},{1,17},{... | collective-permute-start | bytes 3244040 | tf_op jit(solution)/shard_map/ppermute | solution.py:1802
  144.0 74.6 %collective-permute-start.22 = (bf16[4,352,352]{2,1,0:T(8,128)(2,1)}, bf16[4,352,352]{2,1,0:T(8,128)(2,1)}, u32[]{:S(2)}, u32[]{:S(2)}) collective-permute-start(bf16[4,352,352]{2,1,0:T(8,128)(2,1)} %pad_maximum_fusion.2), channel_id=1, source_target_pairs={{0,16},{4,12},{8,24},{12,4},{16,0},{20,28},{24,8},{28,20},{1,17},{... | collective-permute-start | bytes 2973704 | tf_op jit(solution)/shard_map/ppermute | solution.py:1802
  144.7 74.0 %collective-permute-start.40 = (bf16[4,176,704]{2,1,0:T(8,128)(2,1)}, bf16[4,176,704]{2,1,0:T(8,128)(2,1)}, u32[]{:S(2)}, u32[]{:S(2)}) collective-permute-start(bf16[4,176,704]{2,1,0:T(8,128)(2,1)} %constant_dynamic-slice_fusion.7), channel_id=1, source_target_pairs={{0,8},{4,20},{8,0},{12,28},{16,24},{20,4},{24,16},{28,12},{1,9},{5... | collective-permute-start | bytes 2973704 | tf_op jit(solution)/shard_map/ppermute | solution.py:1801
  145.4 73.8 %collective-permute-start.23 = (bf16[4,352,352]{2,1,0:T(8,128)(2,1)}, bf16[4,352,352]{2,1,0:T(8,128)(2,1)}, u32[]{:S(2)}, u32[]{:S(2)}) collective-permute-start(bf16[4,352,352]{2,1,0:T(8,128)(2,1)} %collective-permute-done.21.refs_2_), channel_id=1, source_target_pairs={{0,16},{4,12},{8,24},{12,4},{16,0},{20,28},{24,8},{28,20},{1,17},{... | collective-permute-start | bytes 2973704 | tf_op jit(solution)/shard_map/ppermute | solution.py:1803
  190.7 46.0 %collective-permute-start.33 = (bf16[352,1536]{1,0:T(8,128)(2,1)}, bf16[352,1536]{1,0:T(8,128)(2,1)}, u32[]{:S(2)}, u32[]{:S(2)}) collective-permute-start(bf16[352,1536]{1,0:T(8,128)(2,1)} %collective-permute-done.31.refs_0_), channel_id=1, source_target_pairs={{0,16},{4,12},{8,24},{12,4},{16,0},{20,28},{24,8},{28,20},{1,17},{... | collective-permute-start | bytes 3244040 | tf_op jit(solution)/shard_map/ppermute | solution.py:1803
  193.6 44.8 %collective-permute-start.24 = (bf16[4,352,352]{2,1,0:T(8,128)(2,1)}, bf16[4,352,352]{2,1,0:T(8,128)(2,1)S(1)}, u32[]{:S(2)}, u32[]{:S(2)}) collective-permute-start(bf16[4,352,352]{2,1,0:T(8,128)(2,1)} %collective-permute-done.21.refs_2_), channel_id=1, source_target_pairs={{0,4},{4,0},{1,5},{5,1},{2,6},{6,2},{3,7},{7,3},{8,12},{12,8},{9,1... | collective-permute-start | bytes 2973704 | tf_op jit(solution)/shard_map/ppermute | solution.py:1796
  236.6 140.8 %collective-permute-start.41 = (bf16[4,176,704]{2,1,0:T(8,128)(2,1)}, bf16[4,176,704]{2,1,0:T(8,128)(2,1)}, u32[]{:S(2)}, u32[]{:S(2)}) collective-permute-start(bf16[4,176,704]{2,1,0:T(8,128)(2,1)} %constant_dynamic-slice_fusion.7), channel_id=1, source_target_pairs={{0,16},{4,12},{8,24},{12,4},{16,0},{20,28},{24,8},{28,20},{1,17},{... | collective-permute-start | bytes 2973704 | tf_op jit(solution)/shard_map/ppermute | solution.py:1802
  238.4 139.1 %collective-permute-start.34 = (bf16[352,1536]{1,0:T(8,128)(2,1)}, bf16[352,1536]{1,0:T(8,128)(2,1)}, u32[]{:S(2)}, u32[]{:S(2)}) collective-permute-start(bf16[352,1536]{1,0:T(8,128)(2,1)} %collective-permute-done.31.refs_0_), channel_id=1, source_target_pairs={{0,4},{4,0},{1,5},{5,1},{2,6},{6,2},{3,7},{7,3},{8,12},{12,8},{9,1... | collective-permute-start | bytes 3244040 | tf_op jit(solution)/shard_map/ppermute | solution.py:1796
  238.4 139.7 %collective-permute-start.35 = (bf16[352,1536]{1,0:T(8,128)(2,1)}, bf16[352,1536]{1,0:T(8,128)(2,1)}, u32[]{:S(2)}, u32[]{:S(2)}) collective-permute-start(bf16[352,1536]{1,0:T(8,128)(2,1)} %collective-permute-done.32.refs_1_), channel_id=1, source_target_pairs={{0,4},{4,0},{1,5},{5,1},{2,6},{6,2},{3,7},{7,3},{8,12},{12,8},{9,1... | collective-permute-start | bytes 3244040 | tf_op jit(solution)/shard_map/ppermute | solution.py:1796
  238.9 139.1 %collective-permute-start.42 = (bf16[4,176,704]{2,1,0:T(8,128)(2,1)}, bf16[4,176,704]{2,1,0:T(8,128)(2,1)}, u32[]{:S(2)}, u32[]{:S(2)}) collective-permute-start(bf16[4,176,704]{2,1,0:T(8,128)(2,1)} %collective-permute-done.40.refs_0_), channel_id=1, source_target_pairs={{0,16},{4,12},{8,24},{12,4},{16,0},{20,28},{24,8},{28,20},{1,17},{... | collective-permute-start | bytes 2973704 | tf_op jit(solution)/shard_map/ppermute | solution.py:1803
  239.0 139.1 %collective-permute-start.36 = (bf16[352,1536]{1,0:T(8,128)(2,1)}, bf16[352,1536]{1,0:T(8,128)(2,1)}, u32[]{:S(2)}, u32[]{:S(2)}) collective-permute-start(bf16[352,1536]{1,0:T(8,128)(2,1)} %collective-permute-done.33.refs_2_), channel_id=1, source_target_pairs={{0,4},{4,0},{1,5},{5,1},{2,6},{6,2},{3,7},{7,3},{8,12},{12,8},{9,1... | collective-permute-start | bytes 3244040 | tf_op jit(solution)/shard_map/ppermute | solution.py:1796
  377.4 181.7 %collective-permute-start.43 = (bf16[4,176,704]{2,1,0:T(8,128)(2,1)}, bf16[4,176,704]{2,1,0:T(8,128)(2,1)S(1)}, u32[]{:S(2)}, u32[]{:S(2)}) collective-permute-start(bf16[4,176,704]{2,1,0:T(8,128)(2,1)} %collective-permute-done.40.refs_0_), channel_id=1, source_target_pairs={{0,4},{4,0},{1,5},{5,1},{2,6},{6,2},{3,7},{7,3},{8,12},{12,8},{9,1... | collective-permute-start | bytes 2973704 | tf_op jit(solution)/shard_map/ppermute | solution.py:1796
  377.5 181.6 %collective-permute-start.44 = (bf16[4,176,704]{2,1,0:T(8,128)(2,1)}, bf16[4,176,704]{2,1,0:T(8,128)(2,1)S(1)}, u32[]{:S(2)}, u32[]{:S(2)}) collective-permute-start(bf16[4,176,704]{2,1,0:T(8,128)(2,1)} %collective-permute-done.41.refs_1_), channel_id=1, source_target_pairs={{0,4},{4,0},{1,5},{5,1},{2,6},{6,2},{3,7},{7,3},{8,12},{12,8},{9,1... | collective-permute-start | bytes 2973704 | tf_op jit(solution)/shard_map/ppermute | solution.py:1796
  378.0 181.1 %collective-permute-start.45 = (bf16[4,176,704]{2,1,0:T(8,128)(2,1)}, bf16[4,176,704]{2,1,0:T(8,128)(2,1)}, u32[]{:S(2)}, u32[]{:S(2)}) collective-permute-start(bf16[4,176,704]{2,1,0:T(8,128)(2,1)} %collective-permute-done.42.refs_2_), channel_id=1, source_target_pairs={{0,4},{4,0},{1,5},{5,1},{2,6},{6,2},{3,7},{7,3},{8,12},{12,8},{9,1... | collective-permute-start | bytes 2973704 | tf_op jit(solution)/shard_map/ppermute | solution.py:1796
  613.9 66.8 %collective-permute-start.50 = (f32[1,352]{1,0:T(1,128)S(1)}, f32[1,352]{1,0:T(1,128)S(1)}, u32[]{:S(2)}, u32[]{:S(2)}) collective-permute-start(f32[1,352]{1,0:T(1,128)S(1)} %get-tuple-element.136), channel_id=1, source_target_pairs={{0,8},{8,0},{16,24},{24,16},{1,9},{9,1},{17,25},{25,17},{2,10},{10... | collective-permute-start | bytes 4232 | tf_op jit(solution)/shard_map/ppermute | solution.py:1817
  614.0 67.0 %collective-permute-start.51 = (f32[1,352]{1,0:T(1,128)S(1)}, f32[1,352]{1,0:T(1,128)S(1)}, u32[]{:S(2)}, u32[]{:S(2)}) collective-permute-start(f32[1,352]{1,0:T(1,128)S(1)} %get-tuple-element.135), channel_id=1, source_target_pairs={{0,16},{8,24},{16,0},{24,8},{1,17},{9,25},{17,1},{25,9},{2,18},{10... | collective-permute-start | bytes 4232 | tf_op jit(solution)/shard_map/ppermute | solution.py:1817
  614.9 66.4 %collective-permute-start.52 = (f32[1,352]{1,0:T(1,128)S(1)}, f32[1,352]{1,0:T(1,128)S(1)}, u32[]{:S(2)}, u32[]{:S(2)}) collective-permute-start(f32[1,352]{1,0:T(1,128)S(1)} %get-tuple-element.134), channel_id=1, source_target_pairs={{0,24},{8,16},{16,8},{24,0},{1,25},{9,17},{17,9},{25,1},{2,26},{10... | collective-permute-start | bytes 4232 | tf_op jit(solution)/shard_map/ppermute | solution.py:1817
  (78 other events, 1108.7 us)
Sparse Core Ops, SparseCore 0:
  594.0 72.9 all-reduce.3

commit v2 on v1

--- a/solution.py
+++ b/solution.py
@@ -661,7 +661,7 @@
         return push(source, target, self.sems[2].at[slot], self.sems[3].at[slot], self.left)
 
 
-def line_reduce_all(line, steps, compute, partial_ref, from_left, from_right, stage_right, stage_left, finish):
+def line_reduce_all(line, steps, compute, partial_ref, from_left, from_right, stage_right, stage_left, finish, beside=None):
     me, count = line.me, line.count
     far = count - 1 - me
 
@@ -716,6 +716,8 @@
 
                 line.to_left(stage_left.at[slot], from_right.at[slot], slot).start()
 
+        if beside is not None:
+            beside(number)
         slot_f = number - lax.max(me, far)
 
         @pl.when((slot_f >= 0) & (slot_f < steps))
@@ -910,36 +912,6 @@
     if number == 2:
         return place + 2 - 4 * (place // 2)
     return 3 - place
-
-
-def assemble(target, own, pieces, offset, sem, lead=None):
-    dp = lax.axis_index("dp")
-    core = lax.axis_index("ctx")
-    rows = own.shape[-2]
-    half = rows // 2
-    copies = []
-
-    def view(ref, start, size, place):
-        if lead is None:
-            return ref.at[pl.ds(start, size), :]
-        return ref.at[lead[place], pl.ds(start, size), :]
-
-    copies.append(
-        pltpu.make_async_copy(
-            view(own, 0, rows, 0), view(target, pl.multiple_of(dp * rows, 16), rows, 1), sem
-        )
-    )
-    first = jnp.where(core == 0, xor_place(dp, 1), xor_place(dp, 2))
-    second = jnp.where(core == 0, xor_place(dp, 2), xor_place(dp, 1))
-    third = xor_place(dp, 3)
-    blocks = (first, second, third, second, first, third)
-    halves = (core, core, core, 1 - core, 1 - core, 1 - core)
-    for piece, block, which in zip(pieces, blocks, halves):
-        start = pl.multiple_of(block * rows + which * half, 16)
-        copies.append(
-            pltpu.make_async_copy(view(piece, offset, half, 0), view(target, start, half, 1), sem)
-        )
-    return copies
 
 
 def call(kernel, inputs, outs, scratch, collective=None, cost=None):
@@ -979,235 +951,34 @@
     return pl.ds(pl.multiple_of(index * size, size), size)
 
 
-def skip_forward(count, own, pieces, hidden, long_skip, part, part_gain, down, up, gain_row, shift_row):
-    tokens, width = hidden.shape
-    span = part.shape[1]
-    block = min(128, tokens)
-    chunk = min(64, tokens)
-    steps = tokens // chunk
-    each = block // chunk
-
-    def kernel(own_ref, *refs):
-        piece_refs = refs[:6]
-        (hid, lsk, par, pgain, a_ref, b_ref, gain, shift, skip_out, attn_in, w, partial_ref, from_left, from_right,
-         stage_right, stage_left, wsem, *sems) = refs[6:]
-        me = lax.axis_index("tensor")
-        line = Line(me, count, *sems)
-        for copy in assemble(w, own_ref, piece_refs, 0, wsem):
-            copy.start()
-        greet(line_partners(me, count))
-        whole_wait(w, wsem)
-
-        def compute(number):
-            @pl.when(number % each == 0)
-            def _():
-                rows = rows_of(number // each, block)
-                left = hid[rows, :].astype(F32)
-                right = lsk[rows, :].astype(F32)
-                mean = (jnp.sum(left, axis=-1, keepdims=True) + jnp.sum(right, axis=-1, keepdims=True)) / (2 * width)
-                spread = jnp.sum((left - mean) ** 2, axis=-1, keepdims=True)
-                spread += jnp.sum((right - mean) ** 2, axis=-1, keepdims=True)
-                inverse = lax.rsqrt(spread / (2 * width) + NORM_EPS)
-                x = ((par[rows, :].astype(F32) - mean) * inverse * pgain[...]).astype(BF)
-                u = dot_nt(x, a_ref[...]).astype(BF)
-                y = (dot_nt(x, w[...]) + dot_nn(u, b_ref[...])).astype(BF)
-                for piece in range(each):
-                    partial_ref[number + piece] = y[piece * chunk : (piece + 1) * chunk]
-
-        def finish(slot, total):
-            rows = rows_of(slot, chunk)
-            skip_out[rows, :] = total
-            normal, _ = stats(total)
-            attn_in[rows, :] = (normal * gain[...] + shift[...]).astype(BF)
-
-        line_reduce_all(line, steps, compute, partial_ref, from_left, from_right, stage_right, stage_left, finish)
-
-    buffers = [vmem(steps, chunk, width) for _ in range(5)]
-    return call(
-        kernel,
-        [(own, False)] + [(piece, False) for piece in pieces]
-        + [(array, True) for array in (hidden, long_skip, part, part_gain, down, up, gain_row, shift_row)],
-        [((tokens, width), F32, True), ((tokens, width), BF, True)],
-        [vmem(width, span)] + buffers + [dma()] + [dma(steps) for _ in range(4)],
-        collective=1,
-        cost=cost_of(2 * tokens * width * span, 40e6),
-    )
-
-
-def text_forward(heads, text, own_key, own_value, pieces, key_row, value_row, down, up_key, up_value):
-    tokens, width = text.shape
-    local = own_key.shape[1]
-
-    def kernel(own_k, own_v, *refs):
-        piece_refs = refs[:6]
-        t_ref, a_ref, bk, bv, out, w, wsem = refs[6:]
-        core = lax.axis_index("ctx")
-
-        @pl.when(core == 0)
-        def _():
-            for copy in assemble(w, own_k, piece_refs, key_row, wsem):
-                copy.start()
-
-        @pl.when(core == 1)
-        def _():
-            for copy in assemble(w, own_v, piece_refs, value_row, wsem):
-                copy.start()
-
-        whole_wait(w, wsem)
-        x = t_ref[...]
-        u = dot_nt(x, a_ref[...]).astype(BF)
-        y = dot_nn(x, w[...])
-
-        @pl.when(core == 0)
-        def _():
-            z = y + dot_nn(u[:, :RANK], bk[...])
-            for head in range(heads):
-                normal, inverse = stats(z[:, head * HD : (head + 1) * HD])
-                upper = inverse.astype(BF)
-                lower = (inverse - upper.astype(F32)).astype(BF)
-                out[head] = jnp.concatenate([normal.astype(BF), upper, lower], axis=1)
-
-        @pl.when(core == 1)
-        def _():
-            z = (y + dot_nn(u[:, RANK:], bv[...])).astype(BF)
-            filler = jnp.zeros((tokens, 2), BF)
-            for head in range(heads):
-                out[head] = jnp.concatenate([z[:, head * HD : (head + 1) * HD], filler], axis=1)
-
-    return call(
-        kernel,
-        [(own_key, False), (own_value, False)] + [(piece, False) for piece in pieces]
-        + [(array, True) for array in (text, down, up_key, up_value)],
-        [((heads, tokens, HD + 2), BF, True)],
-        [vmem(width, local), dma()],
-        cost=cost_of(2 * tokens * width * local, 3e6),
-    )[0]
-
-
-def attention_forward(count, heads, attn_in, own_list, pieces, offsets, down, ups, out_down, out_up):
-    tokens, width = attn_in.shape
-    local = own_list[0].shape[1]
-    share = tokens // count
-    block = min(128, tokens)
+def cross_forward(count, heads, summed, skip_out, query_weight, out_weight, skip_piece, text_kv, gains, down, up,
+                  out_down, out_up):
+    share, width = summed.shape
+    local = query_weight.shape[-1]
     scale = HD ** (-0.5)
-
-    def kernel(x_ref, *refs):
-        owns = refs[:4]
-        piece_refs = refs[4:10]
-        (a_ref, bq, bk, bv, ao, bo, q_out, keys, values, low_out, log_out, inv_q, inv_k, summed, wq, wk, wv, wo,
-         partial_ref, from_left, from_right, stage_right, stage_left, wsem, xsend, xrecv, *sems) = refs[10:]
+    rows, span = skip_piece.shape
+
+    def kernel(sum_ref, skip_ref, hbm_q, hbm_o, piece, kv, gain, a_ref, b_ref, ao, bo, first_out, second_out, in_out,
+               mlp_out, q_out, inv_out, log_out, low_out, uo_out, skip_half, wq, wo, wsem, zsend, zrecv):
         me = lax.axis_index("tensor")
         core = lax.axis_index("ctx")
-        line = Line(me, count, *sems)
-        for number, (w, own) in enumerate(zip((wq, wk, wv, wo), owns)):
-            for copy in assemble(w, own, piece_refs, offsets[number], wsem.at[number]):
-                copy.start()
-        peer = {"ctx": 1 - core}
-        greet(line_partners(me, count) + [(core >= 0, peer)])
-        for number, w in enumerate((wq, wk, wv)):
-            whole_wait(w, wsem.at[number])
-
-        def project(number, carry):
-            rows = rows_of(number, block)
-            x = x_ref[rows, :]
-            u = dot_nt(x, a_ref[...]).astype(BF)
-            yq = dot_nn(x, wq[...]) + dot_nn(u[:, :RANK], bq[...])
-            yk = dot_nn(x, wk[...]) + dot_nn(u[:, RANK : 2 * RANK], bk[...])
-            yv = (dot_nn(x, wv[...]) + dot_nn(u[:, 2 * RANK :], bv[...])).astype(BF)
-            for head in range(heads):
-                span = slice(head * HD, (head + 1) * HD)
-                normal, inverse = stats(yq[:, span])
-                q_out[head, rows, :] = normal.astype(BF)
-                inv_q[head, rows, :] = inverse
-                normal, inverse = stats(yk[:, span])
-                keys[core, head, rows, :] = normal.astype(BF)
-                inv_k[head, rows, :] = inverse
-                values[core, head, rows, :] = yv[:, span]
-            return carry
-
-        lax.fori_loop(0, tokens // block, project, 0)
-        swaps = [
-            push(ref.at[core], ref.at[core], xsend.at[number], xrecv.at[number], peer)
-            for number, ref in enumerate((keys, values))
+        loads = [
+            pltpu.make_async_copy(source, target, wsem.at[number])
+            for number, (source, target) in enumerate(((hbm_q, wq), (hbm_o, wo)))
         ]
-        for swap in swaps:
-            swap.start()
-        whole_wait(wo, wsem.at[3])
-        for number, ref in enumerate((keys, values)):
-            push(ref.at[1 - core], ref.at[1 - core], xsend.at[number], xrecv.at[number], peer).wait_recv()
-
-        def attend(place, carry):
-            dest = scatter_order(me, count, place)
-            rows = rows_of(dest, share)
-            outs = []
-            for head in range(heads):
-                q = q_out[head, rows, :]
-                s0 = dot_nt(q, keys[0, head]) * scale
-                s1 = dot_nt(q, keys[1, head]) * scale
-                top = jnp.maximum(jnp.max(s0, axis=-1, keepdims=True), jnp.max(s1, axis=-1, keepdims=True))
-                e0 = jnp.exp(s0 - top)
-                e1 = jnp.exp(s1 - top)
-                total = jnp.sum(e0, axis=-1, keepdims=True) + jnp.sum(e1, axis=-1, keepdims=True)
-                share_of = 1.0 / total
-                p0 = (e0 * share_of).astype(BF)
-                p1 = (e1 * share_of).astype(BF)
-                outs.append(dot_nn(p0, values[0, head]) + dot_nn(p1, values[1, head]))
-                log_out[head, rows, :] = top + jnp.log(total)
-            low = jnp.concatenate(outs, axis=1).astype(BF)
-            low_out[rows, :] = low
-            u = dot_nt(low, ao[...]).astype(BF)
-            partial_ref[dest] = (dot_nt(low, wo[...]) + dot_nn(u, bo[...])).astype(BF)
-
-            @pl.when(place < count - 1)
-            def _():
-                line_scatter_step(line, place, partial_ref, from_left, from_right, stage_right, stage_left)
-
-            return carry
-
-        lax.fori_loop(0, count, attend, 0)
-        line_scatter_finish(line, partial_ref, from_left, from_right, stage_right, stage_left, summed)
-        for swap in swaps:
-            swap.wait_send()
-
-    buffers = [vmem(count, share, width) for _ in range(5)]
-    return call(
-        kernel,
-        [(attn_in, True)] + [(own, False) for own in own_list] + [(piece, False) for piece in pieces]
-        + [(array, True) for array in (down, *ups, out_down, out_up)],
-        [
-            ((heads, tokens, HD), BF, True),
-            ((2, heads, tokens, HD), BF, True),
-            ((2, heads, tokens, HD), BF, True),
-            ((tokens, local), BF, True),
-            ((heads, tokens, 1), F32, True),
-            ((heads, tokens, 1), F32, True),
-            ((heads, tokens, 1), F32, True),
-            ((share, width), F32, True),
-        ],
-        [vmem(width, local) for _ in range(4)] + buffers + [dma(4), dma(2), dma(2)] + [dma(count) for _ in range(4)],
-        collective=2,
-        cost=cost_of(8 * tokens * width * local, 60e6),
-    )
-
-
-def cross_forward(count, heads, summed, skip_out, query_stack, out_stack, keys, values, gains, down, up, out_down,
-                  out_up, offsets):
-    share, width = summed.shape
-    local = query_stack[0].shape[-1]
-    scale = HD ** (-0.5)
-    text = keys.shape[2]
-
-    def kernel(sum_ref, skip_ref, *refs):
-        own_q, own_o = refs[:2]
-        piece_refs = refs[2:8]
-        (kc, vc, gain, a_ref, b_ref, ao, bo, first_out, second_out, in_out, mlp_out, q_out, inv_out, log_out, low_out,
-         uo_out, wq, wo, wsem) = refs[8:]
-        me = lax.axis_index("tensor")
-        for number, (w, own) in enumerate(((wq, own_q), (wo, own_o))):
-            for far in range(count):
-                lead = (far, xor_place(me, far))
-                for copy in assemble(w, own, piece_refs, offsets[number], wsem.at[number], lead):
-                    copy.start()
+        for load in loads:
+            load.start()
+        half = pl.ds(pl.multiple_of(core * (rows // 2), 16), rows // 2)
+        own = pltpu.make_async_copy(piece.at[half, :], skip_half.at[me], wsem.at[2])
+        own.start()
+        z_peers = [{"tensor": xor_place(me, number)} for number in range(1, count)]
+        greet([(core >= 0, device) for device in z_peers])
+        sends = [
+            push(piece.at[half, :], skip_half.at[me], zsend.at[number], zrecv.at[number], device)
+            for number, device in enumerate(z_peers)
+        ]
+        for send in sends:
+            send.start()
         first = skip_ref[rows_of(me, share), :] + sum_ref[...]
         first_out[...] = first
         normal, _ = stats(first)
@@ -1215,8 +986,8 @@
         in_out[...] = x
         u = dot_nt(x, a_ref[...]).astype(BF)
         second_out[...] = first
-        whole_wait(wq, wsem.at[0])
-        whole_wait(wo, wsem.at[1])
+        for load in loads:
+            load.wait()
 
         def chunk(place, u_low):
             y = dot_nn(x, wq[place]) + dot_nn(u, b_ref[place])
@@ -1226,12 +997,12 @@
                 q = normal.astype(BF)
                 q_out[place, head] = q
                 inv_out[place, head] = inverse
-                s = dot_nt(q, kc[place, head, :, :HD]) * scale
+                s = dot_nt(q, kv[0, place, head, :, :HD]) * scale
                 top = jnp.max(s, axis=-1, keepdims=True)
                 e = jnp.exp(s - top)
                 total = jnp.sum(e, axis=-1, keepdims=True)
                 p = (e * (1.0 / total)).astype(BF)
-                outs.append(dot_nn(p, vc[place, head, :, :HD]))
+                outs.append(dot_nn(p, kv[1, place, head, :, :HD]))
                 log_out[place, head] = top + jnp.log(total)
             low = jnp.concatenate(outs, axis=1).astype(BF)
             low_out[place] = low
@@ -1244,12 +1015,17 @@
         second_out[...] = second
         normal, _ = stats(second)
         mlp_out[...] = (normal * gain[2:3, :]).astype(BF)
+        own.wait()
+        for number in range(count - 1):
+            arrived = skip_half.at[xor_place(me, number + 1)]
+            push(arrived, arrived, zsend.at[number], zrecv.at[number], z_peers[number]).wait_recv()
+        for send in sends:
+            send.wait_send()
 
     return call(
         kernel,
-        [(summed, True), (skip_out, True), (query_stack[0], False), (out_stack[0], False)]
-        + [(piece, False) for piece in query_stack[1]]
-        + [(array, True) for array in (keys, values, gains, down, up, out_down, out_up)],
+        [(summed, True), (skip_out, True), (query_weight, False), (out_weight, False), (skip_piece, False)]
+        + [(array, True) for array in (text_kv, gains, down, up, out_down, out_up)],
         [
             ((share, width), F32, True),
             ((share, width), F32, True),
@@ -1260,34 +1036,46 @@
             ((count, heads, share, 1), F32, True),
             ((count, share, local), BF, True),
             ((share, RANK), BF, True),
+            ((count, rows // 2, span), BF, False),
         ],
-        [vmem(count, width, local), vmem(count, width, local), dma(2)],
+        [vmem(count, width, local), vmem(count, width, local), dma(3), dma(count), dma(count)],
+        collective=6,
         cost=cost_of(4 * share * width * width, 20e6),
     )
 
 
-def feed_forward(count, block_in, cotangent, second, own_up, own_down, pieces, offsets, up_a, up_b, down_a, down_b):
+def feed_forward(count, block_in, cotangent, second, up_weight, down_weight, skip_half, up_a, up_b, down_a, down_b):
     share, width = block_in.shape
     tokens = cotangent.shape[0]
-    hidden_units = own_up.shape[1]
-
-    def kernel(x_ref, cot, sec, own_u, own_d, *refs):
-        piece_refs = refs[:6]
-        (ua, ub, da, db, summed, down_out, g_ua, g_ub, g_da, g_db, slots, wu, wd, partial_ref, from_left, from_right,
-         stage_right, stage_left, wsem, *sems) = refs[6:]
+    hidden_units = up_weight.shape[1]
+    rows = 2 * skip_half.shape[1]
+    span = skip_half.shape[2]
+
+    def kernel(x_ref, cot, sec, hbm_u, hbm_d, shalf, ua, ub, da, db, summed, down_out, g_ua, g_ub, g_da, g_db, skip_all,
+               slots, wu, wd, partial_ref, from_left, from_right, stage_right, stage_left, wsem, wsend, wrecv, *sems):
         me = lax.axis_index("tensor")
+        core = lax.axis_index("ctx")
+        dp = lax.axis_index("dp")
         gather_line = Line(me, count, *sems[:4])
         scatter_line = Line(me, count, *sems[4:])
-        for number, (w, own) in enumerate(((wu, own_u), (wd, own_d))):
-            for copy in assemble(w, own, piece_refs, offsets[number], wsem.at[number]):
-                copy.start()
+        loads = [
+            pltpu.make_async_copy(source, target, wsem.at[number])
+            for number, (source, target) in enumerate(((hbm_u, wu), (hbm_d, wd)))
+        ]
+        for load in loads:
+            load.start()
+        skip = Shared(skip_all, rows, (wsend, wrecv, 0), stacked=True)
+        own = pltpu.make_async_copy(shalf, skip.view(dp, core), wsem.at[2])
+        own.start()
         slots[me] = x_ref[...]
         for ref in (g_ua, g_ub, g_da, g_db):
             ref[...] = jnp.zeros_like(ref)
-        greet(line_partners(me, count))
+        peers = [{"dp": xor_place(dp, 1)}, {"dp": xor_place(dp, 2)}, {"ctx": 1 - core}]
+        greet(line_partners(me, count) + [(core >= 0, device) for device in peers])
         line_gather_step(gather_line, 0, slots)
-        whole_wait(wu, wsem.at[0])
-        whole_wait(wd, wsem.at[1])
+        skip.send_own(shalf)
+        for load in loads:
+            load.wait()
 
         def compute(block):
             rows = rows_of(block, share)
@@ -1335,20 +1123,30 @@
             return lax.fori_loop(0, 2, side, carry)
 
         lax.fori_loop(1, count, step, 0)
+        own.wait()
+        skip.wait(0)
+        skip.forward()
+        skip.swap(0)
+        skip.swap(3)
 
         def scatter(number, carry):
             line_scatter_step(scatter_line, number, partial_ref, from_left, from_right, stage_right, stage_left)
             return carry
 
         lax.fori_loop(0, count - 1, scatter, 0)
+        skip.wait(1)
+        skip.swap(1)
         line_gather_drain(gather_line, slots)
         line_scatter_finish(scatter_line, partial_ref, from_left, from_right, stage_right, stage_left, summed)
+        skip.wait(2)
+        skip.swap(2)
+        skip.wait_swaps()
+        skip.drain()
 
     buffers = [vmem(count, share, width) for _ in range(5)]
     return call(
         kernel,
-        [(block_in, True), (cotangent, True), (second, True), (own_up, False), (own_down, False)]
-        + [(piece, False) for piece in pieces]
+        [(block_in, True), (cotangent, True), (second, True), (up_weight, False), (down_weight, False), (skip_half, False)]
         + [(array, True) for array in (up_a, up_b, down_a, down_b)],
         [
             ((share, width), F32, True),
@@ -1357,11 +1155,445 @@
             ((RANK, hidden_units), F32, True),
             ((RANK, hidden_units), F32, True),
             ((RANK, width), F32, True),
+            ((count, 4 * rows, span), BF, False),
         ],
         [vmem(count, share, width), vmem(width, hidden_units), vmem(width, hidden_units)]
-        + buffers + [dma(2)] + [dma(count) for _ in range(8)],
+        + buffers + [dma(3), dma(1, 7), dma(1, 7)] + [dma(count) for _ in range(8)],
         collective=3,
         cost=cost_of(8 * tokens * width * hidden_units, 60e6),
+    )
+
+
+class Shared:
+    def __init__(self, target, rows, sems, stacked=False, split=True):
+        self.target, self.rows, self.stacked, self.split = target, rows, stacked, split
+        self.send_sem, self.recv_sem, self.index = sems
+        dp, core = lax.axis_index("dp"), lax.axis_index("ctx")
+        self.dp, self.core = dp, core
+        self.first = jnp.where(core == 0, xor_place(dp, 1), xor_place(dp, 2))
+        self.second = jnp.where(core == 0, xor_place(dp, 2), xor_place(dp, 1))
+        self.third = xor_place(dp, 3)
+
+    def view(self, block, which):
+        size = self.rows // 2 if self.split else self.rows
+        start = block * self.rows + (which * size if self.split else 0)
+        rows = pl.ds(pl.multiple_of(start, 16), size)
+        return self.target.at[:, rows, :] if self.stacked else self.target.at[rows, :]
+
+    def copy(self, number, source, block, which, device):
+        target = self.view(block, which)
+        source = target if source is None else source
+        return push(source, target, self.send_sem.at[self.index, number], self.recv_sem.at[self.index, number], device)
+
+    def send_own(self, source=None):
+        self.copy(0, source, self.dp, self.core, {"dp": self.first}).start()
+        self.copy(1, source, self.dp, self.core, {"dp": self.second}).start()
+
+    def blocks(self):
+        return [self.first, self.second, self.third] + ([self.dp] if self.stacked else [])
+
+    def wait(self, number):
+        self.copy(number, None, self.blocks()[number], self.core, {"dp": self.first}).wait_recv()
+
+    def forward(self):
+        self.copy(2, None, self.first, self.core, {"dp": self.second}).start()
+
+    def swap(self, number):
+        self.copy(3 + number, None, self.blocks()[number], self.core, {"ctx": 1 - self.core}).start()
+
+    def wait_swaps(self):
+        other = [self.second, self.first, self.third, self.dp]
+        for number in range(len(self.blocks())):
+            self.copy(3 + number, None, other[number], 1 - self.core, {"ctx": 1 - self.core}).wait_recv()
+
+    def drain(self):
+        for number in range(3 + (len(self.blocks()) if self.split else 0)):
+            self.copy(number, None, self.dp, self.core, {"dp": self.first}).wait_send()
+
+
+def front(count, heads, act, tag, hidden, long_skip, part, part_gain, text, weights, mods, gain_row, skip_ab, text_ab,
+          qkv_ab, out_ab):
+    tokens, width = hidden.shape
+    span = part.shape[1]
+    words, text_width = text.shape
+    local = weights["q"].shape[1]
+    units = weights["up"].shape[1]
+    share = tokens // count
+    block = min(128, tokens)
+    chunk = min(64, tokens)
+    steps = tokens // chunk
+    each = block // chunk
+    scale = HD ** (-0.5)
+    rows = weights["q"].shape[0]
+    text_rows = weights["ck"].shape[0]
+    mod_rows = mods[0].shape[0]
+
+    def kernel(skip_own, q_own, k_own, v_own, o_own, ck_own, cv_own, cq_own, co_own, up_own, dn_own,
+               act_ref, tag_ref, hid, lsk, par, pgain, t_ref, wm, ma, mb, gain, sa, sb, ta, tk, tv, qa, qb, kb, vb, oa, ob,
+               skip_out, attn_in, q_out, keys, values, low_out, log_out, inv_q, inv_k, summed, act_all, text_kv,
+               wq, wk, wv, wo, wcq, wco, wup, wdn,
+               wskip, wtext, mod_in, mod_slice, mod_out, partial_a, left_a, right_a, sr_a, sl_a,
+               partial_b, left_b, right_b, sr_b, sl_b, wsend, wrecv, local_sem, zsend, zrecv, msend, mrecv, tsend, trecv,
+               xsend, xrecv, *sems):
+        me = lax.axis_index("tensor")
+        core = lax.axis_index("ctx")
+        dp = lax.axis_index("dp")
+        always = core >= 0
+        peer = {"ctx": 1 - core}
+        dp_peers = [{"dp": xor_place(dp, number)} for number in (1, 2, 3)]
+        z_peers = [{"tensor": xor_place(me, number)} for number in range(1, count)]
+        reduce_line = Line(me, count, *sems[:4])
+        scatter_line = Line(me, count, *sems[4:])
+
+        def sems_of(number):
+            return (wsend, wrecv, number)
+
+        skip = Shared(wskip, rows, sems_of(0))
+        shared = {
+            name: Shared(target, rows, sems_of(number))
+            for name, target, number in (("q", wq, 1), ("k", wk, 2), ("v", wv, 3), ("o", wo, 4))
+        }
+        words_w = Shared(wtext, text_rows, sems_of(5), split=False)
+        cross = [Shared(wcq, rows, sems_of(6), stacked=True), Shared(wco, rows, sems_of(7), stacked=True)]
+        wide = [Shared(wup, rows, sems_of(8)), Shared(wdn, rows, sems_of(9))]
+        owns = {"q": q_own, "k": k_own, "v": v_own, "o": o_own}
+        half = pl.ds(pl.multiple_of(core * (rows // 2), 16), rows // 2)
+        mine = pl.ds(pl.multiple_of(dp * rows, 16), rows)
+        my_half = pl.ds(pl.multiple_of(dp * rows + core * (rows // 2), 16), rows // 2)
+
+        places = [
+            pltpu.make_async_copy(source, target.at[mine, :], local_sem.at[number])
+            for number, (source, target) in enumerate(
+                ((skip_own, wskip), (q_own, wq), (k_own, wk), (v_own, wv), (o_own, wo), (up_own, wup), (dn_own, wdn))
+            )
+        ]
+        for place in places:
+            place.start()
+        crossing = [
+            pltpu.make_async_copy(source.at[half, :], target.at[me, my_half, :], local_sem.at[7 + number])
+            for number, (source, target) in enumerate(((cq_own, wcq), (co_own, wco)))
+        ]
+        text_mine = pl.ds(pl.multiple_of(dp * text_rows, 16), text_rows)
+
+        def text_place(source):
+            return pltpu.make_async_copy(source, wtext.at[text_mine, :], local_sem.at[9])
+
+        @pl.when(core == 0)
+        def _():
+            text_place(ck_own).start()
+
+        @pl.when(core == 1)
+        def _():
+            text_place(cv_own).start()
+
+        for place in crossing:
+            place.start()
+        act_all[dp] = jnp.concatenate([act_ref[...].astype(F32), tag_ref[...]], axis=1)
+        greet([(always, device) for device in dp_peers + z_peers + [peer]])
+        skip.send_own(skip_own.at[half, :])
+
+        def z_copies(number):
+            return [
+                push(source.at[half, :], target.at[me, my_half, :], zsend.at[which, number], zrecv.at[which, number],
+                     z_peers[number])
+                for which, (source, target) in enumerate(((cq_own, wcq), (co_own, wco)))
+            ]
+
+        for number in range(count - 1):
+            for copy in z_copies(number):
+                copy.start()
+        spread = [
+            push(act_all.at[dp], act_all.at[dp], msend.at[0, number], mrecv.at[0, number], device)
+            for number, device in enumerate(dp_peers)
+        ]
+        for copy in spread:
+            copy.start()
+        skip.wait(0)
+        skip.forward()
+        for name in ("q", "k", "v", "o"):
+            shared[name].send_own(owns[name].at[half, :])
+
+        @pl.when(core == 0)
+        def _():
+            words_w.send_own(ck_own)
+
+        @pl.when(core == 1)
+        def _():
+            words_w.send_own(cv_own)
+
+        skip.swap(0)
+
+        for number in (1, 2, 3):
+            source = act_all.at[xor_place(dp, number)]
+            push(source, source, msend.at[0, number - 1], mrecv.at[0, number - 1], dp_peers[number - 1]).wait_recv()
+        for owner in range(4):
+            @pl.when(dp == owner)
+            def _(owner=owner):
+                span_of = slice(owner * mod_rows, (owner + 1) * mod_rows)
+                for sequence in range(4):
+                    mod_slice[sequence : sequence + 1, :] = act_all[sequence, :, span_of]
+
+        products = dot_nn(mod_slice[...].astype(BF), wm[...])
+        for sequence in range(4):
+            mod_out[sequence] = products[sequence : sequence + 1]
+        backs = [
+            push(mod_out.at[xor_place(dp, number)], mod_in.at[dp], msend.at[1, number - 1], mrecv.at[1, number - 1],
+                 dp_peers[number - 1])
+            for number in (1, 2, 3)
+        ]
+        for copy in backs:
+            copy.start()
+        skip.wait(1)
+        skip.swap(1)
+        mod_in[dp] = mod_out[dp]
+        mod_u = dot_nt(act_ref[...], ma[...]).astype(BF)
+        mod_low = dot_nn(mod_u, mb[...])
+        for number in (1, 2, 3):
+            target = mod_in.at[xor_place(dp, number)]
+            push(target, target, msend.at[1, number - 1], mrecv.at[1, number - 1], dp_peers[number - 1]).wait_recv()
+        shift = mod_in[0] + mod_in[1] + mod_in[2] + mod_in[3] + mod_low
+        skip.wait(2)
+        skip.swap(2)
+        places[0].wait()
+        skip.wait_swaps()
+
+        def compute(number):
+            @pl.when(number % each == 0)
+            def _():
+                here = rows_of(number // each, block)
+                left = hid[here, :].astype(F32)
+                right = lsk[here, :].astype(F32)
+                mean = (jnp.sum(left, axis=-1, keepdims=True) + jnp.sum(right, axis=-1, keepdims=True)) / (2 * width)
+                spread = jnp.sum((left - mean) ** 2, axis=-1, keepdims=True)
+                spread += jnp.sum((right - mean) ** 2, axis=-1, keepdims=True)
+                inverse = lax.rsqrt(spread / (2 * width) + NORM_EPS)
+                x = ((par[here, :].astype(F32) - mean) * inverse * pgain[...]).astype(BF)
+                u = dot_nt(x, sa[...]).astype(BF)
+                y = (dot_nt(x, wskip[...]) + dot_nn(u, sb[...])).astype(BF)
+                for piece in range(each):
+                    partial_a[number + piece] = y[piece * chunk : (piece + 1) * chunk]
+
+        def finish(slot, total):
+            here = rows_of(slot, chunk)
+            skip_out[here, :] = total
+            normal, _ = stats(total)
+            attn_in[here, :] = (normal * gain[...] + shift).astype(BF)
+
+        def beside(number):
+            @pl.when(number == 3)
+            def _():
+                for weight in (*shared.values(), words_w):
+                    weight.wait(0)
+                    weight.forward()
+                for weight in shared.values():
+                    weight.swap(0)
+
+            @pl.when(number == 4)
+            def _():
+                for weight in (*shared.values(), words_w):
+                    weight.wait(1)
+                for weight in shared.values():
+                    weight.swap(1)
+
+            @pl.when(number == 6)
+            def _():
+                for place in crossing:
+                    place.wait()
+                for other in range(count - 1):
+                    for which, target in enumerate((wcq, wco)):
+                        block_in = target.at[xor_place(me, other + 1), my_half, :]
+                        push(block_in, block_in, zsend.at[which, other], zrecv.at[which, other], z_peers[other]).wait_recv()
+                for weight in cross:
+                    weight.send_own()
+
+            @pl.when(number == 7)
+            def _():
+                for weight in (*shared.values(), words_w):
+                    weight.wait(2)
+                for weight in shared.values():
+                    weight.swap(2)
+
+        line_reduce_all(reduce_line, steps, compute, partial_a, left_a, right_a, sr_a, sl_a, finish, beside)
+
+        @pl.when(core == 0)
+        def _():
+            text_place(ck_own).wait()
+
+        @pl.when(core == 1)
+        def _():
+            text_place(cv_own).wait()
+
+        x = t_ref[...]
+        u = dot_nt(x, ta[...]).astype(BF)
+        y = dot_nn(x, wtext[...])
+
+        @pl.when(core == 0)
+        def _():
+            z = y + dot_nn(u[:, :RANK], tk[...])
+            for head in range(heads):
+                normal, inverse = stats(z[:, head * HD : (head + 1) * HD])
+                upper = inverse.astype(BF)
+                lower = (inverse - upper.astype(F32)).astype(BF)
+                text_kv[0, me, head] = jnp.concatenate([normal.astype(BF), upper, lower], axis=1)
+
+        @pl.when(core == 1)
+        def _():
+            z = (y + dot_nn(u[:, RANK:], tv[...])).astype(BF)
+            filler = jnp.zeros((words, 2), BF)
+            for head in range(heads):
+                text_kv[1, me, head] = jnp.concatenate([z[:, head * HD : (head + 1) * HD], filler], axis=1)
+
+        texts = [
+            push(text_kv.at[core, me], text_kv.at[core, me], tsend.at[number], trecv.at[number], z_peers[number])
+            for number in range(count - 1)
+        ]
+        for copy in texts:
+            copy.start()
+
+        for number in range(1, 5):
+            places[number].wait()
+        for weight in shared.values():
+            weight.wait_swaps()
+
+        def project(number, carry):
+            here = rows_of(number, block)
+            x = attn_in[here, :]
+            u = dot_nt(x, qa[...]).astype(BF)
+            yq = dot_nn(x, wq[...]) + dot_nn(u[:, :RANK], qb[...])
+            yk = dot_nn(x, wk[...]) + dot_nn(u[:, RANK : 2 * RANK], kb[...])
+            yv = (dot_nn(x, wv[...]) + dot_nn(u[:, 2 * RANK :], vb[...])).astype(BF)
+            for head in range(heads):
+                span_of = slice(head * HD, (head + 1) * HD)
+                normal, inverse = stats(yq[:, span_of])
+                q_out[head, here, :] = normal.astype(BF)
+                inv_q[head, here, :] = inverse
+                normal, inverse = stats(yk[:, span_of])
+                keys[core, head, here, :] = normal.astype(BF)
+                inv_k[head, here, :] = inverse
+                values[core, head, here, :] = yv[:, span_of]
+            return carry
+
+        lax.fori_loop(0, tokens // block, project, 0)
+        swaps = [
+            push(ref.at[core], ref.at[core], xsend.at[number], xrecv.at[number], peer)
+            for number, ref in enumerate((keys, values))
+        ]
+        for swap in swaps:
+            swap.start()
+        for weight in cross:
+            weight.wait(0)
+            weight.forward()
+            weight.swap(0)
+            weight.swap(3)
+        for weight, own in zip(wide, (up_own, dn_own)):
+            weight.send_own(own.at[half, :])
+        for number, ref in enumerate((keys, values)):
+            push(ref.at[1 - core], ref.at[1 - core], xsend.at[number], xrecv.at[number], peer).wait_recv()
+
+        def attend(place, carry):
+            dest = scatter_order(me, count, place)
+            here = rows_of(dest, share)
+            outs = []
+            for head in range(heads):
+                q = q_out[head, here, :]
+                s0 = dot_nt(q, keys[0, head]) * scale
+                s1 = dot_nt(q, keys[1, head]) * scale
+                top = jnp.maximum(jnp.max(s0, axis=-1, keepdims=True), jnp.max(s1, axis=-1, keepdims=True))
+                e0 = jnp.exp(s0 - top)
+                e1 = jnp.exp(s1 - top)
+                total = jnp.sum(e0, axis=-1, keepdims=True) + jnp.sum(e1, axis=-1, keepdims=True)
+                share_of = 1.0 / total
+                p0 = (e0 * share_of).astype(BF)
+                p1 = (e1 * share_of).astype(BF)
+                outs.append(dot_nn(p0, values[0, head]) + dot_nn(p1, values[1, head]))
+                log_out[head, here, :] = top + jnp.log(total)
+            low = jnp.concatenate(outs, axis=1).astype(BF)
+            low_out[here, :] = low
+            u = dot_nt(low, oa[...]).astype(BF)
+            partial_b[dest] = (dot_nt(low, wo[...]) + dot_nn(u, ob[...])).astype(BF)
+
+            @pl.when(place < count - 1)
+            def _():
+                line_scatter_step(scatter_line, place, partial_b, left_b, right_b, sr_b, sl_b)
+
+            @pl.when(place == 1)
+            def _():
+                for weight in cross:
+                    weight.wait(1)
+                    weight.swap(1)
+                for number in range(count - 1):
+                    arrived = text_kv.at[core, xor_place(me, number + 1)]
+                    push(arrived, arrived, tsend.at[number], trecv.at[number], z_peers[number]).wait_recv()
+                push(text_kv.at[core], text_kv.at[core], tsend.at[count - 1], trecv.at[count - 1], peer).start()
+
+            @pl.when(place == 2)
+            def _():
+                for weight in cross:
+                    weight.wait(2)
+                    weight.swap(2)
+
+            return carry
+
+        lax.fori_loop(0, count, attend, 0)
+        for weight in wide:
+            weight.wait(0)
+            weight.forward()
+            weight.swap(0)
+        for weight in wide:
+            weight.wait(1)
+            weight.swap(1)
+        line_scatter_finish(scatter_line, partial_b, left_b, right_b, sr_b, sl_b, summed)
+        for weight in wide:
+            weight.wait(2)
+            weight.swap(2)
+        others = text_kv.at[1 - core]
+        push(others, others, tsend.at[count - 1], trecv.at[count - 1], peer).wait_recv()
+        for weight in cross + wide:
+            weight.wait_swaps()
+        places[5].wait()
+        places[6].wait()
+        for weight in (skip, *shared.values(), words_w, *cross, *wide):
+            weight.drain()
+        for number in range(count - 1):
+            for copy in z_copies(number):
+                copy.wait_send()
+        for copy in spread + backs + texts:
+            copy.wait_send()
+        push(text_kv.at[core], text_kv.at[core], tsend.at[count - 1], trecv.at[count - 1], peer).wait_send()
+        for swap in swaps:
+            swap.wait_send()
+
+    names = ("skip", "q", "k", "v", "o", "ck", "cv", "cq", "co", "up", "dn")
+    return call(
+        kernel,
+        [(weights[name], False) for name in names]
+        + [(array, True) for array in (act, tag, hidden, long_skip, part, part_gain, text, *mods, gain_row, *skip_ab,
+                                       *text_ab, *qkv_ab, *out_ab)],
+        [
+            ((tokens, width), F32, True),
+            ((tokens, width), BF, True),
+            ((heads, tokens, HD), BF, True),
+            ((2, heads, tokens, HD), BF, True),
+            ((2, heads, tokens, HD), BF, True),
+            ((tokens, local), BF, True),
+            ((heads, tokens, 1), F32, True),
+            ((heads, tokens, 1), F32, True),
+            ((heads, tokens, 1), F32, True),
+            ((share, width), F32, True),
+            ((4, 1, width + 128), F32, True),
+            ((2, count, heads, words, HD + 2), BF, True),
+        ]
+        + [((width, local), BF, True) for _ in range(4)]
+        + [((count, width, local), BF, False) for _ in range(2)]
+        + [((width, units), BF, False) for _ in range(2)],
+        [vmem(width, span), vmem(text_width, local), vmem(4, 1, width, dtype=F32), vmem(4, mod_rows, dtype=F32),
+         vmem(4, 1, width, dtype=F32)]
+        + [vmem(steps, chunk, width) for _ in range(5)] + [vmem(count, share, width) for _ in range(5)]
+        + [dma(10, 7), dma(10, 7), dma(10), dma(2, count), dma(2, count), dma(2, 3), dma(2, 3), dma(count), dma(count),
+           dma(2), dma(2)]
+        + [dma(steps) for _ in range(4)] + [dma(count) for _ in range(4)],
+        collective=1,
+        cost=cost_of(8 * tokens * width * local, 60e6),
     )
 
 
@@ -1374,24 +1606,22 @@
 
 
 def cross_backward(count, heads, g_in, cotangent, first, second, block_in, query, inverses, logs, low, u_low, text,
-                   query_stack, out_stack, keys, values, gains, down, up, out_down, out_up, text_down, up_key,
-                   up_value, offsets):
+                   query_weight, out_weight, text_kv, gains, down, up, out_down, out_up, text_down, up_key, up_value):
     share, width = g_in.shape
-    local = query_stack[0].shape[-1]
+    local = query_weight.shape[-1]
     words, text_width = text.shape
     scale = HD ** (-0.5)
 
-    def kernel(g_ref, cot, first_ref, second_ref, x_ref, q_ref, inv_ref, log_ref, low_ref, uo_ref, t_ref, *refs):
-        own_q, own_o = refs[:2]
-        piece_refs = refs[2:8]
-        (kc, vc, gain, a_ref, b_ref, ao, bo, at, bk, bv, g_first, ga_q, gb_q, ga_k, gb_k, ga_v, gb_v, ga_o, gb_o,
-         acc, wq, wo, wsem) = refs[8:]
+    def kernel(g_ref, cot, first_ref, second_ref, x_ref, q_ref, inv_ref, log_ref, low_ref, uo_ref, t_ref, hbm_q, hbm_o,
+               kv, gain, a_ref, b_ref, ao, bo, at, bk, bv, g_first, ga_q, gb_q, ga_k, gb_k, ga_v, gb_v, ga_o, gb_o,
+               acc, wq, wo, wsem):
         me = lax.axis_index("tensor")
-        for number, (w, own) in enumerate(((wq, own_q), (wo, own_o))):
-            for far in range(count):
-                lead = (far, xor_place(me, far))
-                for copy in assemble(w, own, piece_refs, offsets[number], wsem.at[number], lead):
-                    copy.start()
+        loads = [
+            pltpu.make_async_copy(source, target, wsem.at[number])
+            for number, (source, target) in enumerate(((hbm_q, wq), (hbm_o, wo)))
+        ]
+        for load in loads:
+            load.start()
         normal, inverse = stats(second_ref[...])
         g_second = cot[rows_of(me, share), :].astype(F32) + norm_backward(normal, inverse, g_ref[...] * gain[2:3, :])
         g_low = g_second.astype(BF)
@@ -1403,8 +1633,8 @@
         ut = dot_nt(words_in, at[...]).astype(BF)
         uk, uv = ut[:, :RANK], ut[:, RANK:]
         acc[...] = jnp.zeros_like(acc)
-        whole_wait(wq, wsem.at[0])
-        whole_wait(wo, wsem.at[1])
+        for load in loads:
+            load.wait()
 
         def chunk(place, carry):
             gq_sum, gk_sum, gv_sum = carry
@@ -1414,9 +1644,9 @@
             for head in range(heads):
                 gh = g_attn[:, head * HD : (head + 1) * HD]
                 q = q_ref[place, head]
-                kfull = kc[place, head]
+                kfull = kv[0, place, head]
                 k = kfull[:, :HD]
-                v = vc[place, head, :, :HD]
+                v = kv[1, place, head, :, :HD]
                 p = jnp.exp(dot_nt(q, k) * scale - log_ref[place, head])
                 dp = dot_nt(gh, v)
                 inner = jnp.sum(p * dp, axis=-1, keepdims=True)
@@ -1454,9 +1684,8 @@
     return call(
         kernel,
         [(array, True) for array in (g_in, cotangent, first, second, block_in, query, inverses, logs, low, u_low, text)]
-        + [(query_stack[0], False), (out_stack[0], False)]
-        + [(piece, False) for piece in query_stack[1]]
-        + [(array, True) for array in (keys, values, gains, down, up, out_down, out_up, text_down, up_key, up_value)],
+        + [(query_weight, False), (out_weight, False)]
+        + [(array, True) for array in (text_kv, gains, down, up, out_down, out_up, text_down, up_key, up_value)],
         [
             ((share, width), BF, True),
             ((RANK, width), F32, True),
@@ -1473,11 +1702,11 @@
     )
 
 
-def attention_backward(count, heads, g_first, attn_in, query, keys, values, low, logs, inv_q, inv_k, own_list, pieces,
-                       offsets, down, ups, out_down, out_up):
+def attention_backward(count, heads, g_first, attn_in, query, keys, values, low, logs, inv_q, inv_k, weights, down, ups,
+                       out_down, out_up):
     share, width = g_first.shape
     tokens = attn_in.shape[0]
-    local = own_list[0].shape[1]
+    local = weights[0].shape[1]
     block = min(128, tokens)
     chunk = min(64, tokens)
     steps = tokens // chunk
@@ -1485,26 +1714,19 @@
     scale = HD ** (-0.5)
 
     def kernel(g_ref, x_ref, q_ref, k_ref, v_ref, low_ref, log_ref, iq_ref, ik_ref, *refs):
-        owns = refs[:4]
-        piece_refs = refs[4:10]
-        (a_ref, bq, bk, bv, ao, bo, total_out, gall, ga_in, gb_q, gb_k, gb_v, ga_o, gb_o, wq, wk, wv, wo, gq_low, gk_acc,
-         gv_acc, swap_out, swap_in, partial_ref, from_left, from_right, stage_right, stage_left, wsem, xsend, xrecv,
-         *sems) = refs[10:]
+        (wq, wk, wv, wo, a_ref, bq, bk, bv, ao, bo, total_out, gall, ga_in, gb_q, gb_k, gb_v, ga_o, gb_o, gq_low, gk_acc,
+         gv_acc, swap_out, swap_in, partial_ref, from_left, from_right, stage_right, stage_left, xsend, xrecv,
+         *sems) = refs
         me = lax.axis_index("tensor")
         core = lax.axis_index("ctx")
         peer = {"ctx": 1 - core}
         gather_line = Line(me, count, *sems[:4])
         reduce_line = Line(me, count, *sems[4:])
-        for number, (w, own) in enumerate(zip((wq, wk, wv, wo), owns)):
-            for copy in assemble(w, own, piece_refs, offsets[number], wsem.at[number]):
-                copy.start()
         gall[me] = g_ref[...]
         for ref in (ga_in, gb_q, gb_k, gb_v, ga_o, gb_o, gk_acc, gv_acc):
             ref[...] = jnp.zeros_like(ref)
         greet(line_partners(me, count) + [(core >= 0, peer)])
         line_gather_step(gather_line, 0, gall)
-        for number, w in enumerate((wq, wk, wv, wo)):
-            whole_wait(w, wsem.at[number])
 
         def attend(place):
             rows = rows_of(place, share)
@@ -1596,8 +1818,7 @@
     return call(
         kernel,
         [(array, True) for array in (g_first, attn_in, query, keys, values, low, logs, inv_q, inv_k)]
-        + [(own, False) for own in own_list] + [(piece, False) for piece in pieces]
-        + [(array, True) for array in (down, *ups, out_down, out_up)],
+        + [(array, True) for array in (*weights, down, *ups, out_down, out_up)],
         [
             ((tokens, width), F32, True),
             ((count, share, width), BF, True),
@@ -1608,31 +1829,27 @@
             ((RANK, local), F32, True),
             ((RANK, width), F32, True),
         ],
-        [vmem(width, local) for _ in range(4)]
-        + [vmem(tokens, local), vmem(2, heads, tokens, HD, dtype=F32), vmem(2, heads, tokens, HD, dtype=F32)]
+        [vmem(tokens, local), vmem(2, heads, tokens, HD, dtype=F32), vmem(2, heads, tokens, HD, dtype=F32)]
         + [vmem(2, heads, tokens, HD), vmem(2, heads, tokens, HD)]
-        + buffers + [dma(4), dma(), dma()] + [dma(count) for _ in range(4)] + [dma(steps) for _ in range(4)],
+        + buffers + [dma(), dma()] + [dma(count) for _ in range(4)] + [dma(steps) for _ in range(4)],
         collective=4,
         cost=cost_of(16 * tokens * width * local, 60e6),
     )
 
 
-def skip_backward(count, g_attn, g_first, skip_out, hidden, long_skip, own, pieces, gain_halves, down, up, gain_row):
+def skip_backward(count, g_attn, g_first, skip_out, hidden, long_skip, weight, gain_halves, down, up, gain_row):
     tokens, width = hidden.shape
-    span = own.shape[-1]
+    span = weight.shape[-1]
     share = tokens // count
     block = share
 
-    def kernel(g_ref, gf_ref, skip_ref, hid, lsk, own_ref, *refs):
-        piece_refs = refs[:6]
-        (gains, a_ref, b_ref, gain, out_h, out_l, g_shift, ga, gb, w, buf_h, buf_l, low, grads, wsem, osem) = refs[6:]
+    def kernel(g_ref, gf_ref, skip_ref, hid, lsk, hbm_w, gains, a_ref, b_ref, gain, out_h, out_l, g_shift,
+               ga, gb, w, buf_h, buf_l, low, wsem, osem):
         me = lax.axis_index("tensor")
-        for far in range(count):
-            lead = (far, xor_place(me, far))
-            for copy in assemble(w, own_ref, piece_refs, 0, wsem, lead):
-                copy.start()
+        load = pltpu.make_async_copy(hbm_w, w, wsem)
+        load.start()
         g_shift[...] = jnp.zeros_like(g_shift)
-        whole_wait(w, wsem)
+        load.wait()
 
         def step(number, carry):
             rows = rows_of(number, block)
@@ -1690,7 +1907,7 @@
     return call(
         kernel,
         [(array, True) for array in (g_attn, g_first, skip_out, hidden, long_skip)]
-        + [(own, False)] + [(piece, False) for piece in pieces]
+        + [(weight, False)]
         + [(array, True) for array in (gain_halves, down, up, gain_row)],
         [
             ((tokens, width), F32, False),
@@ -1704,7 +1921,6 @@
             vmem(blocks, block, width, dtype=F32),
             vmem(blocks, block, width, dtype=F32),
             vmem(block, 2 * width, dtype=F32),
-            vmem(8, 128, dtype=F32),
             dma(),
             dma(2, blocks),
         ],
@@ -1781,32 +1997,8 @@
     )[0]
 
 
-PAIR = ("dp", "ctx")
-
-
-def pair_permutation(core0, core1):
-    pairs = []
-    for dp in range(4):
-        for core in range(2):
-            pairs.append((dp * 2 + core, (dp ^ (core0 if core == 0 else core1)) * 2 + core))
-    return pairs
-
-
 def swap_cores(value):
     return lax.ppermute(value, "ctx", [(0, 1), (1, 0)])
-
-
-def share_pieces(half):
-    first, second = pair_permutation(1, 2), pair_permutation(2, 1)
-    a = lax.ppermute(half, PAIR, first)
-    b = lax.ppermute(half, PAIR, second)
-    c = lax.ppermute(a, PAIR, second)
-    return [a, b, c, swap_cores(a), swap_cores(b), swap_cores(c)]
-
-
-def core_half(value, axis=0):
-    size = value.shape[axis] // 2
-    return lax.dynamic_slice_in_dim(value, lax.axis_index("ctx") * size, size, axis)
 
 
 def exchange_dp(rows):
@@ -1886,103 +2078,62 @@
     def stack(table):
         return jnp.transpose(table.reshape(RANK, count, -1), (1, 0, 2))
 
-    skip_t = skip_projection_weight.T
-    attn_out_t = attention_output_weight.T
-    cross_out_t = cross_output_weight.T
-    ff_down_t = feedforward_down_weight.T
-
-    skip_half = core_half(skip_t)
-    skip_pieces = share_pieces(skip_half)
-
-    narrow = [self_query_weight, self_key_weight, self_value_weight, attn_out_t, cross_key_weight, cross_value_weight]
-    narrow_at = [sum(weight.shape[0] for weight in narrow[:number]) // 2 for number in range(6)]
-    narrow_pieces = share_pieces(jnp.concatenate([core_half(weight) for weight in narrow], axis=0))
-
-    def along_tensor(value):
-        others = [
-            lax.ppermute(value, "tensor", [(place, place ^ number) for place in range(count)])
-            for number in range(1, count)
-        ]
-        return jnp.stack([value] + others)
-
-    cross_own = along_tensor(jnp.concatenate([cross_query_weight, cross_out_t], axis=0))
-    rows_q = cross_query_weight.shape[0]
-    cross_half = jnp.concatenate(
-        [core_half(cross_own[:, :rows_q], 1), core_half(cross_own[:, rows_q:], 1)], axis=1
-    )
-    cross_pieces = share_pieces(cross_half)
-    cross_at = [0, rows_q // 2]
-    query_stack = (cross_own[:, :rows_q], cross_pieces)
-    out_stack = (cross_own[:, rows_q:], cross_pieces)
-
-    wide_pieces = share_pieces(jnp.concatenate([core_half(feedforward_up_weight), core_half(ff_down_t)], axis=0))
-    wide_at = [0, feedforward_up_weight.shape[0] // 2]
-
-    skip_own = along_tensor(skip_t)
-    skip_all_pieces = share_pieces(core_half(skip_own, 1))
-
+    weights = {
+        "skip": skip_projection_weight.T,
+        "q": self_query_weight,
+        "k": self_key_weight,
+        "v": self_value_weight,
+        "o": attention_output_weight.T,
+        "ck": cross_key_weight,
+        "cv": cross_value_weight,
+        "cq": cross_query_weight,
+        "co": cross_output_weight.T,
+        "up": feedforward_up_weight,
+        "dn": feedforward_down_weight.T,
+    }
+    mod_rows = shift_modulation_weight.shape[0]
     act_wide, silu_pull = jax.vjp(jax.nn.silu, condition.astype(F32))
     act_low = act_wide.astype(BF)
-    tag = jnp.full((1, 128), index, jnp.int32).astype(BF)
-    gathered = gather_dp(jnp.concatenate([act_low, tag], axis=1))
-    indices = gathered[:, MODEL_WIDTH].astype(jnp.int32)
-    mod_rows = shift_modulation_weight.shape[0]
-    act_slice = lax.dynamic_slice_in_dim(gathered, dp * mod_rows, mod_rows, 1)
-    shift_parts = exchange_dp(dot_nn(act_slice, shift_modulation_weight))
     mod_u = dot_nt(act_low, down_full(1))
-    shift_row = sum(shift_parts) + jnp.dot(mod_u, up_full(1).astype(F32), precision=PRECISE)
+    tag = jnp.full((1, 128), index, jnp.int32).astype(F32)
 
     both = jnp.concatenate([hidden, long_skip], axis=1)
     part = lax.dynamic_slice_in_dim(both, rank * span, span, 1)
     part_gain = lax.dynamic_slice_in_dim(skip_norm_gain, rank * span, span, 0)[None, :]
-    skip_out, attn_in = skip_forward(
-        count, skip_t, skip_pieces, hidden, long_skip, part, part_gain, down_local(0, span), up_full(0),
-        norm_gain_rows[0:1], shift_row,
-    )
-    own_text = text_forward(
-        heads, text, cross_key_weight, cross_value_weight, narrow_pieces, narrow_at[4], narrow_at[5],
-        jnp.concatenate([down_full(7), down_full(8)], axis=0), up_local(7, local), up_local(8, local),
-    )
-    text_all = jnp.zeros((count, *own_text.shape), BF)
-    for number in range(count):
-        got = own_text
-        if number:
-            got = lax.ppermute(own_text, "tensor", [(place, place ^ number) for place in range(count)])
-        text_all = lax.dynamic_update_slice_in_dim(text_all, got[None], rank ^ number, 0)
-    text_other = swap_cores(text_all)
-    text_keys = jnp.where(core == 0, text_all, text_other)
-    text_values = jnp.where(core == 0, text_other, text_all)
-
+    text_down = jnp.concatenate([down_full(7), down_full(8)], axis=0)
     qkv_down = jnp.concatenate([down_full(2), down_full(3), down_full(4)], axis=0)
     qkv_up = [up_local(number, local) for number in (2, 3, 4)]
-    attn_own = [self_query_weight, self_key_weight, self_value_weight, attn_out_t]
     out_down, out_up = down_local(5, local), up_full(5)
-    query, keys, values, low, logs, inv_q, inv_k, summed = attention_forward(
-        count, heads, attn_in, attn_own, narrow_pieces, narrow_at[:4], qkv_down, qkv_up, out_down, out_up
-    )
+    (skip_out, attn_in, query, keys, values, low, logs, inv_q, inv_k, summed, act_all, text_kv, wq, wk, wv, wo, wcq, wco,
+     wup, wdn) = front(
+        count, heads, act_low, tag, hidden, long_skip, part, part_gain, text, weights,
+        (shift_modulation_weight, down_full(1), up_full(1)), norm_gain_rows[0:1],
+        (down_local(0, span), up_full(0)), (text_down, up_local(7, local), up_local(8, local)), (qkv_down, *qkv_up),
+        (out_down, out_up),
+    )
+    indices = act_all[:, 0, MODEL_WIDTH].astype(jnp.int32)
     cross_down, cross_up = down_full(6), stack(up_full(6))
     cout_down, cout_up = stack(down_full(9)), up_full(9)
-    first, second, cross_in, mlp_in, cquery, cinv, clogs, clow, cu = cross_forward(
-        count, heads, summed, skip_out, query_stack, out_stack, text_keys, text_values, norm_gain_rows, cross_down,
-        cross_up, cout_down, cout_up, cross_at,
-    )
-    g_mlp_in, down_part, g_up_a, g_up_b, g_down_a, g_down_b = feed_forward(
-        count, mlp_in, cot, second, feedforward_up_weight, ff_down_t, wide_pieces, wide_at, down_full(10),
-        up_local(10, ff), down_local(11, ff), up_full(11),
+    first, second, cross_in, mlp_in, cquery, cinv, clogs, clow, cu, skip_half = cross_forward(
+        count, heads, summed, skip_out, wcq, wco, weights["skip"], text_kv, norm_gain_rows, cross_down, cross_up,
+        cout_down, cout_up,
+    )
+    g_mlp_in, down_part, g_up_a, g_up_b, g_down_a, g_down_b, skip_all = feed_forward(
+        count, mlp_in, cot, second, wup, wdn, skip_half, down_full(10), up_local(10, ff), down_local(11, ff), up_full(11),
     )
     block_out = lax.psum(down_part, "tensor")
     g_first, g_cq_a, g_cq_b, g_ck_a, g_ck_b, g_cv_a, g_cv_b, g_co_a, g_co_b = cross_backward(
-        count, heads, g_mlp_in, cot, first, second, cross_in, cquery, cinv, clogs, clow, cu, text, query_stack,
-        out_stack, text_keys, text_values, norm_gain_rows, cross_down, cross_up, cout_down, cout_up,
-        jnp.concatenate([down_full(7), down_full(8)], axis=0), stack(up_full(7)), stack(up_full(8)), cross_at,
+        count, heads, g_mlp_in, cot, first, second, cross_in, cquery, cinv, clogs, clow, cu, text, wcq, wco,
+        text_kv, norm_gain_rows, cross_down, cross_up, cout_down, cout_up, text_down, stack(up_full(7)),
+        stack(up_full(8)),
     )
     g_attn, g_first_all, g_qkv_a, g_q_b, g_k_b, g_v_b, g_o_a, g_o_b = attention_backward(
-        count, heads, g_first, attn_in, query, keys, values, low, logs, inv_q, inv_k, attn_own, narrow_pieces,
-        narrow_at[:4], qkv_down, qkv_up, out_down, out_up,
+        count, heads, g_first, attn_in, query, keys, values, low, logs, inv_q, inv_k, (wq, wk, wv, wo), qkv_down,
+        qkv_up, out_down, out_up,
     )
     skip_down = jnp.transpose(down_full(0).reshape(RANK, 2, MODEL_WIDTH), (1, 0, 2))
     hidden_grad, skip_grad, g_shift, g_skip_a, g_skip_b = skip_backward(
-        count, g_attn, g_first_all, skip_out, hidden, long_skip, skip_own, skip_all_pieces,
+        count, g_attn, g_first_all, skip_out, hidden, long_skip, skip_all,
         skip_norm_gain.reshape(2, MODEL_WIDTH), skip_down, up_full(0), norm_gain_rows[0:1],
     )
 

time: 704 us -> 567 us (0.81)
  Pallas kernels: 390 us -> 460 us
  starting transfers between devices: 76.1 us -> 10.4 us
  waiting for transfers between devices: 63.5 us -> 0.04 us
  local copies, waits for them, and re-layouts: 118 us -> 61.1 us
  other arithmetic: 23.4 us -> 7.94 us
    pallas_call x9 -> x7, Pallas kernels: 390 us -> 460 us  [call(): pl.pallas_call(kernel, out_shape=[jax.ShapeDtypeStruct(shape, dtype) for...]
    ppermute x24 -> x0, waiting for transfers between devices: 63.4 us -> none  [the longest x6 39.9 us: along_tensor(): lax.ppermute(value, 'tensor', [(place, place ^ number) for place in range...]
    ppermute x17 -> x1, starting transfers between devices: 45 us -> 3.66 us  [swap_cores(): return lax.ppermute(value, 'ctx', [(0, 1), (1, 0)])]
    ppermute x24 -> x0, starting transfers between devices: 20.2 us -> none  [the longest x5 5.9 us: share_pieces(): b = lax.ppermute(half, PAIR, second)]
    ppermute x10 -> x0, local copies, waits for them, and re-layouts: 20 us -> none  [the longest x4 10.2 us: swap_cores(): return lax.ppermute(value, 'ctx', [(0, 1), (1, 0)])]
    dynamic_update_slice x6 -> x3, local copies, waits for them, and re-layouts: 9.77 us -> 0.18 us  [gather_dp(): table = lax.dynamic_update_slice_in_dim(table, got, dp ^ number, 0)]
    dynamic_slice x9 -> x0, local copies, waits for them, and re-layouts: 8.83 us -> none  [core_half(): lax.dynamic_slice_in_dim(value, lax.axis_index('ctx') * size, size, axis)]
    unnamed x141 -> x92, local copies, waits for them, and re-layouts: 30.4 us -> 28.2 us
  transfers between devices with their start and end apart: 54 -> 8, of which waited for: 7 -> 0; matrix products, arithmetic and copies ran while one was open for 20% -> 6% of each run, Pallas kernels for 53% -> 10%
where the time goes in v2:
time: 567 us; the launch traced here: 558 us
  Pallas kernels  460 us (81%)
  local copies, waits for them, and re-layouts  61.1 us (11%)
  between operations  15.7 us (3%)
  starting transfers between devices  10.4 us (2%)
  other arithmetic  7.94 us (1%)
    pallas_call x7, Pallas kernels, call(): pl.pallas_call(kernel, out_shape=[jax.ShapeDtypeStruct(shape, dtype) for...  460 us
    unnamed x92, local copies, waits for them, and re-layouts  28.2 us
  transfers between devices with their start and end apart: 8, of which 0 were waited for; matrix products, arithmetic and copies ran while one was open for 6% of the time, Pallas kernels for 10%

profile of v2, /device:TPU:9, one launch (start us, length us, event | category | flops | bytes accessed | tf_op | source)
XLA Modules:
  0.0 557.9 jit_solution(9629982397921581171)
XLA Ops:
  7.9 1.2 dynamic-slice_bitcast_fusion
  10.0 1.1 dynamic-slice_bitcast_fusion.1
  12.0 1.9 fusion.18
  13.9 1.3 reshape.133.gains
  16.6 1.3 fusion.16
  18.9 1.3 slice.89.gain
  20.2 1.8 copy.38
  22.1 1.8 copy.39
  23.9 1.8 copy.40.ck_own
  25.7 1.7 copy.41.cv_own
  34.2 1.4 dynamic-slice_bitcast_fusion.4.sa
  35.6 1.6 fusion.par
  37.8 1.6 dynamic-slice_bitcast_fusion.2
  40.1 1.5 dynamic-slice_bitcast_fusion.6
  42.1 166.4 %shard_map.253 = (f32[512,1408]{1,0:T(8,128)}, bf16[512,1408]{1,0:T(8,128)(2,1)}, bf16[4,512,88]{2,1,0:T(8,128)(2,1)}, bf16[2,4,512,88]{3,2,1,0:T(8,128)(2,1)}, ...) custom-call(bf16[352,704]{1,0:T(8,128)(2,1)} %bitcast.93, ...), custom_call_target="tpu_custom_call" | custom-call | flops 2030043136 | bytes 60000000 | tf_op jit(solution)/shard_map/pallas_call | solution.py:919
  208.5 30.7 %shard_map.254 = (f32[128,1408]{1,0:T(8,128)}, f32[128,1408]{1,0:T(8,128)}, bf16[128,1408]{1,0:T(8,128)(2,1)}, bf16[128,1408]{1,0:T(8,128)(2,1)}, bf16[4,4,128,8...) custom-call(f32[128,1408]{1,0:T(8,128)} %get-tuple-element.65.sum_re, ...), custom_call_target="tpu_custom_call" | custom-call | flops 1015021568 | bytes 20000000 | tf_op jit(solution)/shard_map/pallas_call | solution.py:919
  239.2 76.5 %shard_map.255 = (f32[128,1408]{1,0:T(8,128)}, bf16[512,1408]{1,0:T(8,128)(2,1)}, f32[16,1408]{1,0:T(8,128)}, f32[16,1536]{1,0:T(8,128)}, f32[16,1536]{1,0:T(8,1...) custom-call(bf16[128,1408]{1,0:T(8,128)(2,1)} %get-tuple-element.70.x_ref, bf16[512,1408]{1,0:T(8,128)(2,1)} %bitcast.102, ...), custom_call_target="tpu_custom_call" | custom-call | flops 8858370048 | bytes 60000000 | tf_op jit(solution)/shard_map/pallas_call | solution.py:919
  315.7 23.8 %shard_map.256 = (bf16[128,1408]{1,0:T(8,128)(2,1)}, f32[16,1408]{1,0:T(8,128)}, f32[4,16,352]{2,1,0:T(8,128)}, f32[16,1024]{1,0:T(8,128)}, f32[4,16,352]{2,1,0:...) custom-call(f32[128,1408]{1,0:T(8,128)} %get-tuple-element.76.g_ref, ...), custom_call_target="tpu_custom_call" | custom-call | flops 2030043136 | bytes 20000000 | tf_op jit(solution)/shard_map/pallas_call | solution.py:919
  339.5 87.5 %shard_map.257 = (f32[512,1408]{1,0:T(8,128)}, bf16[4,128,1408]{2,1,0:T(8,128)(2,1)}, f32[48,1408]{1,0:T(8,128)}, f32[16,352]{1,0:T(8,128)}, f32[16,352]{1,0:T(8...) custom-call(bf16[128,1408]{1,0:T(8,128)(2,1)} %get-tuple-element.84.g_ref, ...), custom_call_target="tpu_custom_call" | custom-call | flops 4060086272 | bytes 60000000 | tf_op jit(solution)/shard_map/pallas_call | solution.py:919
  427.0 21.9 %shard_map.258 = (f32[512,1408]{1,0:T(8,128)}, f32[512,1408]{1,0:T(8,128)}, f32[1,1408]{1,0:T(1,128)}, f32[2,16,1408]{2,1,0:T(8,128)}, f32[16,1408]{1,0:T(8,128)}) custom-call(f32[512,1408]{1,0:T(8,128)} %get-tuple-element.97.g_ref, bf16[4,128,1408]{2,1,0:T(8,128)(2,1)} %get-tuple-element.98.gf_ref, f32[512,1408]{1,0:T(8,128)} %get-tuple-element.66.skip_ref, ...), custom_call_target="tpu_custom_call" | custom-call | flops 4060086272 | bytes 30000000 | tf_op jit(solution)/shard_map/pallas_call | solution.py:919
  448.9 3.7 collective-permute-start
  453.7 1.6 bitcast_dynamic-update-slice_fusion.1
  455.2 1.5 bitcast_dynamic-update-slice_fusion
  469.6 2.3 collective-permute-start.2
  471.9 1.1 collective-permute-start.3
  482.4 1.3 collective-permute-start.5
  484.9 2.2 reshape.143
  487.1 1.9 pad.4.t_ref
  489.6 53.5 %shard_map.259 = f32[2,4,176,128]{3,2,1,0:T(8,128)} custom-call(f32[16,352,128]{2,1,0:T(8,128)} %pad.4.t_ref, f32[2,4,1,128]{3,2,1,0:T(1,128)} %broadcast_in_dim.36.sel), custom_call_target="tpu_custom_call" | custom-call | flops 1000000 | bytes 10000000 | tf_op jit(solution)/shard_map/pallas_call | solution.py:919
  543.1 1.2 copy.51
  546.9 1.3 fusion.8
  548.3 2.6 copy.105
  (165 shorter events, 40.0 us)
Async XLA Ops:
  7.2 541.1 %all-reduce.3.cloned.1.call-start = ((), (), s32[]{:S(2)}) async-start(), calls=%async_computation | async-start | bytes 2883584 | tf_op jit(solution)/shard_map/psum | solution.py:2124
  12.0 21.5 %slice-start = ((bf16[16,22272]{1,0:T(8,128)(2,1)}), bf16[16,2816]{1,0:T(8,128)(2,1)S(1)}, s32[]{:S(2)}) async-start(bf16[16,22272]{1,0:T(8,128)(2,1)} %copy-done.3), calls=%async_computation.1 | async-start | bytes 180224 | tf_op jit(solution)/shard_map/slice | solution.py:2067
  12.0 23.6 %copy-start = (bf16[1,512,1408]{2,1,0:T(8,128)(2,1)S(1)}, bf16[1,512,1408]{2,1,0:T(8,128)(2,1)}, u32[]{:S(2)}) copy-start(bf16[1,512,1408]{2,1,0:T(8,128)(2,1)} %param.22) | copy-start | bytes 4325380
  12.0 23.6 %copy-start.1 = (bf16[1,512,1408]{2,1,0:T(8,128)(2,1)S(1)}, bf16[1,512,1408]{2,1,0:T(8,128)(2,1)}, u32[]{:S(2)}) copy-start(bf16[1,512,1408]{2,1,0:T(8,128)(2,1)} %param.23) | copy-start | bytes 4325380
  23.9 13.3 %copy-start.11 = (bf16[16,1024]{1,0:T(8,128)(2,1)S(1)}, bf16[16,1024]{1,0:T(8,128)(2,1)}, u32[]{:S(2)}) copy-start(bf16[16,1024]{1,0:T(8,128)(2,1)} %get-tuple-element.142) | copy-start | bytes 98308
  23.9 15.5 %copy-start.8 = (bf16[16,1408]{1,0:T(8,128)(2,1)S(1)}, bf16[16,1408]{1,0:T(8,128)(2,1)}, u32[]{:S(2)}) copy-start(bf16[16,1408]{1,0:T(8,128)(2,1)} %get-tuple-element.137) | copy-start | bytes 135172
  23.9 15.5 %copy-start.9 = (bf16[16,1408]{1,0:T(8,128)(2,1)S(1)}, bf16[16,1408]{1,0:T(8,128)(2,1)}, u32[]{:S(2)}) copy-start(bf16[16,1408]{1,0:T(8,128)(2,1)} %get-tuple-element.138) | copy-start | bytes 135172
  23.9 15.5 %copy-start.10 = (bf16[16,1408]{1,0:T(8,128)(2,1)S(1)}, bf16[16,1408]{1,0:T(8,128)(2,1)}, u32[]{:S(2)}) copy-start(bf16[16,1408]{1,0:T(8,128)(2,1)} %get-tuple-element.139) | copy-start | bytes 135172
  427.0 30.5 %copy-start.7 = (f32[48,1408]{1,0:T(8,128)S(1)}, f32[48,1408]{1,0:T(8,128)}, u32[]{:S(2)}) copy-start(f32[48,1408]{1,0:T(8,128)} %get-tuple-element.104) | copy-start | bytes 811012
  427.0 32.5 %copy-start.17 = (f32[4,16,352]{2,1,0:T(8,128)S(1)}, f32[4,16,352]{2,1,0:T(8,128)}, u32[]{:S(2)}) copy-start(f32[4,16,352]{2,1,0:T(8,128)} %get-tuple-element.109) | copy-start | bytes 270340
  448.9 13.4 %copy-start.25 = (f32[16,1024]{1,0:T(8,128)S(1)}, f32[16,1024]{1,0:T(8,128)}, u32[]{:S(2)}) copy-start(f32[16,1024]{1,0:T(8,128)} %get-tuple-element.107) | copy-start | bytes 196612
  448.9 14.1 %copy-start.24 = (f32[16,1024]{1,0:T(8,128)S(1)}, f32[16,1024]{1,0:T(8,128)}, u32[]{:S(2)}) copy-start(f32[16,1024]{1,0:T(8,128)} %get-tuple-element.108) | copy-start | bytes 196612
  448.9 15.3 %copy-start.21 = (f32[16,1408]{1,0:T(8,128)S(1)}, f32[16,1408]{1,0:T(8,128)}, u32[]{:S(2)}) copy-start(f32[16,1408]{1,0:T(8,128)} %get-tuple-element.110) | copy-start | bytes 270340
  448.9 16.0 %copy-start.16 = (f32[16,1536]{1,0:T(8,128)S(1)}, f32[16,1536]{1,0:T(8,128)}, u32[]{:S(2)}) copy-start(f32[16,1536]{1,0:T(8,128)} %get-tuple-element.111) | copy-start | bytes 294916
  448.9 16.8 %copy-start.23 = (f32[16,1408]{1,0:T(8,128)S(1)}, f32[16,1408]{1,0:T(8,128)}, u32[]{:S(2)}) copy-start(f32[16,1408]{1,0:T(8,128)} %get-tuple-element.112) | copy-start | bytes 270340
  448.9 20.0 %collective-permute-start = (f32[1,1408]{1,0:T(1,128)}, f32[1,1408]{1,0:T(1,128)S(1)}, u32[]{:S(2)}, u32[]{:S(2)}) collective-permute-start(f32[1,1408]{1,0:T(1,128)} %get-tuple-element.102), channel_id=1, source_target_pairs={{0,4},{4,0},{1,5},{5,1},{2,6},{6,2},{3,7},{7,3},{8,12},{12,8},{9,1... | collective-permute-start | bytes 16904 | tf_op jit(solution)/shard_map/ppermute | solution.py:2001
  452.6 13.8 %copy-start.15 = (f32[16,1536]{1,0:T(8,128)S(1)}, f32[16,1536]{1,0:T(8,128)}, u32[]{:S(2)}) copy-start(f32[16,1536]{1,0:T(8,128)} %get-tuple-element.121) | copy-start | bytes 294916
  452.6 13.9 %copy-start.4 = (bf16[16,22272]{1,0:T(8,128)(2,1)S(1)}, bf16[16,22272]{1,0:T(8,128)(2,1)}, u32[]{:S(2)}) copy-start(bf16[16,22272]{1,0:T(8,128)(2,1)} %copy-done.3) | copy-start | bytes 2138116
  452.6 13.9 %copy-start.30 = (bf16[1,1408]{1,0:T(2,128)(2,1)S(1)}, bf16[1,1408]{1,0:T(2,128)(2,1)}, u32[]{:S(2)}) copy-start(bf16[1,1408]{1,0:T(2,128)(2,1)} %get-tuple-element.125.act_ref) | copy-start | bytes 8452
  452.6 14.0 %copy-start.14 = (f32[4,16,352]{2,1,0:T(8,128)S(1)}, f32[4,16,352]{2,1,0:T(8,128)}, u32[]{:S(2)}) copy-start(f32[4,16,352]{2,1,0:T(8,128)} %get-tuple-element.117) | copy-start | bytes 270340
  452.6 14.2 %copy-start.13 = (f32[4,16,352]{2,1,0:T(8,128)S(1)}, f32[4,16,352]{2,1,0:T(8,128)}, u32[]{:S(2)}) copy-start(f32[4,16,352]{2,1,0:T(8,128)} %get-tuple-element.118) | copy-start | bytes 270340
  453.7 13.3 %copy-start.12 = (f32[4,16,352]{2,1,0:T(8,128)S(1)}, f32[4,16,352]{2,1,0:T(8,128)}, u32[]{:S(2)}) copy-start(f32[4,16,352]{2,1,0:T(8,128)} %get-tuple-element.119) | copy-start | bytes 270340
  460.5 15.2 %copy-start.20 = (f32[16,1408]{1,0:T(8,128)S(1)}, f32[16,1408]{1,0:T(8,128)}, u32[]{:S(2)}) copy-start(f32[16,1408]{1,0:T(8,128)} %get-tuple-element.116) | copy-start | bytes 270340
  463.6 14.7 %copy-start.19 = (f32[16,1408]{1,0:T(8,128)S(1)}, f32[16,1408]{1,0:T(8,128)}, u32[]{:S(2)}) copy-start(f32[16,1408]{1,0:T(8,128)} %get-tuple-element.120) | copy-start | bytes 270340
  464.9 14.8 %copy-start.18 = (f32[16,1408]{1,0:T(8,128)S(1)}, f32[16,1408]{1,0:T(8,128)}, u32[]{:S(2)}) copy-start(f32[16,1408]{1,0:T(8,128)} %get-tuple-element.122) | copy-start | bytes 270340
  464.9 16.7 %copy-start.2 = (bf16[352,1408]{1,0:T(8,128)(2,1)S(1)}, bf16[352,1408]{1,0:T(8,128)(2,1)}, u32[]{:S(2)}) copy-start(bf16[352,1408]{1,0:T(8,128)(2,1)} %wm.1) | copy-start | bytes 2973700
  469.0 12.4 %collective-permute-start.1 = (bf16[1,1408]{1,0:T(2,128)(2,1)S(1)}, bf16[1,1408]{1,0:T(2,128)(2,1)S(1)}, u32[]{:S(2)}, u32[]{:S(2)}) collective-permute-start(bf16[1,1408]{1,0:T(2,128)(2,1)S(1)} %convert.10), channel_id=1, source_target_pairs={{0,8},{8,0},{16,24},{24,16},{1,9},{9,1},{17,25},{25,17},{2,10},{10... | collective-permute-start | bytes 8456 | tf_op jit(solution)/shard_map/ppermute | solution.py:2018
  469.6 11.9 %collective-permute-start.2 = (bf16[1,1408]{1,0:T(2,128)(2,1)S(1)}, bf16[1,1408]{1,0:T(2,128)(2,1)S(1)}, u32[]{:S(2)}, u32[]{:S(2)}) collective-permute-start(bf16[1,1408]{1,0:T(2,128)(2,1)S(1)} %convert.10), channel_id=1, source_target_pairs={{0,16},{8,24},{16,0},{24,8},{1,17},{9,25},{17,1},{25,9},{2,18},{10... | collective-permute-start | bytes 8456 | tf_op jit(solution)/shard_map/ppermute | solution.py:2018
  471.9 9.6 %collective-permute-start.3 = (bf16[1,1408]{1,0:T(2,128)(2,1)S(1)}, bf16[1,1408]{1,0:T(2,128)(2,1)S(1)}, u32[]{:S(2)}, u32[]{:S(2)}) collective-permute-start(bf16[1,1408]{1,0:T(2,128)(2,1)S(1)} %get-tuple-element.127), channel_id=1, source_target_pairs={{0,24},{8,16},{16,8},{24,0},{1,25},{9,17},{17,9},{25,1},{2,26},{10... | collective-permute-start | bytes 8456 | tf_op jit(solution)/shard_map/ppermute | solution.py:2018
  482.0 63.9 %collective-permute-start.4 = (f32[1,352]{1,0:T(1,128)S(1)}, f32[1,352]{1,0:T(1,128)S(1)}, u32[]{:S(2)}, u32[]{:S(2)}) collective-permute-start(f32[1,352]{1,0:T(1,128)S(1)} %get-tuple-element.153), channel_id=1, source_target_pairs={{0,8},{8,0},{16,24},{24,16},{1,9},{9,1},{17,25},{25,17},{2,10},{10... | collective-permute-start | bytes 4232 | tf_op jit(solution)/shard_map/ppermute | solution.py:2009
  482.4 63.9 %collective-permute-start.5 = (f32[1,352]{1,0:T(1,128)S(1)}, f32[1,352]{1,0:T(1,128)S(1)}, u32[]{:S(2)}, u32[]{:S(2)}) collective-permute-start(f32[1,352]{1,0:T(1,128)S(1)} %get-tuple-element.152), channel_id=1, source_target_pairs={{0,16},{8,24},{16,0},{24,8},{1,17},{9,25},{17,1},{25,9},{2,18},{10... | collective-permute-start | bytes 4232 | tf_op jit(solution)/shard_map/ppermute | solution.py:2009
  483.7 63.0 %collective-permute-start.6 = (f32[1,352]{1,0:T(1,128)S(1)}, f32[1,352]{1,0:T(1,128)S(1)}, u32[]{:S(2)}, u32[]{:S(2)}) collective-permute-start(f32[1,352]{1,0:T(1,128)S(1)} %get-tuple-element.151), channel_id=1, source_target_pairs={{0,24},{8,16},{16,8},{24,0},{1,25},{9,17},{17,9},{25,1},{2,26},{10... | collective-permute-start | bytes 4232 | tf_op jit(solution)/shard_map/ppermute | solution.py:2009
  (9 other events, 75.9 us)
Sparse Core Ops, SparseCore 0:
  452.8 75.7 all-reduce.2

commit v3 on v2

--- a/solution.py
+++ b/solution.py
@@ -915,7 +915,7 @@
 
 
 def call(kernel, inputs, outs, scratch, collective=None, cost=None):
-    space = {True: pltpu.VMEM, False: pl.ANY}
+    space = {True: pltpu.VMEM, False: pl.ANY, None: pltpu.SMEM}
     return pl.pallas_call(
         kernel,
         out_shape=[jax.ShapeDtypeStruct(shape, dtype) for shape, dtype, _ in outs],
@@ -951,15 +951,42 @@
     return pl.ds(pl.multiple_of(index * size, size), size)
 
 
-def cross_forward(count, heads, summed, skip_out, query_weight, out_weight, skip_piece, text_kv, gains, down, up,
-                  out_down, out_up):
+IN_SIZES = [2 * MODEL_WIDTH] + [MODEL_WIDTH] * 6 + [TW, TW, MODEL_WIDTH, MODEL_WIDTH, FF]
+OUT_SIZES = [MODEL_WIDTH] * 10 + [FF, MODEL_WIDTH]
+IN_AT = [sum(IN_SIZES[:number]) for number in range(13)]
+OUT_AT = [sum(OUT_SIZES[:number]) for number in range(13)]
+
+
+def down_of(table, number):
+    return table[:, IN_AT[number] : IN_AT[number + 1]]
+
+
+def up_of(table, number):
+    return table[:, OUT_AT[number] : OUT_AT[number + 1]]
+
+
+def take_local(target, table, start, me, count):
+    size = target.shape[-1]
+    for place in range(count):
+        @pl.when(me == place)
+        def _(place=place):
+            target[...] = table[:, start + place * size : start + (place + 1) * size]
+
+
+def take_stack(target, table, start, count):
+    size = target.shape[-1]
+    for place in range(count):
+        target[place] = table[:, start + place * size : start + (place + 1) * size]
+
+
+def cross_forward(count, heads, summed, skip_out, query_weight, out_weight, skip_piece, text_kv, gains, tables):
     share, width = summed.shape
     local = query_weight.shape[-1]
     scale = HD ** (-0.5)
     rows, span = skip_piece.shape
 
-    def kernel(sum_ref, skip_ref, hbm_q, hbm_o, piece, kv, gain, a_ref, b_ref, ao, bo, first_out, second_out, in_out,
-               mlp_out, q_out, inv_out, log_out, low_out, uo_out, skip_half, wq, wo, wsem, zsend, zrecv):
+    def kernel(sum_ref, skip_ref, hbm_q, hbm_o, piece, kv, gain, dtab, utab, first_out, second_out, in_out,
+               mlp_out, q_out, inv_out, log_out, low_out, uo_out, skip_half, wq, wo, b_ref, ao, wsem, zsend, zrecv):
         me = lax.axis_index("tensor")
         core = lax.axis_index("ctx")
         loads = [
@@ -979,12 +1006,14 @@
         ]
         for send in sends:
             send.start()
+        take_stack(b_ref, utab, OUT_AT[6], count)
+        take_stack(ao, dtab, IN_AT[9], count)
         first = skip_ref[rows_of(me, share), :] + sum_ref[...]
         first_out[...] = first
         normal, _ = stats(first)
         x = (normal * gain[1:2, :]).astype(BF)
         in_out[...] = x
-        u = dot_nt(x, a_ref[...]).astype(BF)
+        u = dot_nt(x, down_of(dtab, 6)).astype(BF)
         second_out[...] = first
         for load in loads:
             load.wait()
@@ -1011,7 +1040,7 @@
 
         u_low = lax.fori_loop(0, count, chunk, jnp.zeros((share, RANK), F32)).astype(BF)
         uo_out[...] = u_low
-        second = second_out[...] + dot_nn(u_low, bo[...])
+        second = second_out[...] + dot_nn(u_low, up_of(utab, 9))
         second_out[...] = second
         normal, _ = stats(second)
         mlp_out[...] = (normal * gain[2:3, :]).astype(BF)
@@ -1025,7 +1054,7 @@
     return call(
         kernel,
         [(summed, True), (skip_out, True), (query_weight, False), (out_weight, False), (skip_piece, False)]
-        + [(array, True) for array in (text_kv, gains, down, up, out_down, out_up)],
+        + [(array, True) for array in (text_kv, gains, *tables)],
         [
             ((share, width), F32, True),
             ((share, width), F32, True),
@@ -1038,21 +1067,22 @@
             ((share, RANK), BF, True),
             ((count, rows // 2, span), BF, False),
         ],
-        [vmem(count, width, local), vmem(count, width, local), dma(3), dma(count), dma(count)],
+        [vmem(count, width, local), vmem(count, width, local), vmem(count, RANK, local), vmem(count, RANK, local),
+         dma(3), dma(count), dma(count)],
         collective=6,
         cost=cost_of(4 * share * width * width, 20e6),
     )
 
 
-def feed_forward(count, block_in, cotangent, second, up_weight, down_weight, skip_half, up_a, up_b, down_a, down_b):
+def feed_forward(count, block_in, cotangent, second, up_weight, down_weight, skip_half, tables):
     share, width = block_in.shape
     tokens = cotangent.shape[0]
     hidden_units = up_weight.shape[1]
     rows = 2 * skip_half.shape[1]
     span = skip_half.shape[2]
 
-    def kernel(x_ref, cot, sec, hbm_u, hbm_d, shalf, ua, ub, da, db, summed, down_out, g_ua, g_ub, g_da, g_db, skip_all,
-               slots, wu, wd, partial_ref, from_left, from_right, stage_right, stage_left, wsem, wsend, wrecv, *sems):
+    def kernel(x_ref, cot, sec, hbm_u, hbm_d, shalf, dtab, utab, summed, down_out, g_ua, g_ub, g_da, g_db, skip_all,
+               slots, wu, wd, ub, da, partial_ref, from_left, from_right, stage_right, stage_left, wsem, wsend, wrecv, *sems):
         me = lax.axis_index("tensor")
         core = lax.axis_index("ctx")
         dp = lax.axis_index("dp")
@@ -1074,6 +1104,8 @@
         greet(line_partners(me, count) + [(core >= 0, device) for device in peers])
         line_gather_step(gather_line, 0, slots)
         skip.send_own(shalf)
+        take_local(ub, utab, OUT_AT[10], me, count)
+        take_local(da, dtab, IN_AT[11], me, count)
         for load in loads:
             load.wait()
 
@@ -1081,7 +1113,8 @@
             rows = rows_of(block, share)
             x = slots[block]
             ct = cot[rows, :]
-            u = dot_nt(x, ua[...]).astype(BF)
+            ua, db = down_of(dtab, 10), up_of(utab, 11)
+            u = dot_nt(x, ua).astype(BF)
             up = dot_nn(x, wu[...]) + dot_nn(u, ub[...])
             square = up * up
             curve = jnp.tanh(0.7978845608028654 * (up + 0.044715 * square * up))
@@ -1089,32 +1122,32 @@
             active = (up * half).astype(BF)
             slope = half + 0.5 * up * (1.0 - curve * curve) * (0.7978845608028654 * (1.0 + 0.134145 * square))
             ud = dot_nt(active, da[...]).astype(BF)
-            down = dot_nt(active, wd[...]) + dot_nn(ud, db[...])
+            down = dot_nt(active, wd[...]) + dot_nn(ud, db)
             down_out[rows, :] = down.astype(BF)
 
             @pl.when(block == me)
             def _():
                 down_out[rows, :] = (down + sec[...]).astype(BF)
 
-            gd = dot_nt(ct, db[...]).astype(BF)
+            gd = dot_nt(ct, db).astype(BF)
             g_active = dot_nn(ct, wd[...]) + dot_nn(gd, da[...])
             g_up = (g_active * slope).astype(BF)
             gu = dot_nt(g_up, ub[...]).astype(BF)
-            partial_ref[block] = (dot_nt(g_up, wu[...]) + dot_nn(gu, ua[...])).astype(BF)
+            partial_ref[block] = (dot_nt(g_up, wu[...]) + dot_nn(gu, ua)).astype(BF)
             g_ub[...] += dot_tn(u, g_up)
             g_ua[...] += dot_tn(gu, x)
             g_db[...] += dot_tn(ud, ct)
             g_da[...] += dot_tn(gd, active)
 
-        compute(me)
-
         def step(number, carry):
-            line_gather_step(gather_line, number, slots)
+            @pl.when(number > 0)
+            def _():
+                line_gather_step(gather_line, number, slots)
 
             def side(which, inner):
                 block = me + (2 * which - 1) * number
 
-                @pl.when((block >= 0) & (block < count))
+                @pl.when((block >= 0) & (block < count) & ((number > 0) | (which == 0)))
                 def _():
                     compute(lax.clamp(0, block, count - 1))
 
@@ -1122,7 +1155,7 @@
 
             return lax.fori_loop(0, 2, side, carry)
 
-        lax.fori_loop(1, count, step, 0)
+        lax.fori_loop(0, count, step, 0)
         own.wait()
         skip.wait(0)
         skip.forward()
@@ -1147,7 +1180,7 @@
     return call(
         kernel,
         [(block_in, True), (cotangent, True), (second, True), (up_weight, False), (down_weight, False), (skip_half, False)]
-        + [(array, True) for array in (up_a, up_b, down_a, down_b)],
+        + [(array, True) for array in tables],
         [
             ((share, width), F32, True),
             ((tokens, width), BF, True),
@@ -1157,7 +1190,8 @@
             ((RANK, width), F32, True),
             ((count, 4 * rows, span), BF, False),
         ],
-        [vmem(count, share, width), vmem(width, hidden_units), vmem(width, hidden_units)]
+        [vmem(count, share, width), vmem(width, hidden_units), vmem(width, hidden_units), vmem(RANK, hidden_units),
+         vmem(RANK, hidden_units)]
         + buffers + [dma(3), dma(1, 7), dma(1, 7)] + [dma(count) for _ in range(8)],
         collective=3,
         cost=cost_of(8 * tokens * width * hidden_units, 60e6),
@@ -1165,8 +1199,8 @@
 
 
 class Shared:
-    def __init__(self, target, rows, sems, stacked=False, split=True):
-        self.target, self.rows, self.stacked, self.split = target, rows, stacked, split
+    def __init__(self, target, rows, sems, stacked=False, split=True, columns=False):
+        self.target, self.rows, self.stacked, self.split, self.columns = target, rows, stacked, split, columns
         self.send_sem, self.recv_sem, self.index = sems
         dp, core = lax.axis_index("dp"), lax.axis_index("ctx")
         self.dp, self.core = dp, core
@@ -1175,6 +1209,8 @@
         self.third = xor_place(dp, 3)
 
     def view(self, block, which):
+        if self.columns:
+            return self.target.at[:, pl.ds(pl.multiple_of(block * self.rows, 128), self.rows)]
         size = self.rows // 2 if self.split else self.rows
         start = block * self.rows + (which * size if self.split else 0)
         rows = pl.ds(pl.multiple_of(start, 16), size)
@@ -1211,10 +1247,9 @@
             self.copy(number, None, self.dp, self.core, {"dp": self.first}).wait_send()
 
 
-def front(count, heads, act, tag, hidden, long_skip, part, part_gain, text, weights, mods, gain_row, skip_ab, text_ab,
-          qkv_ab, out_ab):
+def front(count, heads, condition, index, hidden, long_skip, text, weights, mod_weight, gain_halves, gain_rows, tables):
     tokens, width = hidden.shape
-    span = part.shape[1]
+    span = weights["skip"].shape[1]
     words, text_width = text.shape
     local = weights["q"].shape[1]
     units = weights["up"].shape[1]
@@ -1225,14 +1260,14 @@
     each = block // chunk
     scale = HD ** (-0.5)
     rows = weights["q"].shape[0]
-    text_rows = weights["ck"].shape[0]
-    mod_rows = mods[0].shape[0]
+    text_rows = weights["ck"].shape[1]
+    mod_rows = mod_weight.shape[0]
 
     def kernel(skip_own, q_own, k_own, v_own, o_own, ck_own, cv_own, cq_own, co_own, up_own, dn_own,
-               act_ref, tag_ref, hid, lsk, par, pgain, t_ref, wm, ma, mb, gain, sa, sb, ta, tk, tv, qa, qb, kb, vb, oa, ob,
+               index_ref, cond, hid, lsk, t_ref, wm, halves, gain, dtab, utab,
                skip_out, attn_in, q_out, keys, values, low_out, log_out, inv_q, inv_k, summed, act_all, text_kv,
                wq, wk, wv, wo, wcq, wco, wup, wdn,
-               wskip, wtext, mod_in, mod_slice, mod_out, partial_a, left_a, right_a, sr_a, sl_a,
+               wskip, wtext, part_x, pgain, sa, tk, tv, qa, qb, kb, vb, oa, mod_in, mod_slice, mod_out, partial_a, left_a, right_a, sr_a, sl_a,
                partial_b, left_b, right_b, sr_b, sl_b, wsend, wrecv, local_sem, zsend, zrecv, msend, mrecv, tsend, trecv,
                xsend, xrecv, *sems):
         me = lax.axis_index("tensor")
@@ -1253,7 +1288,7 @@
             name: Shared(target, rows, sems_of(number))
             for name, target, number in (("q", wq, 1), ("k", wk, 2), ("v", wv, 3), ("o", wo, 4))
         }
-        words_w = Shared(wtext, text_rows, sems_of(5), split=False)
+        words_w = Shared(wtext, text_rows, sems_of(5), split=False, columns=True)
         cross = [Shared(wcq, rows, sems_of(6), stacked=True), Shared(wco, rows, sems_of(7), stacked=True)]
         wide = [Shared(wup, rows, sems_of(8)), Shared(wdn, rows, sems_of(9))]
         owns = {"q": q_own, "k": k_own, "v": v_own, "o": o_own}
@@ -1273,10 +1308,10 @@
             pltpu.make_async_copy(source.at[half, :], target.at[me, my_half, :], local_sem.at[7 + number])
             for number, (source, target) in enumerate(((cq_own, wcq), (co_own, wco)))
         ]
-        text_mine = pl.ds(pl.multiple_of(dp * text_rows, 16), text_rows)
+        text_mine = pl.ds(pl.multiple_of(dp * text_rows, 128), text_rows)
 
         def text_place(source):
-            return pltpu.make_async_copy(source, wtext.at[text_mine, :], local_sem.at[9])
+            return pltpu.make_async_copy(source, wtext.at[:, text_mine], local_sem.at[9])
 
         @pl.when(core == 0)
         def _():
@@ -1288,7 +1323,10 @@
 
         for place in crossing:
             place.start()
-        act_all[dp] = jnp.concatenate([act_ref[...].astype(F32), tag_ref[...]], axis=1)
+        value = cond[...].astype(F32)
+        act_low = (value / (1.0 + jnp.exp(-value))).astype(BF)
+        tag = jnp.full((1, 128), index_ref[0], jnp.int32).astype(F32)
+        act_all[dp] = jnp.concatenate([act_low.astype(F32), tag], axis=1)
         greet([(always, device) for device in dp_peers + z_peers + [peer]])
         skip.send_own(skip_own.at[half, :])
 
@@ -1308,6 +1346,19 @@
         ]
         for copy in spread:
             copy.start()
+        for place in range(count):
+            @pl.when(me == place)
+            def _(place=place):
+                side = place * span // width
+                start = place * span % width
+                pgain[...] = halves[side : side + 1, start : start + span]
+        take_local(sa, dtab, 0, me, count)
+        take_local(tk, utab, OUT_AT[7], me, count)
+        take_local(tv, utab, OUT_AT[8], me, count)
+        for number, target in enumerate((qb, kb, vb)):
+            qa[number * RANK : (number + 1) * RANK, :] = down_of(dtab, 2 + number)
+            take_local(target, utab, OUT_AT[2 + number], me, count)
+        take_local(oa, dtab, IN_AT[5], me, count)
         skip.wait(0)
         skip.forward()
         for name in ("q", "k", "v", "o"):
@@ -1346,8 +1397,8 @@
         skip.wait(1)
         skip.swap(1)
         mod_in[dp] = mod_out[dp]
-        mod_u = dot_nt(act_ref[...], ma[...]).astype(BF)
-        mod_low = dot_nn(mod_u, mb[...])
+        mod_u = dot_nt(act_low, down_of(dtab, 1)).astype(BF)
+        mod_low = dot_nn(mod_u, up_of(utab, 1))
         for number in (1, 2, 3):
             target = mod_in.at[xor_place(dp, number)]
             push(target, target, msend.at[1, number - 1], mrecv.at[1, number - 1], dp_peers[number - 1]).wait_recv()
@@ -1367,9 +1418,15 @@
                 spread = jnp.sum((left - mean) ** 2, axis=-1, keepdims=True)
                 spread += jnp.sum((right - mean) ** 2, axis=-1, keepdims=True)
                 inverse = lax.rsqrt(spread / (2 * width) + NORM_EPS)
-                x = ((par[here, :].astype(F32) - mean) * inverse * pgain[...]).astype(BF)
+                for place in range(count):
+                    @pl.when(me == place)
+                    def _(place=place):
+                        source = hid if place * span < width else lsk
+                        start = place * span % width
+                        part_x[...] = source[here, start : start + span].astype(F32)
+                x = ((part_x[...] - mean) * inverse * pgain[...]).astype(BF)
                 u = dot_nt(x, sa[...]).astype(BF)
-                y = (dot_nt(x, wskip[...]) + dot_nn(u, sb[...])).astype(BF)
+                y = (dot_nt(x, wskip[...]) + dot_nn(u, up_of(utab, 0))).astype(BF)
                 for piece in range(each):
                     partial_a[number + piece] = y[piece * chunk : (piece + 1) * chunk]
 
@@ -1377,7 +1434,7 @@
             here = rows_of(slot, chunk)
             skip_out[here, :] = total
             normal, _ = stats(total)
-            attn_in[here, :] = (normal * gain[...] + shift).astype(BF)
+            attn_in[here, :] = (normal * gain[0:1, :] + shift).astype(BF)
 
         def beside(number):
             @pl.when(number == 3)
@@ -1424,12 +1481,11 @@
             text_place(cv_own).wait()
 
         x = t_ref[...]
-        u = dot_nt(x, ta[...]).astype(BF)
-        y = dot_nn(x, wtext[...])
+        y = dot_nt(x, wtext[...])
 
         @pl.when(core == 0)
         def _():
-            z = y + dot_nn(u[:, :RANK], tk[...])
+            z = y + dot_nn(dot_nt(x, down_of(dtab, 7)).astype(BF), tk[...])
             for head in range(heads):
                 normal, inverse = stats(z[:, head * HD : (head + 1) * HD])
                 upper = inverse.astype(BF)
@@ -1438,7 +1494,7 @@
 
         @pl.when(core == 1)
         def _():
-            z = (y + dot_nn(u[:, RANK:], tv[...])).astype(BF)
+            z = (y + dot_nn(dot_nt(x, down_of(dtab, 8)).astype(BF), tv[...])).astype(BF)
             filler = jnp.zeros((words, 2), BF)
             for head in range(heads):
                 text_kv[1, me, head] = jnp.concatenate([z[:, head * HD : (head + 1) * HD], filler], axis=1)
@@ -1510,7 +1566,7 @@
             low = jnp.concatenate(outs, axis=1).astype(BF)
             low_out[here, :] = low
             u = dot_nt(low, oa[...]).astype(BF)
-            partial_b[dest] = (dot_nt(low, wo[...]) + dot_nn(u, ob[...])).astype(BF)
+            partial_b[dest] = (dot_nt(low, wo[...]) + dot_nn(u, up_of(utab, 5))).astype(BF)
 
             @pl.when(place < count - 1)
             def _():
@@ -1566,9 +1622,8 @@
     names = ("skip", "q", "k", "v", "o", "ck", "cv", "cq", "co", "up", "dn")
     return call(
         kernel,
-        [(weights[name], False) for name in names]
-        + [(array, True) for array in (act, tag, hidden, long_skip, part, part_gain, text, *mods, gain_row, *skip_ab,
-                                       *text_ab, *qkv_ab, *out_ab)],
+        [(weights[name], False) for name in names] + [(index, None)]
+        + [(array, True) for array in (condition, hidden, long_skip, text, mod_weight, gain_halves, gain_rows, *tables)],
         [
             ((tokens, width), F32, True),
             ((tokens, width), BF, True),
@@ -1586,7 +1641,10 @@
         + [((width, local), BF, True) for _ in range(4)]
         + [((count, width, local), BF, False) for _ in range(2)]
         + [((width, units), BF, False) for _ in range(2)],
-        [vmem(width, span), vmem(text_width, local), vmem(4, 1, width, dtype=F32), vmem(4, mod_rows, dtype=F32),
+        [vmem(width, span), vmem(local, text_width), vmem(block, span, dtype=F32), vmem(1, span, dtype=F32),
+         vmem(RANK, span), vmem(RANK, local), vmem(RANK, local), vmem(3 * RANK, width)]
+        + [vmem(RANK, local) for _ in range(4)]
+        + [vmem(4, 1, width, dtype=F32), vmem(4, mod_rows, dtype=F32),
          vmem(4, 1, width, dtype=F32)]
         + [vmem(steps, chunk, width) for _ in range(5)] + [vmem(count, share, width) for _ in range(5)]
         + [dma(10, 7), dma(10, 7), dma(10), dma(2, count), dma(2, count), dma(2, 3), dma(2, 3), dma(count), dma(count),
@@ -1606,15 +1664,15 @@
 
 
 def cross_backward(count, heads, g_in, cotangent, first, second, block_in, query, inverses, logs, low, u_low, text,
-                   query_weight, out_weight, text_kv, gains, down, up, out_down, out_up, text_down, up_key, up_value):
+                   query_weight, out_weight, text_kv, gains, tables):
     share, width = g_in.shape
     local = query_weight.shape[-1]
     words, text_width = text.shape
     scale = HD ** (-0.5)
 
     def kernel(g_ref, cot, first_ref, second_ref, x_ref, q_ref, inv_ref, log_ref, low_ref, uo_ref, t_ref, hbm_q, hbm_o,
-               kv, gain, a_ref, b_ref, ao, bo, at, bk, bv, g_first, ga_q, gb_q, ga_k, gb_k, ga_v, gb_v, ga_o, gb_o,
-               acc, wq, wo, wsem):
+               kv, gain, dtab, utab, g_first, ga_q, gb_q, ga_k, gb_k, ga_v, gb_v, ga_o, gb_o,
+               acc, wq, wo, b_ref, ao, bk, bv, wsem):
         me = lax.axis_index("tensor")
         loads = [
             pltpu.make_async_copy(source, target, wsem.at[number])
@@ -1625,13 +1683,17 @@
         normal, inverse = stats(second_ref[...])
         g_second = cot[rows_of(me, share), :].astype(F32) + norm_backward(normal, inverse, g_ref[...] * gain[2:3, :])
         g_low = g_second.astype(BF)
-        go = dot_nt(g_low, bo[...]).astype(BF)
+        take_stack(b_ref, utab, OUT_AT[6], count)
+        take_stack(ao, dtab, IN_AT[9], count)
+        take_stack(bk, utab, OUT_AT[7], count)
+        take_stack(bv, utab, OUT_AT[8], count)
+        go = dot_nt(g_low, up_of(utab, 9)).astype(BF)
         gb_o[...] = dot_tn(uo_ref[...], g_low)
         x = x_ref[...]
-        uq = dot_nt(x, a_ref[...]).astype(BF)
+        uq = dot_nt(x, down_of(dtab, 6)).astype(BF)
         words_in = t_ref[...]
-        ut = dot_nt(words_in, at[...]).astype(BF)
-        uk, uv = ut[:, :RANK], ut[:, RANK:]
+        uk = dot_nt(words_in, down_of(dtab, 7)).astype(BF)
+        uv = dot_nt(words_in, down_of(dtab, 8)).astype(BF)
         acc[...] = jnp.zeros_like(acc)
         for load in loads:
             load.wait()
@@ -1677,7 +1739,7 @@
         ga_q[...] = dot_tn(gq_sum, x)
         ga_k[...] = dot_tn(gk_sum.astype(BF), words_in)
         ga_v[...] = dot_tn(gv_sum.astype(BF), words_in)
-        g_x = acc[...] + dot_nn(gq_sum, a_ref[...])
+        g_x = acc[...] + dot_nn(gq_sum, down_of(dtab, 6))
         normal, inverse = stats(first_ref[...])
         g_first[...] = (g_second + norm_backward(normal, inverse, g_x * gain[1:2, :])).astype(BF)
 
@@ -1685,7 +1747,7 @@
         kernel,
         [(array, True) for array in (g_in, cotangent, first, second, block_in, query, inverses, logs, low, u_low, text)]
         + [(query_weight, False), (out_weight, False)]
-        + [(array, True) for array in (text_kv, gains, down, up, out_down, out_up, text_down, up_key, up_value)],
+        + [(array, True) for array in (text_kv, gains, *tables)],
         [
             ((share, width), BF, True),
             ((RANK, width), F32, True),
@@ -1697,13 +1759,13 @@
             ((count, RANK, local), F32, True),
             ((RANK, width), F32, True),
         ],
-        [vmem(share, width, dtype=F32), vmem(count, width, local), vmem(count, width, local), dma(2)],
+        [vmem(share, width, dtype=F32), vmem(count, width, local), vmem(count, width, local)]
+        + [vmem(count, RANK, local) for _ in range(4)] + [dma(2)],
         cost=cost_of(8 * share * width * width, 20e6),
     )
 
 
-def attention_backward(count, heads, g_first, attn_in, query, keys, values, low, logs, inv_q, inv_k, weights, down, ups,
-                       out_down, out_up):
+def attention_backward(count, heads, g_first, attn_in, query, keys, values, low, logs, inv_q, inv_k, weights, tables):
     share, width = g_first.shape
     tokens = attn_in.shape[0]
     local = weights[0].shape[1]
@@ -1714,9 +1776,9 @@
     scale = HD ** (-0.5)
 
     def kernel(g_ref, x_ref, q_ref, k_ref, v_ref, low_ref, log_ref, iq_ref, ik_ref, *refs):
-        (wq, wk, wv, wo, a_ref, bq, bk, bv, ao, bo, total_out, gall, ga_in, gb_q, gb_k, gb_v, ga_o, gb_o, gq_low, gk_acc,
-         gv_acc, swap_out, swap_in, partial_ref, from_left, from_right, stage_right, stage_left, xsend, xrecv,
-         *sems) = refs
+        (wq, wk, wv, wo, dtab, utab, total_out, gall, ga_in, gb_q, gb_k, gb_v, ga_o, gb_o, gq_low, gk_acc,
+         gv_acc, swap_out, swap_in, partial_ref, from_left, from_right, stage_right, stage_left, a_ref, bq, bk,
+         bv, ao, xsend, xrecv, *sems) = refs
         me = lax.axis_index("tensor")
         core = lax.axis_index("ctx")
         peer = {"ctx": 1 - core}
@@ -1727,11 +1789,15 @@
             ref[...] = jnp.zeros_like(ref)
         greet(line_partners(me, count) + [(core >= 0, peer)])
         line_gather_step(gather_line, 0, gall)
+        for number, target in enumerate((bq, bk, bv)):
+            a_ref[number * RANK : (number + 1) * RANK, :] = down_of(dtab, 2 + number)
+            take_local(target, utab, OUT_AT[2 + number], me, count)
+        take_local(ao, dtab, IN_AT[5], me, count)
 
         def attend(place):
             rows = rows_of(place, share)
             g = gall[place]
-            go = dot_nt(g, bo[...]).astype(BF)
+            go = dot_nt(g, up_of(utab, 5)).astype(BF)
             g_attn = (dot_nn(g, wo[...]) + dot_nn(go, ao[...])).astype(BF)
             low = low_ref[rows, :]
             uo = dot_nt(low, ao[...]).astype(BF)
@@ -1758,15 +1824,15 @@
                 parts.append(norm_backward(q.astype(F32), iq_ref[head, rows, :], dq * scale))
             gq_low[rows, :] = jnp.concatenate(parts, axis=1).astype(BF)
 
-        attend(me)
-
         def gather(number, carry):
-            line_gather_step(gather_line, number, gall)
+            @pl.when(number > 0)
+            def _():
+                line_gather_step(gather_line, number, gall)
 
             def side(which, inner):
                 place = me + (2 * which - 1) * number
 
-                @pl.when((place >= 0) & (place < count))
+                @pl.when((place >= 0) & (place < count) & ((number > 0) | (which == 0)))
                 def _():
                     attend(lax.clamp(0, place, count - 1))
 
@@ -1774,7 +1840,7 @@
 
             return lax.fori_loop(0, 2, side, carry)
 
-        lax.fori_loop(1, count, gather, 0)
+        lax.fori_loop(0, count, gather, 0)
         swap_out[0] = (gk_acc[1 - core] * scale).astype(BF)
         swap_out[1] = gv_acc[1 - core].astype(BF)
         swap = push(swap_out, swap_in, xsend, xrecv, peer)
@@ -1818,7 +1884,7 @@
     return call(
         kernel,
         [(array, True) for array in (g_first, attn_in, query, keys, values, low, logs, inv_q, inv_k)]
-        + [(array, True) for array in (*weights, down, *ups, out_down, out_up)],
+        + [(array, True) for array in (*weights, *tables)],
         [
             ((tokens, width), F32, True),
             ((count, share, width), BF, True),
@@ -1831,33 +1897,81 @@
         ],
         [vmem(tokens, local), vmem(2, heads, tokens, HD, dtype=F32), vmem(2, heads, tokens, HD, dtype=F32)]
         + [vmem(2, heads, tokens, HD), vmem(2, heads, tokens, HD)]
-        + buffers + [dma(), dma()] + [dma(count) for _ in range(4)] + [dma(steps) for _ in range(4)],
+        + buffers + [vmem(3 * RANK, width)] + [vmem(RANK, local) for _ in range(4)] + [dma(), dma()] + [dma(count) for _ in range(4)] + [dma(steps) for _ in range(4)],
         collective=4,
         cost=cost_of(16 * tokens * width * local, 60e6),
     )
 
 
-def skip_backward(count, g_attn, g_first, skip_out, hidden, long_skip, weight, gain_halves, down, up, gain_row):
+def back_end(count, g_attn, g_first, skip_out, hidden, long_skip, weight, mod_weight, gain_halves, gain_rows, tables,
+             condition, act_all, wide_grads, local_down, local_up, stacked):
     tokens, width = hidden.shape
     span = weight.shape[-1]
-    share = tokens // count
-    block = share
-
-    def kernel(g_ref, gf_ref, skip_ref, hid, lsk, hbm_w, gains, a_ref, b_ref, gain, out_h, out_l, g_shift,
-               ga, gb, w, buf_h, buf_l, low, wsem, osem):
+    block = tokens // count
+    own_rows = RANK // count
+    columns = IN_AT[12] + OUT_AT[12]
+    half = -(-columns // 256) * 128
+    mod_rows = mod_weight.shape[0]
+    wide_at, wide = list(wide_grads), list(wide_grads.values())
+    local_at = [number for number in local_down] + [IN_AT[12] + number for number in local_up]
+    local = list(local_down.values()) + list(local_up.values())
+    stacked_at, stack = list(stacked), list(stacked.values())
+
+    def kernel(g_ref, gf_ref, skip_ref, hid, lsk, hbm_w, wm, gains, gain, dtab, utab, cond, act_ref, *refs):
+        wide_refs, refs = refs[: len(wide)], refs[len(wide) :]
+        local_refs, refs = refs[: len(local)], refs[len(local) :]
+        stack_refs, refs = refs[: len(stack)], refs[len(stack) :]
+        (out_h, out_l, out_a, out_b, out_c, w, buf_h, buf_l, low, table, swap_out, swap_in, partial_ref, from_left,
+         from_right, stage_right, stage_left, summed, slots, other_out, other_in, shifts, shift_in, act_out, act_in, g_act,
+         wsem, osem, ssem, rsem, dsend, drecv, msend, mrecv, *sems) = refs
         me = lax.axis_index("tensor")
+        core = lax.axis_index("ctx")
+        dp = lax.axis_index("dp")
+        peer = {"ctx": 1 - core}
+        line = Line(me, count, *sems)
+        peers = [{"dp": xor_place(dp, number)} for number in (1, 2, 3)]
         load = pltpu.make_async_copy(hbm_w, w, wsem)
         load.start()
-        g_shift[...] = jnp.zeros_like(g_shift)
+        greet(line_partners(me, count) + [(core >= 0, peer)] + [(core >= 0, device) for device in peers])
+
+        g_shift = jnp.sum(g_ref[...], axis=0, keepdims=True)
+        shift_in[0] = g_shift
+        swap_shift = push(shift_in.at[0], shift_in.at[1], ssem.at[2], rsem.at[2], peer)
+        swap_shift.start()
+        act = act_ref[dp, :, :width]
+        act_low = act.astype(BF)
+        mod_u = dot_nt(act_low, down_of(dtab, 1))
+        once = jnp.where(me == 0, 1.0, 0.0)
+        shift_u = dot_nt(g_shift.astype(BF), up_of(utab, 1))
+        mod_a = jnp.concatenate([shift_u * once, jnp.zeros((7, RANK), F32)], axis=0).astype(BF)
+        mod_b = jnp.concatenate([mod_u * once, jnp.zeros((7, RANK), F32)], axis=0).astype(BF)
+        act_pad = jnp.concatenate([act_low.astype(F32), jnp.zeros((7, width), F32)], axis=0).astype(BF)
+        shift_pad = jnp.concatenate([g_shift, jnp.zeros((7, width), F32)], axis=0).astype(BF)
+
+        table[...] = jnp.zeros_like(table)
+        table[:, IN_AT[1] : IN_AT[2]] = dot_tn(mod_a, act_pad)
+        table[:, IN_AT[12] + OUT_AT[1] : IN_AT[12] + OUT_AT[2]] = dot_tn(mod_b, shift_pad)
+        for start, ref in zip(wide_at, wide_refs):
+            table[:, start : start + ref.shape[1]] = ref[...]
+        for start, ref in zip(stacked_at, stack_refs):
+            size = ref.shape[2]
+            for place in range(count):
+                table[:, start + place * size : start + (place + 1) * size] = ref[place]
+        for place in range(count):
+            @pl.when(me == place)
+            def _(place=place):
+                for start, ref in zip(local_at, local_refs):
+                    size = ref.shape[1]
+                    table[:, start + place * size : start + (place + 1) * size] = ref[...]
+
         load.wait()
 
-        def step(number, carry):
+        def skip_block(number, own):
             rows = rows_of(number, block)
             ga_in = g_ref[rows, :]
-            g_shift[...] += jnp.sum(ga_in, axis=0, keepdims=True)
             normal, inverse = stats(skip_ref[rows, :])
             g_low = (
-                gf_ref[number].astype(F32) + norm_backward(normal, inverse, ga_in * gain[...])
+                gf_ref[number].astype(F32) + norm_backward(normal, inverse, ga_in * gain[0:1, :])
             ).astype(BF)
             left = hid[rows, :].astype(F32)
             right = lsk[rows, :].astype(F32)
@@ -1868,21 +1982,22 @@
             inverse = lax.rsqrt(spread / (2 * width) + NORM_EPS)
             left = left * inverse
             right = right * inverse
-            gu = dot_nt(g_low, b_ref[...]).astype(BF)
-
-            @pl.when(number == me)
+            gu = dot_nt(g_low, up_of(utab, 0)).astype(BF)
+            a_left, a_right = dtab[:, :width], dtab[:, width : 2 * width]
+
+            @pl.when(own)
             def _():
                 low_l = (left * gains[0:1, :]).astype(BF)
                 low_r = (right * gains[1:2, :]).astype(BF)
-                u = (dot_nt(low_l, a_ref[0]) + dot_nt(low_r, a_ref[1])).astype(BF)
-                ga[0] = dot_tn(gu, low_l)
-                ga[1] = dot_tn(gu, low_r)
-                gb[...] = dot_tn(u, g_low)
+                u = (dot_nt(low_l, a_left) + dot_nt(low_r, a_right)).astype(BF)
+                table[:, :width] = dot_tn(gu, low_l)
+                table[:, width : 2 * width] = dot_tn(gu, low_r)
+                table[:, IN_AT[12] : IN_AT[12] + width] = dot_tn(u, g_low)
 
             for place in range(count):
                 low[:, place * span : (place + 1) * span] = dot_nn(g_low, w[place])
-            gl = (low[:, :width] + dot_nn(gu, a_ref[0])) * gains[0:1, :]
-            gr = (low[:, width:] + dot_nn(gu, a_ref[1])) * gains[1:2, :]
+            gl = (low[:, :width] + dot_nn(gu, a_left)) * gains[0:1, :]
+            gr = (low[:, width:] + dot_nn(gu, a_right)) * gains[1:2, :]
             mean = (jnp.sum(gl, axis=-1, keepdims=True) + jnp.sum(gr, axis=-1, keepdims=True)) / (2 * width)
             inner = (
                 jnp.sum(gl * left, axis=-1, keepdims=True) + jnp.sum(gr * right, axis=-1, keepdims=True)
@@ -1891,71 +2006,63 @@
             buf_l[number] = inverse * (gr - mean - right * inner)
             pltpu.make_async_copy(buf_h.at[number], out_h.at[rows, :], osem.at[0, number]).start()
             pltpu.make_async_copy(buf_l.at[number], out_l.at[rows, :], osem.at[1, number]).start()
+
+        swap = push(swap_out, swap_in, ssem.at[0], rsem.at[0], peer)
+        shift_sends = [
+            push(shifts.at[dp], shifts.at[dp], msend.at[0, number], mrecv.at[0, number], device)
+            for number, device in enumerate(peers)
+        ]
+        act_sends = [
+            push(act_out.at[xor_place(dp, number)], act_in.at[dp], msend.at[1, number - 1], mrecv.at[1, number - 1],
+                 peers[number - 1])
+            for number in (1, 2, 3)
+        ]
+
+        def step(number, carry):
+            place = lax.rem(me + number, count)
+            skip_block(place, number == 0)
+
+            @pl.when(number == 0)
+            def _():
+                for which in range(2):
+                    @pl.when(core == which)
+                    def _(which=which):
+                        swap_out[...] = table[:, (1 - which) * half : (2 - which) * half].astype(BF)
+
+                swap.start()
+                swap_shift.wait()
+                shifts[dp] = shift_in[0] + shift_in[1]
+                for send in shift_sends:
+                    send.start()
+
+            @pl.when(number == 1)
+            def _():
+                swap.wait()
+                for which in range(2):
+                    @pl.when(core == which)
+                    def _(which=which):
+                        for part in range(count):
+                            at = slice(part * own_rows, (part + 1) * own_rows)
+                            mine = table[at, which * half : (which + 1) * half]
+                            partial_ref[part] = (mine + swap_in[at, :].astype(F32)).astype(BF)
+
+                for other in (1, 2, 3):
+                    source = shifts.at[xor_place(dp, other)]
+                    push(source, source, msend.at[0, other - 1], mrecv.at[0, other - 1], peers[other - 1]).wait_recv()
+                every = jnp.concatenate([shifts[sequence] for sequence in range(4)], axis=0).astype(BF)
+                products = dot_nt(every, wm[...])
+                for sequence in range(4):
+                    act_out[sequence] = products[sequence : sequence + 1]
+                for send in act_sends:
+                    send.start()
+
+            @pl.when((number >= 1) & (number < count))
+            def _():
+                line_scatter_step(line, number - 1, partial_ref, from_left, from_right, stage_right, stage_left)
+
             return carry
 
-        lax.fori_loop(0, tokens // block, step, 0)
-
-        def drain(number, carry):
-            rows = rows_of(number, block)
-            pltpu.make_async_copy(buf_h.at[number], out_h.at[rows, :], osem.at[0, number]).wait()
-            pltpu.make_async_copy(buf_l.at[number], out_l.at[rows, :], osem.at[1, number]).wait()
-            return carry
-
-        lax.fori_loop(0, tokens // block, drain, 0)
-
-    blocks = tokens // block
-    return call(
-        kernel,
-        [(array, True) for array in (g_attn, g_first, skip_out, hidden, long_skip)]
-        + [(weight, False)]
-        + [(array, True) for array in (gain_halves, down, up, gain_row)],
-        [
-            ((tokens, width), F32, False),
-            ((tokens, width), F32, False),
-            ((1, width), F32, True),
-            ((2, RANK, width), F32, True),
-            ((RANK, width), F32, True),
-        ],
-        [
-            vmem(count, width, span),
-            vmem(blocks, block, width, dtype=F32),
-            vmem(blocks, block, width, dtype=F32),
-            vmem(block, 2 * width, dtype=F32),
-            dma(),
-            dma(2, blocks),
-        ],
-        cost=cost_of(4 * tokens * width * width, 30e6),
-    )
-
-
-def adapter_reduce(count, table, chosen):
-    ranks, tiles, lanes = table.shape
-    half = tiles // 2
-    own_rows = ranks // count
-
-    def kernel(t_ref, sel, out, swap_out, swap_in, partial_ref, from_left, from_right, stage_right, stage_left, summed,
-               slots, other_out, other_in, ssem, rsem, dsend, drecv, *sems):
-        me = lax.axis_index("tensor")
-        core = lax.axis_index("ctx")
-        dp = lax.axis_index("dp")
-        peer = {"ctx": 1 - core}
-        line = Line(me, count, *sems)
-        peers = [{"dp": xor_place(dp, number)} for number in (1, 2, 3)]
-        greet(line_partners(me, count) + [(core >= 0, peer)] + [(core >= 0, device) for device in peers])
-        swap_out[...] = t_ref[:, pl.ds(pl.multiple_of((1 - core) * half, 16), half), :].astype(BF)
-        swap = push(swap_out, swap_in, ssem.at[0], rsem.at[0], peer)
-        swap.start()
-        swap.wait()
-        for number in range(count):
-            part = slice(number * own_rows, (number + 1) * own_rows)
-            mine = t_ref[part, pl.ds(pl.multiple_of(core * half, 16), half), :]
-            partial_ref[number] = (mine + swap_in[part].astype(F32)).astype(BF)
-
-        def scatter(number, carry):
-            line_scatter_step(line, number, partial_ref, from_left, from_right, stage_right, stage_left)
-            return carry
-
-        lax.fori_loop(0, count - 1, scatter, 0)
+        lax.fori_loop(0, count, step, 0)
         line_scatter_finish(line, partial_ref, from_left, from_right, stage_right, stage_left, summed)
         slots[dp] = summed[...].astype(BF)
         sends = [
@@ -1964,60 +2071,89 @@
         ]
         for send in sends:
             send.start()
+
+        act_in[dp] = act_out[dp]
+        for number in (1, 2, 3):
+            source = act_in.at[xor_place(dp, number)]
+            push(source, source, msend.at[1, number - 1], mrecv.at[1, number - 1], peers[number - 1]).wait_recv()
+        for place in range(4):
+            g_act[:, place * mod_rows : (place + 1) * mod_rows] = act_in[place]
+        full_u = dot_nt(shifts[dp].astype(BF), up_of(utab, 1)).astype(BF)
+        grad = g_act[...] + dot_nn(full_u, down_of(dtab, 1))
+        value = cond[...].astype(F32)
+        gate = 1.0 / (1.0 + jnp.exp(-value))
+        out_c[...] = grad * gate * (1.0 + value * (1.0 - gate))
+
         for number in (1, 2, 3):
             source = slots.at[xor_place(dp, number)]
             push(source, source, dsend.at[number - 1], drecv.at[number - 1], peers[number - 1]).wait_recv()
 
         def total(which):
-            result = jnp.zeros((own_rows, half, lanes), F32)
+            slot = (dp * 2 + which).astype(F32)
+            result = jnp.zeros((own_rows, half), F32)
             for sequence in range(4):
-                result = result + slots[sequence].astype(F32) * sel[which, sequence]
+                chosen = jnp.where(act_ref[sequence, :, width : width + 1] == slot, 1.0, 0.0)
+                result = result + slots[sequence].astype(F32) * chosen
             return result
 
         other_out[...] = total(1 - core).astype(BF)
-        swap = push(other_out, other_in, ssem.at[1], rsem.at[1], peer)
-        swap.start()
-        out[core] = total(core)
-        for send in sends:
+        last = push(other_out, other_in, ssem.at[1], rsem.at[1], peer)
+        last.start()
+        mine = total(core)
+        last.wait_recv()
+        other = other_in[...].astype(F32)
+        for which in range(2):
+            @pl.when(core == which)
+            def _(which=which):
+                both = (mine, other) if which == 0 else (other, mine)
+                cut = IN_AT[12]
+                whole = jnp.concatenate(both, axis=1)
+                out_a[...] = whole[:, :cut]
+                out_b[...] = whole[:, cut:columns]
+
+        last.wait_send()
+        for send in sends + shift_sends + act_sends:
             send.wait_send()
-        swap.wait()
-        out[1 - core] = other_in[...].astype(F32)
-
-    block = (own_rows, half, lanes)
+
+        def drain(number, carry):
+            rows = rows_of(number, block)
+            pltpu.make_async_copy(buf_h.at[number], out_h.at[rows, :], osem.at[0, number]).wait()
+            pltpu.make_async_copy(buf_l.at[number], out_l.at[rows, :], osem.at[1, number]).wait()
+            return carry
+
+        lax.fori_loop(0, count, drain, 0)
+
+    part = (own_rows, half)
     return call(
         kernel,
-        [(table, True), (chosen, True)],
-        [((2, *block), F32, True)],
-        [vmem(ranks, half, lanes), vmem(ranks, half, lanes)]
-        + [vmem(count, *block) for _ in range(5)]
-        + [vmem(*block, dtype=F32), vmem(4, *block), vmem(*block), vmem(*block)]
-        + [dma(2), dma(2), dma(3), dma(3)] + [dma(count) for _ in range(4)],
+        [(array, True) for array in (g_attn, g_first, skip_out, hidden, long_skip)]
+        + [(weight, False)]
+        + [(array, True) for array in (mod_weight, gain_halves, gain_rows, *tables, condition, act_all, *wide, *local,
+                                       *stack)],
+        [
+            ((tokens, width), F32, False),
+            ((tokens, width), F32, False),
+            ((own_rows, IN_AT[12]), F32, True),
+            ((own_rows, OUT_AT[12]), F32, True),
+            ((1, width), F32, True),
+        ],
+        [
+            vmem(count, width, span),
+            vmem(count, block, width, dtype=F32),
+            vmem(count, block, width, dtype=F32),
+            vmem(block, 2 * width, dtype=F32),
+            vmem(RANK, 2 * half, dtype=F32),
+            vmem(RANK, half),
+            vmem(RANK, half),
+        ]
+        + [vmem(count, *part) for _ in range(5)]
+        + [vmem(*part, dtype=F32), vmem(4, *part), vmem(*part), vmem(*part)]
+        + [vmem(4, 1, width, dtype=F32), vmem(2, 1, width, dtype=F32), vmem(4, 1, mod_rows, dtype=F32),
+           vmem(4, 1, mod_rows, dtype=F32), vmem(1, width, dtype=F32)]
+        + [dma(), dma(2, count), dma(3), dma(3), dma(3), dma(3), dma(2, 3), dma(2, 3)] + [dma(count) for _ in range(4)],
         collective=5,
-        cost=cost_of(1e6, 10e6),
-    )[0]
-
-
-def swap_cores(value):
-    return lax.ppermute(value, "ctx", [(0, 1), (1, 0)])
-
-
-def exchange_dp(rows):
-    dp = lax.axis_index("dp")
-    got = [lax.dynamic_slice_in_dim(rows, dp, 1, 0)]
-    for number in (1, 2, 3):
-        row = lax.dynamic_slice_in_dim(rows, dp ^ number, 1, 0)
-        got.append(lax.ppermute(row, "dp", [(place, place ^ number) for place in range(4)]))
-    return got
-
-
-def gather_dp(row):
-    dp = lax.axis_index("dp")
-    table = jnp.zeros((4, row.shape[1]), row.dtype)
-    table = lax.dynamic_update_slice_in_dim(table, row, dp, 0)
-    for number in (1, 2, 3):
-        got = lax.ppermute(row, "dp", [(place, place ^ number) for place in range(4)])
-        table = lax.dynamic_update_slice_in_dim(table, got, dp ^ number, 0)
-    return table
+        cost=cost_of(4 * tokens * width * width, 30e6),
+    )
 
 
 def fused_body(
@@ -2049,34 +2185,14 @@
     core = lax.axis_index("ctx")
     dp = lax.axis_index("dp")
     hidden, long_skip, text, cot = hidden[0], long_skip_input[0], projected_text_tokens[0], cotangent[0]
-    tokens, width = hidden.shape
     local = self_query_weight.shape[1]
     heads = local // HD
-    ff = feedforward_up_weight.shape[1]
-    span = skip_projection_weight.shape[0]
-    share = tokens // count
-    in_sizes = [2 * MODEL_WIDTH] + [MODEL_WIDTH] * 6 + [TW, TW, MODEL_WIDTH, MODEL_WIDTH, FF]
-    out_sizes = [MODEL_WIDTH] * 10 + [FF, MODEL_WIDTH]
-    in_at = [sum(in_sizes[:number]) for number in range(12)]
-    out_at = [sum(out_sizes[:number]) for number in range(12)]
     index = sequence_adapter_index[0]
-    down_table = lax.dynamic_index_in_dim(adapter_down_factor, index, 0, keepdims=False)
-    up_table = lax.dynamic_index_in_dim(adapter_up_factor, index, 0, keepdims=False)
-
-    def down_full(number):
-        return down_table[:, in_at[number] : in_at[number] + in_sizes[number]]
-
-    def up_full(number):
-        return up_table[:, out_at[number] : out_at[number] + out_sizes[number]]
-
-    def down_local(number, size):
-        return lax.dynamic_slice_in_dim(down_table, in_at[number] + rank * size, size, 1)
-
-    def up_local(number, size):
-        return lax.dynamic_slice_in_dim(up_table, out_at[number] + rank * size, size, 1)
-
-    def stack(table):
-        return jnp.transpose(table.reshape(RANK, count, -1), (1, 0, 2))
+    tables = (
+        lax.dynamic_index_in_dim(adapter_down_factor, index, 0, keepdims=False),
+        lax.dynamic_index_in_dim(adapter_up_factor, index, 0, keepdims=False),
+    )
+    gain_halves = skip_norm_gain.reshape(2, MODEL_WIDTH)
 
     weights = {
         "skip": skip_projection_weight.T,
@@ -2084,105 +2200,56 @@
         "k": self_key_weight,
         "v": self_value_weight,
         "o": attention_output_weight.T,
-        "ck": cross_key_weight,
-        "cv": cross_value_weight,
+        "ck": cross_key_weight.T,
+        "cv": cross_value_weight.T,
         "cq": cross_query_weight,
         "co": cross_output_weight.T,
         "up": feedforward_up_weight,
         "dn": feedforward_down_weight.T,
     }
-    mod_rows = shift_modulation_weight.shape[0]
-    act_wide, silu_pull = jax.vjp(jax.nn.silu, condition.astype(F32))
-    act_low = act_wide.astype(BF)
-    mod_u = dot_nt(act_low, down_full(1))
-    tag = jnp.full((1, 128), index, jnp.int32).astype(F32)
-
-    both = jnp.concatenate([hidden, long_skip], axis=1)
-    part = lax.dynamic_slice_in_dim(both, rank * span, span, 1)
-    part_gain = lax.dynamic_slice_in_dim(skip_norm_gain, rank * span, span, 0)[None, :]
-    text_down = jnp.concatenate([down_full(7), down_full(8)], axis=0)
-    qkv_down = jnp.concatenate([down_full(2), down_full(3), down_full(4)], axis=0)
-    qkv_up = [up_local(number, local) for number in (2, 3, 4)]
-    out_down, out_up = down_local(5, local), up_full(5)
     (skip_out, attn_in, query, keys, values, low, logs, inv_q, inv_k, summed, act_all, text_kv, wq, wk, wv, wo, wcq, wco,
      wup, wdn) = front(
-        count, heads, act_low, tag, hidden, long_skip, part, part_gain, text, weights,
-        (shift_modulation_weight, down_full(1), up_full(1)), norm_gain_rows[0:1],
-        (down_local(0, span), up_full(0)), (text_down, up_local(7, local), up_local(8, local)), (qkv_down, *qkv_up),
-        (out_down, out_up),
-    )
-    indices = act_all[:, 0, MODEL_WIDTH].astype(jnp.int32)
-    cross_down, cross_up = down_full(6), stack(up_full(6))
-    cout_down, cout_up = stack(down_full(9)), up_full(9)
+        count, heads, condition, sequence_adapter_index, hidden, long_skip, text, weights, shift_modulation_weight,
+        gain_halves, norm_gain_rows, tables,
+    )
     first, second, cross_in, mlp_in, cquery, cinv, clogs, clow, cu, skip_half = cross_forward(
-        count, heads, summed, skip_out, wcq, wco, weights["skip"], text_kv, norm_gain_rows, cross_down, cross_up,
-        cout_down, cout_up,
+        count, heads, summed, skip_out, wcq, wco, weights["skip"], text_kv, norm_gain_rows, tables
     )
     g_mlp_in, down_part, g_up_a, g_up_b, g_down_a, g_down_b, skip_all = feed_forward(
-        count, mlp_in, cot, second, wup, wdn, skip_half, down_full(10), up_local(10, ff), down_local(11, ff), up_full(11),
+        count, mlp_in, cot, second, wup, wdn, skip_half, tables
     )
     block_out = lax.psum(down_part, "tensor")
     g_first, g_cq_a, g_cq_b, g_ck_a, g_ck_b, g_cv_a, g_cv_b, g_co_a, g_co_b = cross_backward(
-        count, heads, g_mlp_in, cot, first, second, cross_in, cquery, cinv, clogs, clow, cu, text, wcq, wco,
-        text_kv, norm_gain_rows, cross_down, cross_up, cout_down, cout_up, text_down, stack(up_full(7)),
-        stack(up_full(8)),
+        count, heads, g_mlp_in, cot, first, second, cross_in, cquery, cinv, clogs, clow, cu, text, wcq, wco, text_kv,
+        norm_gain_rows, tables,
     )
     g_attn, g_first_all, g_qkv_a, g_q_b, g_k_b, g_v_b, g_o_a, g_o_b = attention_backward(
-        count, heads, g_first, attn_in, query, keys, values, low, logs, inv_q, inv_k, (wq, wk, wv, wo), qkv_down,
-        qkv_up, out_down, out_up,
-    )
-    skip_down = jnp.transpose(down_full(0).reshape(RANK, 2, MODEL_WIDTH), (1, 0, 2))
-    hidden_grad, skip_grad, g_shift, g_skip_a, g_skip_b = skip_backward(
-        count, g_attn, g_first_all, skip_out, hidden, long_skip, skip_all,
-        skip_norm_gain.reshape(2, MODEL_WIDTH), skip_down, up_full(0), norm_gain_rows[0:1],
-    )
-
-    g_mod_u = dot_nt(g_shift.astype(BF), up_full(1))
-    once = (rank == 0).astype(F32)
-    g_mod_a = jnp.dot(g_mod_u.T, act_low.astype(F32), precision=PRECISE) * once
-    g_mod_b = jnp.dot(mod_u.T, g_shift, precision=PRECISE) * once
-    shift_sum = g_shift + swap_cores(g_shift)
-    shift_all = gather_dp(shift_sum).astype(BF)
-    act_parts = exchange_dp(dot_nt(shift_all, shift_modulation_weight))
-    g_act = jnp.zeros((1, MODEL_WIDTH), F32)
-    for number, piece in enumerate(act_parts):
-        g_act = lax.dynamic_update_slice_in_dim(g_act, piece, (dp ^ number) * mod_rows, 1)
-    shift_u = jnp.dot(shift_sum, up_full(1).astype(F32).T, precision=PRECISE)
-    g_act = g_act + jnp.dot(shift_u, down_full(1).astype(F32), precision=PRECISE)
-    g_condition = silu_pull(g_act)[0][0]
+        count, heads, g_first, attn_in, query, keys, values, low, logs, inv_q, inv_k, (wq, wk, wv, wo), tables
+    )
+    base = IN_AT[12]
+    hidden_grad, skip_grad, grad_down, grad_up, g_condition = back_end(
+        count, g_attn, g_first_all, skip_out, hidden, long_skip, skip_all, shift_modulation_weight, gain_halves,
+        norm_gain_rows, tables, condition, act_all,
+        {
+            IN_AT[6]: g_cq_a, IN_AT[7]: g_ck_a, IN_AT[8]: g_cv_a, IN_AT[10]: g_up_a,
+            IN_AT[2]: g_qkv_a[:RANK], IN_AT[3]: g_qkv_a[RANK : 2 * RANK], IN_AT[4]: g_qkv_a[2 * RANK :],
+            base + OUT_AT[5]: g_o_b, base + OUT_AT[9]: g_co_b, base + OUT_AT[11]: g_down_b,
+        },
+        {IN_AT[5]: g_o_a, IN_AT[11]: g_down_a},
+        {OUT_AT[2]: g_q_b, OUT_AT[3]: g_k_b, OUT_AT[4]: g_v_b, OUT_AT[10]: g_up_b},
+        {
+            IN_AT[9]: g_co_a, base + OUT_AT[6]: g_cq_b, base + OUT_AT[7]: g_ck_b, base + OUT_AT[8]: g_cv_b,
+        },
+    )
     size = MODEL_WIDTH // (2 * count)
-    condition_gradient = lax.dynamic_slice_in_dim(g_condition, (core * count + rank) * size, size, 0)
-
-    def unstack(value):
-        return jnp.transpose(value, (1, 0, 2)).reshape(RANK, -1)
-
-    def place_local(value, total):
-        return lax.dynamic_update_slice_in_dim(jnp.zeros((RANK, total), F32), value, rank * value.shape[1], 1)
-
-    table = jnp.concatenate(
-        [
-            g_skip_a[0], g_skip_a[1], g_mod_a, g_qkv_a[:RANK], g_qkv_a[RANK : 2 * RANK], g_qkv_a[2 * RANK :],
-            place_local(g_o_a, MODEL_WIDTH), g_cq_a, g_ck_a, g_cv_a, unstack(g_co_a), g_up_a, place_local(g_down_a, FF),
-            g_skip_b, g_mod_b, place_local(g_q_b, MODEL_WIDTH), place_local(g_k_b, MODEL_WIDTH),
-            place_local(g_v_b, MODEL_WIDTH), g_o_b, unstack(g_cq_b), unstack(g_ck_b), unstack(g_cv_b), g_co_b,
-            place_local(g_up_b, FF), g_down_b,
-        ],
-        axis=1,
-    )
-    wide_a, wide_b = sum(in_sizes) // 128, sum(out_sizes) // 128
-    tiles = -(-(wide_a + wide_b) // 32) * 32
-    table = jnp.pad(table.reshape(RANK, wide_a + wide_b, 128), ((0, 0), (0, tiles - wide_a - wide_b), (0, 0)))
-    chosen = (indices[None, :] == (dp * 2 + jnp.arange(2, dtype=jnp.int32))[:, None]).astype(F32)
-    chosen = jnp.broadcast_to(chosen[:, :, None, None], (2, 4, 1, 128))
-    reduced = adapter_reduce(count, table, chosen)
-    reduced = jnp.transpose(reduced, (1, 0, 2, 3)).reshape(RANK // count, tiles, 128)
+    condition_gradient = lax.dynamic_slice_in_dim(g_condition[0], (core * count + rank) * size, size, 0)
     return (
         block_out[None],
         hidden_grad[None],
         skip_grad[None],
         condition_gradient,
-        reduced[:, :wide_a].reshape(-1),
-        reduced[:, wide_a : wide_a + wide_b].reshape(-1),
+        grad_down.reshape(-1),
+        grad_up.reshape(-1),
     )
 
 

time: 567 us -> 503 us (0.89)
  the two profiles are of different devices: /device:TPU:9 before, /device:TPU:0 now
where the time goes in v3:
time: 503 us; the launch traced here: 494 us
  Pallas kernels  457 us (91%)
  local copies, waits for them, and re-layouts  21.2 us (4%)
  between operations  15.3 us (3%)
    pallas_call x6, Pallas kernels, call(): pl.pallas_call(kernel, out_shape=[jax.ShapeDtypeStruct(shape, dtype) for...  457 us
  transfers between devices with their start and end apart: 1, of which 0 were waited for; matrix products, arithmetic and copies ran while one was open for 1% of the time, Pallas kernels for 37%

profile of v3, /device:TPU:0, one launch (start us, length us, event | category | flops | bytes accessed | tf_op | source)
XLA Modules:
  0.0 494.1 jit_solution(1767130866386051301)
XLA Ops:
  7.2 0.0 copy-start.2
  7.2 0.0 copy-start.5
  7.2 0.0 copy-start.3
  7.2 0.0 copy-start.4
  7.2 0.0 all-reduce.2.cloned.1.call-start
  8.0 2.0 dynamic-slice_bitcast_fusion.dtab.refs_4_
  10.0 2.0 dynamic-slice_bitcast_fusion.1.utab.refs_5_
  12.0 0.0 copy-done.2
  12.0 1.0 copy.28
  13.0 0.0 copy-done.5
  13.0 0.6 reshape.22.halves.gains
  13.6 0.0 copy-done.3
  13.7 0.9 copy.29
  14.5 0.0 copy-done.4
  14.5 0.9 copy.30
  15.4 166.8 %shard_map.253 = (f32[512,1408]{1,0:T(8,128)}, bf16[512,1408]{1,0:T(8,128)(2,1)}, bf16[4,512,88]{2,1,0:T(8,128)(2,1)}, bf16[2,4,512,88]{3,2,1,0:T(8,128)(2,1)}, ...) custom-call(bf16[352,704]{1,0:T(8,128)(2,1)} %bitcast.26, ...), custom_call_target="tpu_custom_call" | custom-call | flops 2030043136 | bytes 60000000 | tf_op jit(solution)/shard_map/pallas_call | solution.py:919
  182.2 29.9 %shard_map.254 = (f32[128,1408]{1,0:T(8,128)}, f32[128,1408]{1,0:T(8,128)}, bf16[128,1408]{1,0:T(8,128)(2,1)}, bf16[128,1408]{1,0:T(8,128)(2,1)}, bf16[4,4,128,8...) custom-call(f32[128,1408]{1,0:T(8,128)} %get-tuple-element.65.sum_re, ...), custom_call_target="tpu_custom_call" | custom-call | flops 1015021568 | bytes 20000000 | tf_op jit(solution)/shard_map/pallas_call | solution.py:919
  212.1 80.2 %shard_map.255 = (f32[128,1408]{1,0:T(8,128)}, bf16[512,1408]{1,0:T(8,128)(2,1)}, f32[16,1408]{1,0:T(8,128)}, f32[16,1536]{1,0:T(8,128)}, f32[16,1536]{1,0:T(8,1...) custom-call(bf16[128,1408]{1,0:T(8,128)(2,1)} %get-tuple-element.70.x_ref, bf16[512,1408]{1,0:T(8,128)(2,1)} %bitcast.33, ...), custom_call_target="tpu_custom_call" | custom-call | flops 8858370048 | bytes 60000000 | tf_op jit(solution)/shard_map/pallas_call | solution.py:919
  292.3 0.0 all-reduce.2.cloned.1.call-update
  292.3 24.7 %shard_map.256 = (bf16[128,1408]{1,0:T(8,128)(2,1)}, f32[16,1408]{1,0:T(8,128)}, f32[4,16,352]{2,1,0:T(8,128)}, f32[16,1024]{1,0:T(8,128)}, f32[4,16,352]{2,1,0:...) custom-call(f32[128,1408]{1,0:T(8,128)} %get-tuple-element.76.g_ref, ...), custom_call_target="tpu_custom_call" | custom-call | flops 2030043136 | bytes 20000000 | tf_op jit(solution)/shard_map/pallas_call | solution.py:919
  317.0 114.9 %shard_map.257 = (f32[512,1408]{1,0:T(8,128)}, bf16[4,128,1408]{2,1,0:T(8,128)(2,1)}, f32[48,1408]{1,0:T(8,128)}, f32[16,352]{1,0:T(8,128)}, f32[16,352]{1,0:T(8...) custom-call(bf16[128,1408]{1,0:T(8,128)(2,1)} %get-tuple-element.84.g_ref, ...), custom_call_target="tpu_custom_call" | custom-call | flops 4060086272 | bytes 60000000 | tf_op jit(solution)/shard_map/pallas_call | solution.py:919
  431.9 1.7 fusion
  433.6 41.0 %shard_map.258 = (f32[512,1408]{1,0:T(8,128)}, f32[512,1408]{1,0:T(8,128)}, f32[4,22272]{1,0:T(4,128)}, f32[4,21632]{1,0:T(4,128)}, f32[1,1408]{1,0:T(1,128)}) custom-call(f32[512,1408]{1,0:T(8,128)} %get-tuple-element.97.g_ref, bf16[4,128,1408]{2,1,0:T(8,128)(2,1)} %get-tuple-element.98.gf_ref, f32[512,1408]{1,0:T(8,128)} %get-tuple-element.66.skip_ref, ...), custom_call_target="tpu_custom_call" | custom-call | flops 4060086272 | bytes 30000000 | tf_op jit(solution)/shard_map/pallas_call | solution.py:919
  474.6 0.0 copy-start.1
  474.7 2.0 reshape.23
  476.7 1.8 reshape.24
  478.5 1.3 constant_dynamic-slice_fusion
  479.8 2.6 copy.36
  482.3 0.0 copy-done.1
  482.3 1.6 copy.37
  483.9 1.3 copy-done
  485.2 1.6 copy.38
  (2 shorter events, 0.0 us)
Async XLA Ops:
  7.2 4.8 copy-start.2
  7.2 5.9 %copy-start.5 = (f32[2816]{0:T(1024)S(1)}, f32[2816]{0:T(1024)}, u32[]{:S(2)}) copy-start(f32[2816]{0:T(1024)} %param.39) | copy-start | bytes 33796
  7.2 6.5 %copy-start.3 = (bf16[352,352]{1,0:T(8,128)(2,1)S(1)}, bf16[352,352]{1,0:T(8,128)(2,1)}, u32[]{:S(2)}) copy-start(bf16[352,352]{1,0:T(8,128)(2,1)} %param.32) | copy-start | bytes 743428
  7.2 7.3 %copy-start.4 = (bf16[352,352]{1,0:T(8,128)(2,1)S(1)}, bf16[352,352]{1,0:T(8,128)(2,1)}, u32[]{:S(2)}) copy-start(bf16[352,352]{1,0:T(8,128)(2,1)} %param.36) | copy-start | bytes 743428
  7.2 472.6 %all-reduce.2.cloned.1.call-start = ((), (), s32[]{:S(2)}) async-start(), calls=%async_computation | async-start | bytes 2883584 | tf_op jit(solution)/shard_map/psum | solution.py:2221
  474.6 7.7 %copy-start.1 = (f32[512,1408]{1,0:T(8,128)S(1)}, f32[512,1408]{1,0:T(8,128)}, u32[]{:S(2)}) copy-start(f32[512,1408]{1,0:T(8,128)} %get-tuple-element.119) | copy-start | bytes 8650756
  482.3 2.9 copy-start
Sparse Core Ops, SparseCore 0:
  292.4 72.3 all-reduce.1

commit v4 on v3

--- a/solution.py
+++ b/solution.py
@@ -661,7 +661,8 @@
         return push(source, target, self.sems[2].at[slot], self.sems[3].at[slot], self.left)
 
 
-def line_reduce_all(line, steps, compute, partial_ref, from_left, from_right, stage_right, stage_left, finish, beside=None):
+def line_reduce_all(line, steps, compute, partial_ref, from_left, from_right, stage_right, stage_left, finish,
+                    beside=None, after=None):
     me, count = line.me, line.count
     far = count - 1 - me
 
@@ -742,6 +743,9 @@
                 @pl.when(jnp.logical_not(line.has_right))
                 def _():
                     finish(slot, partial_ref[slot].astype(F32) + from_left[slot].astype(F32))
+
+            if after is not None:
+                after(slot)
 
         return carry
 
@@ -979,222 +983,311 @@
         target[place] = table[:, start + place * size : start + (place + 1) * size]
 
 
-def cross_forward(count, heads, summed, skip_out, query_weight, out_weight, skip_piece, text_kv, gains, tables):
+def norm_backward(normal, inverse, grad):
+    return inverse * (
+        grad
+        - jnp.mean(grad, axis=-1, keepdims=True)
+        - normal * jnp.mean(grad * normal, axis=-1, keepdims=True)
+    )
+
+
+def middle(count, heads, summed, skip_out, query_weight, out_weight, up_weight, down_piece, skip_piece, text_kv, text,
+           cotangent, gains, tables):
     share, width = summed.shape
+    tokens = skip_out.shape[0]
     local = query_weight.shape[-1]
+    units = up_weight.shape[1]
+    words, text_width = text.shape
+    rows, span = skip_piece.shape
     scale = HD ** (-0.5)
-    rows, span = skip_piece.shape
-
-    def kernel(sum_ref, skip_ref, hbm_q, hbm_o, piece, kv, gain, dtab, utab, first_out, second_out, in_out,
-               mlp_out, q_out, inv_out, log_out, low_out, uo_out, skip_half, wq, wo, b_ref, ao, wsem, zsend, zrecv):
+    two = count // 2
+    wide = two * share
+
+    def kernel(sum_ref, skip_hbm, q_hbm, o_hbm, u_hbm, d_own, piece, kv, text_hbm, cot_hbm, gain, dtab, utab,
+               g_first, block_sum, ga_q, gb_q, ga_k, gb_k, ga_v, gb_v, ga_o, gb_o, g_ua, g_ub, g_da, g_db, skip_all,
+               wq, wo, wu, wd, cot, t_ref, first_ref, second_ref, x_ref, q_ref, inv_ref, log_ref, low_ref, acc, b_ref, ao,
+               bk, bv, ub, da, slots, skip_half, active, grads, u_all, ud_all, gu_all, gd_all, partial_g, left_g, right_g,
+               sr_g, sl_g, partial_b, left_b, right_b, sr_b, sl_b, lsem, wsend, wrecv, zsend, zrecv, *sems):
         me = lax.axis_index("tensor")
         core = lax.axis_index("ctx")
+        dp = lax.axis_index("dp")
+        always = core >= 0
+        half = pl.ds(pl.multiple_of(core * (rows // 2), 16), rows // 2)
+        down_rows = d_own.shape[0]
+        down_half = pl.ds(pl.multiple_of(core * (down_rows // 2), 16), down_rows // 2)
+        mine = pl.ds(pl.multiple_of(dp * down_rows, 16), down_rows)
         loads = [
-            pltpu.make_async_copy(source, target, wsem.at[number])
-            for number, (source, target) in enumerate(((hbm_q, wq), (hbm_o, wo)))
+            pltpu.make_async_copy(source, target, lsem.at[number])
+            for number, (source, target) in enumerate(
+                ((skip_hbm.at[rows_of(me, share), :], first_ref), (piece.at[half, :], skip_half.at[me]), (q_hbm, wq),
+                 (o_hbm, wo), (d_own, wd.at[mine, :]), (cot_hbm, cot), (u_hbm, wu), (text_hbm, t_ref))
+            )
         ]
         for load in loads:
             load.start()
-        half = pl.ds(pl.multiple_of(core * (rows // 2), 16), rows // 2)
-        own = pltpu.make_async_copy(piece.at[half, :], skip_half.at[me], wsem.at[2])
-        own.start()
+        gather_line = Line(me, count, *sems[:4])
+        grad_line = Line(me, count, *sems[4:8])
+        block_line = Line(me, count, *sems[8:])
+        down = Shared(wd, down_rows, (wsend, wrecv, 0))
+        skip = Shared(skip_all, rows, (wsend, wrecv, 1), stacked=True)
         z_peers = [{"tensor": xor_place(me, number)} for number in range(1, count)]
-        greet([(core >= 0, device) for device in z_peers])
-        sends = [
+        others = [{"dp": xor_place(dp, 1)}, {"dp": xor_place(dp, 2)}, {"ctx": 1 - core}]
+        greet([(always, device) for device in z_peers + others])
+        down.send_own(d_own.at[down_half, :])
+        z_sends = [
             push(piece.at[half, :], skip_half.at[me], zsend.at[number], zrecv.at[number], device)
             for number, device in enumerate(z_peers)
         ]
-        for send in sends:
+        for send in z_sends:
             send.start()
         take_stack(b_ref, utab, OUT_AT[6], count)
         take_stack(ao, dtab, IN_AT[9], count)
-        first = skip_ref[rows_of(me, share), :] + sum_ref[...]
-        first_out[...] = first
+        take_stack(bk, utab, OUT_AT[7], count)
+        take_stack(bv, utab, OUT_AT[8], count)
+        take_local(ub, utab, OUT_AT[10], me, count)
+        take_local(da, dtab, IN_AT[11], me, count)
+
+        loads[0].wait()
+        first = first_ref[...] + sum_ref[...]
+        first_ref[...] = first
+        second_ref[...] = first
         normal, _ = stats(first)
         x = (normal * gain[1:2, :]).astype(BF)
-        in_out[...] = x
+        x_ref[...] = x
         u = dot_nt(x, down_of(dtab, 6)).astype(BF)
-        second_out[...] = first
-        for load in loads:
-            load.wait()
-
-        def chunk(place, u_low):
-            y = dot_nn(x, wq[place]) + dot_nn(u, b_ref[place])
-            outs = []
+        loads[2].wait()
+        loads[3].wait()
+
+        def cross(place, u_low):
+            y = dot_nn(x_ref[...], wq[place]) + dot_nn(u, b_ref[place])
+            outs, inverses, logs = [], [], []
             for head in range(heads):
-                normal, inverse = stats(y[:, head * HD : (head + 1) * HD])
+                at = slice(head * HD, (head + 1) * HD)
+                normal, inverse = stats(y[:, at])
                 q = normal.astype(BF)
-                q_out[place, head] = q
-                inv_out[place, head] = inverse
-                s = dot_nt(q, kv[0, place, head, :, :HD]) * scale
+                q_ref[place, head] = q
+                inverses.append(inverse)
+                s = dot_nt(q, kv[0, place, :, at]) * scale
                 top = jnp.max(s, axis=-1, keepdims=True)
                 e = jnp.exp(s - top)
                 total = jnp.sum(e, axis=-1, keepdims=True)
                 p = (e * (1.0 / total)).astype(BF)
-                outs.append(dot_nn(p, kv[1, place, head, :, :HD]))
-                log_out[place, head] = top + jnp.log(total)
+                outs.append(dot_nn(p, kv[1, place, :, at]))
+                logs.append(top + jnp.log(total))
+            inv_ref[place] = jnp.concatenate(inverses, axis=1)
+            log_ref[place] = jnp.concatenate(logs, axis=1)
             low = jnp.concatenate(outs, axis=1).astype(BF)
-            low_out[place] = low
-            second_out[...] += dot_nt(low, wo[place])
+            low_ref[place] = low
+            second_ref[...] += dot_nt(low, wo[place])
             return u_low + dot_nt(low, ao[place])
 
-        u_low = lax.fori_loop(0, count, chunk, jnp.zeros((share, RANK), F32)).astype(BF)
-        uo_out[...] = u_low
-        second = second_out[...] + dot_nn(u_low, up_of(utab, 9))
-        second_out[...] = second
+        u_low = lax.fori_loop(0, count, cross, jnp.zeros((share, RANK), F32)).astype(BF)
+        second = second_ref[...] + dot_nn(u_low, up_of(utab, 9))
+        second_ref[...] = second
         normal, _ = stats(second)
-        mlp_out[...] = (normal * gain[2:3, :]).astype(BF)
-        own.wait()
+        slots[me] = (normal * gain[2:3, :]).astype(BF)
+
+        line_gather_step(gather_line, 0, slots)
+        down.wait(0)
+        down.forward()
+        down.swap(0)
+        down.wait(1)
+        down.swap(1)
+        loads[1].wait()
         for number in range(count - 1):
             arrived = skip_half.at[xor_place(me, number + 1)]
             push(arrived, arrived, zsend.at[number], zrecv.at[number], z_peers[number]).wait_recv()
-        for send in sends:
-            send.wait_send()
-
-    return call(
-        kernel,
-        [(summed, True), (skip_out, True), (query_weight, False), (out_weight, False), (skip_piece, False)]
-        + [(array, True) for array in (text_kv, gains, *tables)],
-        [
-            ((share, width), F32, True),
-            ((share, width), F32, True),
-            ((share, width), BF, True),
-            ((share, width), BF, True),
-            ((count, heads, share, HD), BF, True),
-            ((count, heads, share, 1), F32, True),
-            ((count, heads, share, 1), F32, True),
-            ((count, share, local), BF, True),
-            ((share, RANK), BF, True),
-            ((count, rows // 2, span), BF, False),
-        ],
-        [vmem(count, width, local), vmem(count, width, local), vmem(count, RANK, local), vmem(count, RANK, local),
-         dma(3), dma(count), dma(count)],
-        collective=6,
-        cost=cost_of(4 * share * width * width, 20e6),
-    )
-
-
-def feed_forward(count, block_in, cotangent, second, up_weight, down_weight, skip_half, tables):
-    share, width = block_in.shape
-    tokens = cotangent.shape[0]
-    hidden_units = up_weight.shape[1]
-    rows = 2 * skip_half.shape[1]
-    span = skip_half.shape[2]
-
-    def kernel(x_ref, cot, sec, hbm_u, hbm_d, shalf, dtab, utab, summed, down_out, g_ua, g_ub, g_da, g_db, skip_all,
-               slots, wu, wd, ub, da, partial_ref, from_left, from_right, stage_right, stage_left, wsem, wsend, wrecv, *sems):
-        me = lax.axis_index("tensor")
-        core = lax.axis_index("ctx")
-        dp = lax.axis_index("dp")
-        gather_line = Line(me, count, *sems[:4])
-        scatter_line = Line(me, count, *sems[4:])
-        loads = [
-            pltpu.make_async_copy(source, target, wsem.at[number])
-            for number, (source, target) in enumerate(((hbm_u, wu), (hbm_d, wd)))
-        ]
-        for load in loads:
-            load.start()
-        skip = Shared(skip_all, rows, (wsend, wrecv, 0), stacked=True)
-        own = pltpu.make_async_copy(shalf, skip.view(dp, core), wsem.at[2])
-        own.start()
-        slots[me] = x_ref[...]
-        for ref in (g_ua, g_ub, g_da, g_db):
-            ref[...] = jnp.zeros_like(ref)
-        peers = [{"dp": xor_place(dp, 1)}, {"dp": xor_place(dp, 2)}, {"ctx": 1 - core}]
-        greet(line_partners(me, count) + [(core >= 0, device) for device in peers])
-        line_gather_step(gather_line, 0, slots)
-        skip.send_own(shalf)
-        take_local(ub, utab, OUT_AT[10], me, count)
-        take_local(da, dtab, IN_AT[11], me, count)
-        for load in loads:
-            load.wait()
-
-        def compute(block):
-            rows = rows_of(block, share)
-            x = slots[block]
-            ct = cot[rows, :]
-            ua, db = down_of(dtab, 10), up_of(utab, 11)
+        skip_place = pltpu.make_async_copy(skip_half, skip.view(dp, core), lsem.at[8])
+        skip_place.start()
+        skip.send_own(skip_half)
+        line_gather_step(gather_line, 1, slots)
+        down.wait(2)
+        down.swap(2)
+        loads[4].wait()
+        loads[5].wait()
+        loads[6].wait()
+        ua, db = down_of(dtab, 10), up_of(utab, 11)
+        down.wait_swaps()
+        line_gather_step(gather_line, 2, slots)
+
+        def part(number):
+            return pl.ds(pl.multiple_of(number * wide, wide), wide)
+
+        def first_grads(number, carry):
+            ct = cot[part(number), :]
+            gd = dot_nt(ct, db).astype(BF)
+            gd_all[part(number), :] = gd
+            grads[part(number), :] = (dot_nn(ct, wd[...]) + dot_nn(gd, da[...])).astype(BF)
+            return carry
+
+        lax.fori_loop(0, 2, first_grads, 0)
+        line_gather_step(gather_line, 3, slots)
+        lead = jnp.where(2 * me < count, 1, 0)
+
+        def forward_half(turn, carry):
+            number = jnp.where(turn == 0, lead, 1 - lead)
+            here = part(number)
+            x = slots[pl.ds(number * two, two)].reshape(wide, width)
             u = dot_nt(x, ua).astype(BF)
+            u_all[here, :] = u
             up = dot_nn(x, wu[...]) + dot_nn(u, ub[...])
             square = up * up
             curve = jnp.tanh(0.7978845608028654 * (up + 0.044715 * square * up))
-            half = 0.5 * (1.0 + curve)
-            active = (up * half).astype(BF)
-            slope = half + 0.5 * up * (1.0 - curve * curve) * (0.7978845608028654 * (1.0 + 0.134145 * square))
-            ud = dot_nt(active, da[...]).astype(BF)
-            down = dot_nt(active, wd[...]) + dot_nn(ud, db)
-            down_out[rows, :] = down.astype(BF)
-
-            @pl.when(block == me)
-            def _():
-                down_out[rows, :] = (down + sec[...]).astype(BF)
-
-            gd = dot_nt(ct, db).astype(BF)
-            g_active = dot_nn(ct, wd[...]) + dot_nn(gd, da[...])
-            g_up = (g_active * slope).astype(BF)
+            flat = 0.5 * (1.0 + curve)
+            active[here, :] = (up * flat).astype(BF)
+            slope = flat + 0.5 * up * (1.0 - curve * curve) * (0.7978845608028654 * (1.0 + 0.134145 * square))
+            g_up = (grads[here, :].astype(F32) * slope).astype(BF)
+            grads[here, :] = g_up
             gu = dot_nt(g_up, ub[...]).astype(BF)
-            partial_ref[block] = (dot_nt(g_up, wu[...]) + dot_nn(gu, ua)).astype(BF)
-            g_ub[...] += dot_tn(u, g_up)
-            g_ua[...] += dot_tn(gu, x)
-            g_db[...] += dot_tn(ud, ct)
-            g_da[...] += dot_tn(gd, active)
-
-        def step(number, carry):
-            @pl.when(number > 0)
-            def _():
-                line_gather_step(gather_line, number, slots)
-
-            def side(which, inner):
-                block = me + (2 * which - 1) * number
-
-                @pl.when((block >= 0) & (block < count) & ((number > 0) | (which == 0)))
-                def _():
-                    compute(lax.clamp(0, block, count - 1))
-
-                return inner
-
-            return lax.fori_loop(0, 2, side, carry)
-
-        lax.fori_loop(0, count, step, 0)
-        own.wait()
+            gu_all[here, :] = gu
+            g_x = (dot_nt(g_up, wu[...]) + dot_nn(gu, ua)).astype(BF)
+            partial_g[pl.ds(number * two, two)] = g_x.reshape(two, share, width)
+            line_scatter_step(grad_line, turn, partial_g, left_g, right_g, sr_g, sl_g)
+            return carry
+
+        lax.fori_loop(0, 2, forward_half, 0)
         skip.wait(0)
         skip.forward()
+        skip.wait(1)
+
+        def down_half_product(turn, carry):
+            number = jnp.where(turn == 0, lead, 1 - lead)
+            here = part(number)
+            act = active[here, :]
+            ud = dot_nt(act, da[...]).astype(BF)
+            ud_all[here, :] = ud
+            y = dot_nt(act, wd[...]) + dot_nn(ud, db)
+            for piece_of in range(two):
+                block = number * two + piece_of
+                own = jnp.where(block == me, 1.0, 0.0)
+                one = y[piece_of * share : (piece_of + 1) * share] + second_ref[...] * own
+                partial_b[block] = one.astype(BF)
+
+            @pl.when(turn == 0)
+            def _():
+                line_scatter_step(grad_line, 2, partial_g, left_g, right_g, sr_g, sl_g)
+
+            return carry
+
+        lax.fori_loop(0, 2, down_half_product, 0)
+        skip_place.wait()
         skip.swap(0)
+        skip.swap(1)
         skip.swap(3)
-
-        def scatter(number, carry):
-            line_scatter_step(scatter_line, number, partial_ref, from_left, from_right, stage_right, stage_left)
-            return carry
-
-        lax.fori_loop(0, count - 1, scatter, 0)
-        skip.wait(1)
-        skip.swap(1)
+        line_scatter_step(block_line, 0, partial_b, left_b, right_b, sr_b, sl_b)
+        g_ub[...] = dot_tn(u_all[...], grads[...])
+        g_ua[...] = dot_tn(gu_all[...], slots[...].reshape(tokens, width))
+        g_db[...] = dot_tn(ud_all[...], cot[...])
+        g_da[...] = dot_tn(gd_all[...], active[...])
+        loads[7].wait()
+        uq = dot_nt(x_ref[...], down_of(dtab, 6)).astype(BF)
+        words_in = t_ref[...]
+        uk = dot_nt(words_in, down_of(dtab, 7)).astype(BF)
+        uv = dot_nt(words_in, down_of(dtab, 8)).astype(BF)
         line_gather_drain(gather_line, slots)
-        line_scatter_finish(scatter_line, partial_ref, from_left, from_right, stage_right, stage_left, summed)
+        line_scatter_finish(grad_line, partial_g, left_g, right_g, sr_g, sl_g, acc)
         skip.wait(2)
         skip.swap(2)
+
+        normal, inverse = stats(second_ref[...])
+        g_second = cot[rows_of(me, share), :].astype(F32) + norm_backward(normal, inverse, acc[...] * gain[2:3, :])
+        second_ref[...] = g_second
+        g_low = g_second.astype(BF)
+        slots[me] = g_low
+        go = dot_nt(g_low, up_of(utab, 9)).astype(BF)
+        gb_o[...] = dot_tn(u_low, g_low)
+        acc[...] = jnp.zeros_like(acc)
+
+        def cross_grads(place, carry):
+            gq_sum, gk_sum, gv_sum = carry
+
+            @pl.when((place > 0) & (place < count - 1))
+            def _():
+                line_scatter_step(block_line, place, partial_b, left_b, right_b, sr_b, sl_b)
+
+            g_attn = (dot_nn(slots[me], wo[place]) + dot_nn(go, ao[place])).astype(BF)
+            ga_o[place] = dot_tn(go, low_ref[place])
+            gq_parts, gk_parts, gv_parts = [], [], []
+            for head in range(heads):
+                at = slice(head * HD, (head + 1) * HD)
+                gh = g_attn[:, at]
+                q = q_ref[place, head]
+                k = kv[0, place, :, at]
+                v = kv[1, place, :, at]
+                p = jnp.exp(dot_nt(q, k) * scale - log_ref[place, :, head : head + 1])
+                dp_ = dot_nt(gh, v)
+                inner = jnp.sum(p * dp_, axis=-1, keepdims=True)
+                ds = (p * (dp_ - inner)).astype(BF)
+                dq = dot_nn(ds, k) * scale
+                dk = dot_tn(ds, q) * scale
+                gq_parts.append(norm_backward(q.astype(F32), inv_ref[place, :, head : head + 1], dq))
+                side = kv[0, place, :, local + 2 * head : local + 2 * head + 2].astype(F32)
+                gk_parts.append(norm_backward(k.astype(F32), side[:, 0:1] + side[:, 1:2], dk))
+                gv_parts.append(dot_tn(p.astype(BF), gh))
+            gq = jnp.concatenate(gq_parts, axis=1).astype(BF)
+            gk = jnp.concatenate(gk_parts, axis=1).astype(BF)
+            gv = jnp.concatenate(gv_parts, axis=1).astype(BF)
+            acc[...] += dot_nt(gq, wq[place])
+            gb_q[place] = dot_tn(uq, gq)
+            gb_k[place] = dot_tn(uk, gk)
+            gb_v[place] = dot_tn(uv, gv)
+            return (
+                gq_sum + dot_nt(gq, b_ref[place]),
+                gk_sum + dot_nt(gk, bk[place]),
+                gv_sum + dot_nt(gv, bv[place]),
+            )
+
+        start = (jnp.zeros((share, RANK), F32), jnp.zeros((words, RANK), F32), jnp.zeros((words, RANK), F32))
+        gq_sum, gk_sum, gv_sum = lax.fori_loop(0, count, cross_grads, start)
+        gq_sum = gq_sum.astype(BF)
+        ga_q[...] = dot_tn(gq_sum, x_ref[...])
+        ga_k[...] = dot_tn(gk_sum.astype(BF), words_in)
+        ga_v[...] = dot_tn(gv_sum.astype(BF), words_in)
+        g_x = acc[...] + dot_nn(gq_sum, down_of(dtab, 6))
+        normal, inverse = stats(first_ref[...])
+        g_first[...] = (second_ref[...] + norm_backward(normal, inverse, g_x * gain[1:2, :])).astype(BF)
+        line_scatter_finish(block_line, partial_b, left_b, right_b, sr_b, sl_b, acc)
+        block_sum[...] = acc[...].astype(BF)
         skip.wait_swaps()
         skip.drain()
+        down.drain()
+        for send in z_sends:
+            send.wait_send()
 
     buffers = [vmem(count, share, width) for _ in range(5)]
     return call(
         kernel,
-        [(block_in, True), (cotangent, True), (second, True), (up_weight, False), (down_weight, False), (skip_half, False)]
-        + [(array, True) for array in tables],
+        [(summed, True)]
+        + [(array, False) for array in (skip_out, query_weight, out_weight, up_weight, down_piece, skip_piece)]
+        + [(text_kv, True), (text, False), (cotangent, False)]
+        + [(array, True) for array in (gains, *tables)],
         [
-            ((share, width), F32, True),
-            ((tokens, width), BF, True),
+            ((share, width), BF, True),
+            ((share, width), BF, True),
             ((RANK, width), F32, True),
-            ((RANK, hidden_units), F32, True),
-            ((RANK, hidden_units), F32, True),
+            ((count, RANK, local), F32, True),
+            ((RANK, text_width), F32, True),
+            ((count, RANK, local), F32, True),
+            ((RANK, text_width), F32, True),
+            ((count, RANK, local), F32, True),
+            ((count, RANK, local), F32, True),
+            ((RANK, width), F32, True),
+            ((RANK, width), F32, True),
+            ((RANK, units), F32, True),
+            ((RANK, units), F32, True),
             ((RANK, width), F32, True),
             ((count, 4 * rows, span), BF, False),
         ],
-        [vmem(count, share, width), vmem(width, hidden_units), vmem(width, hidden_units), vmem(RANK, hidden_units),
-         vmem(RANK, hidden_units)]
-        + buffers + [dma(3), dma(1, 7), dma(1, 7)] + [dma(count) for _ in range(8)],
+        [vmem(count, width, local), vmem(count, width, local), vmem(width, units), vmem(width, units),
+         vmem(tokens, width), vmem(words, text_width), vmem(share, width, dtype=F32), vmem(share, width, dtype=F32),
+         vmem(share, width), vmem(count, heads, share, HD), vmem(count, share, heads, dtype=F32),
+         vmem(count, share, heads, dtype=F32), vmem(count, share, local), vmem(share, width, dtype=F32)]
+        + [vmem(count, RANK, local) for _ in range(4)] + [vmem(RANK, units) for _ in range(2)]
+        + [vmem(count, share, width), vmem(count, rows // 2, span), vmem(tokens, units), vmem(tokens, units)]
+        + [vmem(tokens, RANK) for _ in range(4)] + buffers + buffers
+        + [dma(9), dma(2, 7), dma(2, 7), dma(count), dma(count)] + [dma(count) for _ in range(12)],
         collective=3,
-        cost=cost_of(8 * tokens * width * hidden_units, 60e6),
+        cost=cost_of(12 * tokens * width * units, 60e6),
     )
 
 
@@ -1263,11 +1356,11 @@
     text_rows = weights["ck"].shape[1]
     mod_rows = mod_weight.shape[0]
 
-    def kernel(skip_own, q_own, k_own, v_own, o_own, ck_own, cv_own, cq_own, co_own, up_own, dn_own,
+    def kernel(skip_own, q_own, k_own, v_own, o_own, ck_own, cv_own, cq_own, co_own, up_own,
                index_ref, cond, hid, lsk, t_ref, wm, halves, gain, dtab, utab,
-               skip_out, attn_in, q_out, keys, values, low_out, log_out, inv_q, inv_k, summed, act_all, text_kv,
-               wq, wk, wv, wo, wcq, wco, wup, wdn,
-               wskip, wtext, part_x, pgain, sa, tk, tv, qa, qb, kb, vb, oa, mod_in, mod_slice, mod_out, partial_a, left_a, right_a, sr_a, sl_a,
+               skip_hbm, attn_hbm, q_out, keys, values, low_out, log_out, inv_q, inv_k, summed, act_all, text_kv,
+               wq_hbm, wk_hbm, wv_hbm, wo_hbm, wcq, wco, wup,
+               skip_out, attn_in, wq, wk, wv, wo, out_sem, shift_row, wskip, wtext, part_x, pgain, sa, tk, tv, qa, qb, kb, vb, oa, mod_in, mod_slice, mod_out, partial_a, left_a, right_a, sr_a, sl_a,
                partial_b, left_b, right_b, sr_b, sl_b, wsend, wrecv, local_sem, zsend, zrecv, msend, mrecv, tsend, trecv,
                xsend, xrecv, *sems):
         me = lax.axis_index("tensor")
@@ -1278,7 +1371,8 @@
         dp_peers = [{"dp": xor_place(dp, number)} for number in (1, 2, 3)]
         z_peers = [{"tensor": xor_place(me, number)} for number in range(1, count)]
         reduce_line = Line(me, count, *sems[:4])
-        scatter_line = Line(me, count, *sems[4:])
+        scatter_line = Line(me, count, *sems[4:8])
+        text_line = Line(me, count, *sems[8:])
 
         def sems_of(number):
             return (wsend, wrecv, number)
@@ -1290,16 +1384,23 @@
         }
         words_w = Shared(wtext, text_rows, sems_of(5), split=False, columns=True)
         cross = [Shared(wcq, rows, sems_of(6), stacked=True), Shared(wco, rows, sems_of(7), stacked=True)]
-        wide = [Shared(wup, rows, sems_of(8)), Shared(wdn, rows, sems_of(9))]
+        wide = [Shared(wup, rows, sems_of(8))]
         owns = {"q": q_own, "k": k_own, "v": v_own, "o": o_own}
         half = pl.ds(pl.multiple_of(core * (rows // 2), 16), rows // 2)
         mine = pl.ds(pl.multiple_of(dp * rows, 16), rows)
         my_half = pl.ds(pl.multiple_of(dp * rows + core * (rows // 2), 16), rows // 2)
 
+        for place in range(count):
+            @pl.when(me == place)
+            def _(place=place):
+                side = place * span // width
+                start = place * span % width
+                pgain[...] = halves[side : side + 1, start : start + span]
+
         places = [
             pltpu.make_async_copy(source, target.at[mine, :], local_sem.at[number])
             for number, (source, target) in enumerate(
-                ((skip_own, wskip), (q_own, wq), (k_own, wk), (v_own, wv), (o_own, wo), (up_own, wup), (dn_own, wdn))
+                ((skip_own, wskip), (q_own, wq), (k_own, wk), (v_own, wv), (o_own, wo), (up_own, wup))
             )
         ]
         for place in places:
@@ -1346,12 +1447,6 @@
         ]
         for copy in spread:
             copy.start()
-        for place in range(count):
-            @pl.when(me == place)
-            def _(place=place):
-                side = place * span // width
-                start = place * span % width
-                pgain[...] = halves[side : side + 1, start : start + span]
         take_local(sa, dtab, 0, me, count)
         take_local(tk, utab, OUT_AT[7], me, count)
         take_local(tv, utab, OUT_AT[8], me, count)
@@ -1374,6 +1469,9 @@
 
         skip.swap(0)
 
+        skip.wait(1)
+        skip.swap(1)
+
         for number in (1, 2, 3):
             source = act_all.at[xor_place(dp, number)]
             push(source, source, msend.at[0, number - 1], mrecv.at[0, number - 1], dp_peers[number - 1]).wait_recv()
@@ -1384,6 +1482,8 @@
                 for sequence in range(4):
                     mod_slice[sequence : sequence + 1, :] = act_all[sequence, :, span_of]
 
+        skip.wait(2)
+        skip.swap(2)
         products = dot_nn(mod_slice[...].astype(BF), wm[...])
         for sequence in range(4):
             mod_out[sequence] = products[sequence : sequence + 1]
@@ -1394,17 +1494,7 @@
         ]
         for copy in backs:
             copy.start()
-        skip.wait(1)
-        skip.swap(1)
         mod_in[dp] = mod_out[dp]
-        mod_u = dot_nt(act_low, down_of(dtab, 1)).astype(BF)
-        mod_low = dot_nn(mod_u, up_of(utab, 1))
-        for number in (1, 2, 3):
-            target = mod_in.at[xor_place(dp, number)]
-            push(target, target, msend.at[1, number - 1], mrecv.at[1, number - 1], dp_peers[number - 1]).wait_recv()
-        shift = mod_in[0] + mod_in[1] + mod_in[2] + mod_in[3] + mod_low
-        skip.wait(2)
-        skip.swap(2)
         places[0].wait()
         skip.wait_swaps()
 
@@ -1430,29 +1520,64 @@
                 for piece in range(each):
                     partial_a[number + piece] = y[piece * chunk : (piece + 1) * chunk]
 
+        def text_product():
+            @pl.when(core == 0)
+            def _():
+                text_place(ck_own).wait()
+
+            @pl.when(core == 1)
+            def _():
+                text_place(cv_own).wait()
+
+            x = t_ref[...]
+            y = dot_nt(x, wtext[...])
+
+            @pl.when(core == 0)
+            def _():
+                z = y + dot_nn(dot_nt(x, down_of(dtab, 7)).astype(BF), tk[...])
+                parts, sides = [], []
+                for head in range(heads):
+                    normal, inverse = stats(z[:, head * HD : (head + 1) * HD])
+                    upper = inverse.astype(BF)
+                    parts.append(normal.astype(BF))
+                    sides += [upper, (inverse - upper.astype(F32)).astype(BF)]
+                text_kv[0, me, :, :local] = jnp.concatenate(parts, axis=1)
+                text_kv[0, me, :, local : local + 2 * heads] = jnp.concatenate(sides, axis=1)
+
+            @pl.when(core == 1)
+            def _():
+                z = y + dot_nn(dot_nt(x, down_of(dtab, 8)).astype(BF), tv[...])
+                text_kv[1, me, :, :local] = z.astype(BF)
+
+        text_slots = text_kv.at[core]
+
         def finish(slot, total):
             here = rows_of(slot, chunk)
             skip_out[here, :] = total
             normal, _ = stats(total)
-            attn_in[here, :] = (normal * gain[0:1, :] + shift).astype(BF)
+            attn_in[here, :] = (normal * gain[0:1, :] + shift_row[...]).astype(BF)
 
         def beside(number):
+            @pl.when(number == 1)
+            def _():
+                for other in (1, 2, 3):
+                    target = mod_in.at[xor_place(dp, other)]
+                    push(target, target, msend.at[1, other - 1], mrecv.at[1, other - 1], dp_peers[other - 1]).wait_recv()
+                mod_u = dot_nt(act_low, down_of(dtab, 1)).astype(BF)
+                shift_row[...] = mod_in[0] + mod_in[1] + mod_in[2] + mod_in[3] + dot_nn(mod_u, up_of(utab, 1))
+
             @pl.when(number == 3)
             def _():
                 for weight in (*shared.values(), words_w):
                     weight.wait(0)
                     weight.forward()
-                for weight in shared.values():
-                    weight.swap(0)
-
-            @pl.when(number == 4)
-            def _():
                 for weight in (*shared.values(), words_w):
                     weight.wait(1)
                 for weight in shared.values():
+                    weight.swap(0)
                     weight.swap(1)
 
-            @pl.when(number == 6)
+            @pl.when(number == 4)
             def _():
                 for place in crossing:
                     place.wait()
@@ -1470,46 +1595,25 @@
                 for weight in shared.values():
                     weight.swap(2)
 
+            @pl.when(number == 8)
+            def _():
+                text_product()
+                line_gather_step(text_line, 0, text_slots)
+
         line_reduce_all(reduce_line, steps, compute, partial_a, left_a, right_a, sr_a, sl_a, finish, beside)
-
-        @pl.when(core == 0)
-        def _():
-            text_place(ck_own).wait()
-
-        @pl.when(core == 1)
-        def _():
-            text_place(cv_own).wait()
-
-        x = t_ref[...]
-        y = dot_nt(x, wtext[...])
-
-        @pl.when(core == 0)
-        def _():
-            z = y + dot_nn(dot_nt(x, down_of(dtab, 7)).astype(BF), tk[...])
-            for head in range(heads):
-                normal, inverse = stats(z[:, head * HD : (head + 1) * HD])
-                upper = inverse.astype(BF)
-                lower = (inverse - upper.astype(F32)).astype(BF)
-                text_kv[0, me, head] = jnp.concatenate([normal.astype(BF), upper, lower], axis=1)
-
-        @pl.when(core == 1)
-        def _():
-            z = (y + dot_nn(dot_nt(x, down_of(dtab, 8)).astype(BF), tv[...])).astype(BF)
-            filler = jnp.zeros((words, 2), BF)
-            for head in range(heads):
-                text_kv[1, me, head] = jnp.concatenate([z[:, head * HD : (head + 1) * HD], filler], axis=1)
-
-        texts = [
-            push(text_kv.at[core, me], text_kv.at[core, me], tsend.at[number], trecv.at[number], z_peers[number])
-            for number in range(count - 1)
-        ]
-        for copy in texts:
-            copy.start()
 
         for number in range(1, 5):
             places[number].wait()
         for weight in shared.values():
             weight.wait_swaps()
+        stores = [
+            pltpu.make_async_copy(source, target, out_sem.at[number])
+            for number, (source, target) in enumerate(
+                ((skip_out, skip_hbm), (attn_in, attn_hbm), (wq, wq_hbm), (wk, wk_hbm), (wv, wv_hbm), (wo, wo_hbm))
+            )
+        ]
+        for store in stores:
+            store.start()
 
         def project(number, carry):
             here = rows_of(number, block)
@@ -1518,15 +1622,18 @@
             yq = dot_nn(x, wq[...]) + dot_nn(u[:, :RANK], qb[...])
             yk = dot_nn(x, wk[...]) + dot_nn(u[:, RANK : 2 * RANK], kb[...])
             yv = (dot_nn(x, wv[...]) + dot_nn(u[:, 2 * RANK :], vb[...])).astype(BF)
+            parts_q, parts_k = [], []
             for head in range(heads):
                 span_of = slice(head * HD, (head + 1) * HD)
                 normal, inverse = stats(yq[:, span_of])
                 q_out[head, here, :] = normal.astype(BF)
-                inv_q[head, here, :] = inverse
+                parts_q.append(inverse)
                 normal, inverse = stats(yk[:, span_of])
                 keys[core, head, here, :] = normal.astype(BF)
-                inv_k[head, here, :] = inverse
+                parts_k.append(inverse)
                 values[core, head, here, :] = yv[:, span_of]
+            inv_q[here, :] = jnp.concatenate(parts_q, axis=1)
+            inv_k[here, :] = jnp.concatenate(parts_k, axis=1)
             return carry
 
         lax.fori_loop(0, tokens // block, project, 0)
@@ -1536,20 +1643,21 @@
         ]
         for swap in swaps:
             swap.start()
+        line_gather_step(text_line, 1, text_slots)
         for weight in cross:
             weight.wait(0)
             weight.forward()
             weight.swap(0)
             weight.swap(3)
-        for weight, own in zip(wide, (up_own, dn_own)):
-            weight.send_own(own.at[half, :])
+        for weight in wide:
+            weight.send_own(up_own.at[half, :])
         for number, ref in enumerate((keys, values)):
             push(ref.at[1 - core], ref.at[1 - core], xsend.at[number], xrecv.at[number], peer).wait_recv()
 
         def attend(place, carry):
             dest = scatter_order(me, count, place)
             here = rows_of(dest, share)
-            outs = []
+            outs, logs = [], []
             for head in range(heads):
                 q = q_out[head, here, :]
                 s0 = dot_nt(q, keys[0, head]) * scale
@@ -1562,25 +1670,28 @@
                 p0 = (e0 * share_of).astype(BF)
                 p1 = (e1 * share_of).astype(BF)
                 outs.append(dot_nn(p0, values[0, head]) + dot_nn(p1, values[1, head]))
-                log_out[head, here, :] = top + jnp.log(total)
+                logs.append(top + jnp.log(total))
             low = jnp.concatenate(outs, axis=1).astype(BF)
             low_out[here, :] = low
+            log_out[here, :] = jnp.concatenate(logs, axis=1)
             u = dot_nt(low, oa[...]).astype(BF)
             partial_b[dest] = (dot_nt(low, wo[...]) + dot_nn(u, up_of(utab, 5))).astype(BF)
 
             @pl.when(place < count - 1)
             def _():
                 line_scatter_step(scatter_line, place, partial_b, left_b, right_b, sr_b, sl_b)
+
+            @pl.when(place == 0)
+            def _():
+                line_gather_step(text_line, 2, text_slots)
 
             @pl.when(place == 1)
             def _():
                 for weight in cross:
                     weight.wait(1)
                     weight.swap(1)
-                for number in range(count - 1):
-                    arrived = text_kv.at[core, xor_place(me, number + 1)]
-                    push(arrived, arrived, tsend.at[number], trecv.at[number], z_peers[number]).wait_recv()
-                push(text_kv.at[core], text_kv.at[core], tsend.at[count - 1], trecv.at[count - 1], peer).start()
+                line_gather_step(text_line, 3, text_slots)
+                push(text_slots, text_slots, tsend, trecv, peer).start()
 
             @pl.when(place == 2)
             def _():
@@ -1603,195 +1714,80 @@
             weight.wait(2)
             weight.swap(2)
         others = text_kv.at[1 - core]
-        push(others, others, tsend.at[count - 1], trecv.at[count - 1], peer).wait_recv()
+        push(others, others, tsend, trecv, peer).wait_recv()
         for weight in cross + wide:
             weight.wait_swaps()
         places[5].wait()
-        places[6].wait()
+        for store in stores:
+            store.wait()
         for weight in (skip, *shared.values(), words_w, *cross, *wide):
             weight.drain()
         for number in range(count - 1):
             for copy in z_copies(number):
                 copy.wait_send()
-        for copy in spread + backs + texts:
+        for copy in spread + backs:
             copy.wait_send()
-        push(text_kv.at[core], text_kv.at[core], tsend.at[count - 1], trecv.at[count - 1], peer).wait_send()
+        line_gather_drain(text_line, text_slots)
+        push(text_slots, text_slots, tsend, trecv, peer).wait_send()
         for swap in swaps:
             swap.wait_send()
 
-    names = ("skip", "q", "k", "v", "o", "ck", "cv", "cq", "co", "up", "dn")
+    names = ("skip", "q", "k", "v", "o", "ck", "cv", "cq", "co", "up")
     return call(
         kernel,
-        [(weights[name], False) for name in names] + [(index, None)]
+        [(weights[name], name in ("cq", "co", "up")) for name in names] + [(index, None)]
         + [(array, True) for array in (condition, hidden, long_skip, text, mod_weight, gain_halves, gain_rows, *tables)],
         [
-            ((tokens, width), F32, True),
-            ((tokens, width), BF, True),
+            ((tokens, width), F32, False),
+            ((tokens, width), BF, False),
             ((heads, tokens, HD), BF, True),
             ((2, heads, tokens, HD), BF, True),
             ((2, heads, tokens, HD), BF, True),
             ((tokens, local), BF, True),
-            ((heads, tokens, 1), F32, True),
-            ((heads, tokens, 1), F32, True),
-            ((heads, tokens, 1), F32, True),
+            ((tokens, heads), F32, True),
+            ((tokens, heads), F32, True),
+            ((tokens, heads), F32, True),
             ((share, width), F32, True),
             ((4, 1, width + 128), F32, True),
-            ((2, count, heads, words, HD + 2), BF, True),
+            ((2, count, words, local + 32), BF, True),
         ]
-        + [((width, local), BF, True) for _ in range(4)]
+        + [((width, local), BF, False) for _ in range(4)]
         + [((count, width, local), BF, False) for _ in range(2)]
-        + [((width, units), BF, False) for _ in range(2)],
-        [vmem(width, span), vmem(local, text_width), vmem(block, span, dtype=F32), vmem(1, span, dtype=F32),
+        + [((width, units), BF, False)],
+        [vmem(tokens, width, dtype=F32), vmem(tokens, width)] + [vmem(width, local) for _ in range(4)]
+        + [dma(6), vmem(1, width, dtype=F32), vmem(width, span), vmem(local, text_width), vmem(block, span, dtype=F32), vmem(1, span, dtype=F32),
          vmem(RANK, span), vmem(RANK, local), vmem(RANK, local), vmem(3 * RANK, width)]
         + [vmem(RANK, local) for _ in range(4)]
         + [vmem(4, 1, width, dtype=F32), vmem(4, mod_rows, dtype=F32),
          vmem(4, 1, width, dtype=F32)]
         + [vmem(steps, chunk, width) for _ in range(5)] + [vmem(count, share, width) for _ in range(5)]
-        + [dma(10, 7), dma(10, 7), dma(10), dma(2, count), dma(2, count), dma(2, 3), dma(2, 3), dma(count), dma(count),
+        + [dma(10, 7), dma(10, 7), dma(10), dma(2, count), dma(2, count), dma(2, 3), dma(2, 3), dma(), dma(),
            dma(2), dma(2)]
-        + [dma(steps) for _ in range(4)] + [dma(count) for _ in range(4)],
+        + [dma(steps) for _ in range(4)] + [dma(count) for _ in range(8)],
         collective=1,
         cost=cost_of(8 * tokens * width * local, 60e6),
     )
 
 
-def norm_backward(normal, inverse, grad):
-    return inverse * (
-        grad
-        - jnp.mean(grad, axis=-1, keepdims=True)
-        - normal * jnp.mean(grad * normal, axis=-1, keepdims=True)
-    )
-
-
-def cross_backward(count, heads, g_in, cotangent, first, second, block_in, query, inverses, logs, low, u_low, text,
-                   query_weight, out_weight, text_kv, gains, tables):
-    share, width = g_in.shape
-    local = query_weight.shape[-1]
-    words, text_width = text.shape
+def attention_backward(count, heads, g_first, block_sum, query, keys, values, low, logs, inv_q, inv_k, out_weight, tables):
+    share, width = g_first.shape
+    tokens = query.shape[1]
+    local = low.shape[1]
     scale = HD ** (-0.5)
 
-    def kernel(g_ref, cot, first_ref, second_ref, x_ref, q_ref, inv_ref, log_ref, low_ref, uo_ref, t_ref, hbm_q, hbm_o,
-               kv, gain, dtab, utab, g_first, ga_q, gb_q, ga_k, gb_k, ga_v, gb_v, ga_o, gb_o,
-               acc, wq, wo, b_ref, ao, bk, bv, wsem):
-        me = lax.axis_index("tensor")
-        loads = [
-            pltpu.make_async_copy(source, target, wsem.at[number])
-            for number, (source, target) in enumerate(((hbm_q, wq), (hbm_o, wo)))
-        ]
-        for load in loads:
-            load.start()
-        normal, inverse = stats(second_ref[...])
-        g_second = cot[rows_of(me, share), :].astype(F32) + norm_backward(normal, inverse, g_ref[...] * gain[2:3, :])
-        g_low = g_second.astype(BF)
-        take_stack(b_ref, utab, OUT_AT[6], count)
-        take_stack(ao, dtab, IN_AT[9], count)
-        take_stack(bk, utab, OUT_AT[7], count)
-        take_stack(bv, utab, OUT_AT[8], count)
-        go = dot_nt(g_low, up_of(utab, 9)).astype(BF)
-        gb_o[...] = dot_tn(uo_ref[...], g_low)
-        x = x_ref[...]
-        uq = dot_nt(x, down_of(dtab, 6)).astype(BF)
-        words_in = t_ref[...]
-        uk = dot_nt(words_in, down_of(dtab, 7)).astype(BF)
-        uv = dot_nt(words_in, down_of(dtab, 8)).astype(BF)
-        acc[...] = jnp.zeros_like(acc)
-        for load in loads:
-            load.wait()
-
-        def chunk(place, carry):
-            gq_sum, gk_sum, gv_sum = carry
-            g_attn = (dot_nn(g_low, wo[place]) + dot_nn(go, ao[place])).astype(BF)
-            ga_o[place] = dot_tn(go, low_ref[place])
-            gq_parts, gk_parts, gv_parts = [], [], []
-            for head in range(heads):
-                gh = g_attn[:, head * HD : (head + 1) * HD]
-                q = q_ref[place, head]
-                kfull = kv[0, place, head]
-                k = kfull[:, :HD]
-                v = kv[1, place, head, :, :HD]
-                p = jnp.exp(dot_nt(q, k) * scale - log_ref[place, head])
-                dp = dot_nt(gh, v)
-                inner = jnp.sum(p * dp, axis=-1, keepdims=True)
-                ds = (p * (dp - inner)).astype(BF)
-                dq = dot_nn(ds, k) * scale
-                dk = dot_tn(ds, q) * scale
-                dv = dot_tn(p.astype(BF), gh)
-                gq_parts.append(norm_backward(q.astype(F32), inv_ref[place, head], dq))
-                inv_k = kfull[:, HD : HD + 1].astype(F32) + kfull[:, HD + 1 : HD + 2].astype(F32)
-                gk_parts.append(norm_backward(k.astype(F32), inv_k, dk))
-                gv_parts.append(dv)
-            gq = jnp.concatenate(gq_parts, axis=1).astype(BF)
-            gk = jnp.concatenate(gk_parts, axis=1).astype(BF)
-            gv = jnp.concatenate(gv_parts, axis=1).astype(BF)
-            acc[...] += dot_nt(gq, wq[place])
-            gb_q[place] = dot_tn(uq, gq)
-            gb_k[place] = dot_tn(uk, gk)
-            gb_v[place] = dot_tn(uv, gv)
-            return (
-                gq_sum + dot_nt(gq, b_ref[place]),
-                gk_sum + dot_nt(gk, bk[place]),
-                gv_sum + dot_nt(gv, bv[place]),
-            )
-
-        start = (jnp.zeros((share, RANK), F32), jnp.zeros((words, RANK), F32), jnp.zeros((words, RANK), F32))
-        gq_sum, gk_sum, gv_sum = lax.fori_loop(0, count, chunk, start)
-        gq_sum = gq_sum.astype(BF)
-        ga_q[...] = dot_tn(gq_sum, x)
-        ga_k[...] = dot_tn(gk_sum.astype(BF), words_in)
-        ga_v[...] = dot_tn(gv_sum.astype(BF), words_in)
-        g_x = acc[...] + dot_nn(gq_sum, down_of(dtab, 6))
-        normal, inverse = stats(first_ref[...])
-        g_first[...] = (g_second + norm_backward(normal, inverse, g_x * gain[1:2, :])).astype(BF)
-
-    return call(
-        kernel,
-        [(array, True) for array in (g_in, cotangent, first, second, block_in, query, inverses, logs, low, u_low, text)]
-        + [(query_weight, False), (out_weight, False)]
-        + [(array, True) for array in (text_kv, gains, *tables)],
-        [
-            ((share, width), BF, True),
-            ((RANK, width), F32, True),
-            ((count, RANK, local), F32, True),
-            ((RANK, text_width), F32, True),
-            ((count, RANK, local), F32, True),
-            ((RANK, text_width), F32, True),
-            ((count, RANK, local), F32, True),
-            ((count, RANK, local), F32, True),
-            ((RANK, width), F32, True),
-        ],
-        [vmem(share, width, dtype=F32), vmem(count, width, local), vmem(count, width, local)]
-        + [vmem(count, RANK, local) for _ in range(4)] + [dma(2)],
-        cost=cost_of(8 * share * width * width, 20e6),
-    )
-
-
-def attention_backward(count, heads, g_first, attn_in, query, keys, values, low, logs, inv_q, inv_k, weights, tables):
-    share, width = g_first.shape
-    tokens = attn_in.shape[0]
-    local = weights[0].shape[1]
-    block = min(128, tokens)
-    chunk = min(64, tokens)
-    steps = tokens // chunk
-    each = block // chunk
-    scale = HD ** (-0.5)
-
-    def kernel(g_ref, x_ref, q_ref, k_ref, v_ref, low_ref, log_ref, iq_ref, ik_ref, *refs):
-        (wq, wk, wv, wo, dtab, utab, total_out, gall, ga_in, gb_q, gb_k, gb_v, ga_o, gb_o, gq_low, gk_acc,
-         gv_acc, swap_out, swap_in, partial_ref, from_left, from_right, stage_right, stage_left, a_ref, bq, bk,
-         bv, ao, xsend, xrecv, *sems) = refs
+    def kernel(g_ref, b_in, q_ref, k_ref, v_ref, low_ref, log_ref, iq_ref, ik_ref, wo, dtab, utab, gq_low, gk_low, gv_low,
+               gall, ball, ga_o, gb_o, gk_acc, gv_acc, swap_out, swap_in, ao, xsend, xrecv, *sems):
         me = lax.axis_index("tensor")
         core = lax.axis_index("ctx")
         peer = {"ctx": 1 - core}
-        gather_line = Line(me, count, *sems[:4])
-        reduce_line = Line(me, count, *sems[4:])
+        grad_line = Line(me, count, *sems[:4])
+        block_line = Line(me, count, *sems[4:])
         gall[me] = g_ref[...]
-        for ref in (ga_in, gb_q, gb_k, gb_v, ga_o, gb_o, gk_acc, gv_acc):
+        ball[me] = b_in[...]
+        greet(line_partners(me, count) + [(core >= 0, peer)])
+        line_gather_step(grad_line, 0, gall)
+        for ref in (ga_o, gb_o, gk_acc, gv_acc):
             ref[...] = jnp.zeros_like(ref)
-        greet(line_partners(me, count) + [(core >= 0, peer)])
-        line_gather_step(gather_line, 0, gall)
-        for number, target in enumerate((bq, bk, bv)):
-            a_ref[number * RANK : (number + 1) * RANK, :] = down_of(dtab, 2 + number)
-            take_local(target, utab, OUT_AT[2 + number], me, count)
         take_local(ao, dtab, IN_AT[5], me, count)
 
         def attend(place):
@@ -1810,7 +1806,7 @@
                 probs, grads = [], []
                 inner = 0.0
                 for half in range(2):
-                    p = jnp.exp(dot_nt(q, k_ref[half, head]) * scale - log_ref[head, rows, :])
+                    p = jnp.exp(dot_nt(q, k_ref[half, head]) * scale - log_ref[rows, head : head + 1])
                     dp = dot_nt(gh, v_ref[half, head])
                     inner = inner + jnp.sum(p * dp, axis=-1, keepdims=True)
                     probs.append(p)
@@ -1821,13 +1817,17 @@
                     dq = dq + dot_nn(ds, k_ref[half, head])
                     gk_acc[half, head] += dot_tn(ds, q)
                     gv_acc[half, head] += dot_tn(probs[half].astype(BF), gh)
-                parts.append(norm_backward(q.astype(F32), iq_ref[head, rows, :], dq * scale))
+                parts.append(norm_backward(q.astype(F32), iq_ref[rows, head : head + 1], dq * scale))
             gq_low[rows, :] = jnp.concatenate(parts, axis=1).astype(BF)
 
         def gather(number, carry):
             @pl.when(number > 0)
             def _():
-                line_gather_step(gather_line, number, gall)
+                line_gather_step(grad_line, number, gall)
+
+            @pl.when(number == count - 1)
+            def _():
+                line_gather_step(block_line, 0, ball)
 
             def side(which, inner):
                 place = me + (2 * which - 1) * number
@@ -1845,130 +1845,120 @@
         swap_out[1] = gv_acc[1 - core].astype(BF)
         swap = push(swap_out, swap_in, xsend, xrecv, peer)
         swap.start()
-        line_gather_drain(gather_line, gall)
+        line_gather_step(block_line, 1, ball)
+        line_gather_drain(grad_line, gall)
         swap.wait()
 
-        def compute(number):
-            @pl.when(number % each == 0)
-            def _():
-                rows = rows_of(number // each, block)
-                x = x_ref[rows, :]
-                u = dot_nt(x, a_ref[...]).astype(BF)
-                parts_k, parts_v = [], []
-                for head in range(heads):
-                    dk = gk_acc[core, head, rows, :] * scale + swap_in[0, head, rows, :].astype(F32)
-                    normal = k_ref[core, head, rows, :].astype(F32)
-                    parts_k.append(norm_backward(normal, ik_ref[head, rows, :], dk))
-                    parts_v.append(gv_acc[core, head, rows, :] + swap_in[1, head, rows, :].astype(F32))
-                gq = gq_low[rows, :]
-                gk = jnp.concatenate(parts_k, axis=1).astype(BF)
-                gv = jnp.concatenate(parts_v, axis=1).astype(BF)
-                gu = jnp.concatenate([dot_nt(gq, bq[...]), dot_nt(gk, bk[...]), dot_nt(gv, bv[...])], axis=1).astype(BF)
-                y = dot_nt(gq, wq[...]) + dot_nt(gk, wk[...]) + dot_nt(gv, wv[...]) + dot_nn(gu, a_ref[...])
-                y = y.astype(BF)
-                for piece in range(each):
-                    partial_ref[number + piece] = y[piece * chunk : (piece + 1) * chunk]
-                ga_in[...] += dot_tn(gu, x)
-                gb_q[...] += dot_tn(u[:, :RANK], gq)
-                gb_k[...] += dot_tn(u[:, RANK : 2 * RANK], gk)
-                gb_v[...] += dot_tn(u[:, 2 * RANK :], gv)
-
-        def finish(slot, total):
-            total_out[rows_of(slot, chunk), :] = total
-
-        line_reduce_all(
-            reduce_line, steps, compute, partial_ref, from_left, from_right, stage_right, stage_left, finish
-        )
-
-    buffers = [vmem(steps, chunk, width) for _ in range(5)]
+        def keys_back(place, carry):
+            rows = rows_of(place, share)
+            parts_k, parts_v = [], []
+            for head in range(heads):
+                dk = gk_acc[core, head, rows, :] * scale + swap_in[0, head, rows, :].astype(F32)
+                normal = k_ref[core, head, rows, :].astype(F32)
+                parts_k.append(norm_backward(normal, ik_ref[rows, head : head + 1], dk))
+                parts_v.append(gv_acc[core, head, rows, :] + swap_in[1, head, rows, :].astype(F32))
+            gk_low[rows, :] = jnp.concatenate(parts_k, axis=1).astype(BF)
+            gv_low[rows, :] = jnp.concatenate(parts_v, axis=1).astype(BF)
+            return carry
+
+        lax.fori_loop(0, count, keys_back, 0)
+        line_gather_step(block_line, 2, ball)
+        line_gather_step(block_line, 3, ball)
+        line_gather_drain(block_line, ball)
+
     return call(
         kernel,
-        [(array, True) for array in (g_first, attn_in, query, keys, values, low, logs, inv_q, inv_k)]
-        + [(array, True) for array in (*weights, *tables)],
+        [(array, True) for array in (g_first, block_sum, query, keys, values, low, logs, inv_q, inv_k, out_weight, *tables)],
         [
-            ((tokens, width), F32, True),
+            ((tokens, local), BF, True),
+            ((tokens, local), BF, True),
+            ((tokens, local), BF, True),
             ((count, share, width), BF, True),
-            ((3 * RANK, width), F32, True),
-            ((RANK, local), F32, True),
-            ((RANK, local), F32, True),
-            ((RANK, local), F32, True),
+            ((count, share, width), BF, True),
             ((RANK, local), F32, True),
             ((RANK, width), F32, True),
         ],
-        [vmem(tokens, local), vmem(2, heads, tokens, HD, dtype=F32), vmem(2, heads, tokens, HD, dtype=F32)]
-        + [vmem(2, heads, tokens, HD), vmem(2, heads, tokens, HD)]
-        + buffers + [vmem(3 * RANK, width)] + [vmem(RANK, local) for _ in range(4)] + [dma(), dma()] + [dma(count) for _ in range(4)] + [dma(steps) for _ in range(4)],
+        [vmem(2, heads, tokens, HD, dtype=F32), vmem(2, heads, tokens, HD, dtype=F32), vmem(2, heads, tokens, HD),
+         vmem(2, heads, tokens, HD), vmem(RANK, local), dma(), dma()]
+        + [dma(count) for _ in range(8)],
         collective=4,
         cost=cost_of(16 * tokens * width * local, 60e6),
     )
 
 
-def back_end(count, g_attn, g_first, skip_out, hidden, long_skip, weight, mod_weight, gain_halves, gain_rows, tables,
-             condition, act_all, wide_grads, local_down, local_up, stacked):
+EARLY_A, EARLY_B = IN_AT[2], OUT_AT[2]
+EARLY = IN_AT[12] - EARLY_A + OUT_AT[12] - EARLY_B
+LATE = EARLY_A + EARLY_B
+
+
+def back_end(count, grads, projections, attn_in, g_first, skip_out, hidden, long_skip, weight, mod_weight, gain_halves,
+             gain_rows, tables, condition, act_all, wide_grads, local_down, local_up, stacked):
     tokens, width = hidden.shape
+    local = grads[0].shape[1]
     span = weight.shape[-1]
     block = tokens // count
+    chunk = min(64, block)
+    each = block // chunk
+    steps = tokens // chunk
     own_rows = RANK // count
-    columns = IN_AT[12] + OUT_AT[12]
-    half = -(-columns // 256) * 128
+    half_e = -(-EARLY // 256) * 128
+    half_l = -(-LATE // 256) * 128
+    base = IN_AT[12] - EARLY_A
     mod_rows = mod_weight.shape[0]
-    wide_at, wide = list(wide_grads), list(wide_grads.values())
-    local_at = [number for number in local_down] + [IN_AT[12] + number for number in local_up]
-    local = list(local_down.values()) + list(local_up.values())
-    stacked_at, stack = list(stacked), list(stacked.values())
-
-    def kernel(g_ref, gf_ref, skip_ref, hid, lsk, hbm_w, wm, gains, gain, dtab, utab, cond, act_ref, *refs):
+
+    def early(column):
+        return column - EARLY_A if column < IN_AT[12] else column - EARLY_A - EARLY_B
+
+    wide_at, wide = [early(column) for column in wide_grads], list(wide_grads.values())
+    local_at = [early(column) for column in local_down] + [early(IN_AT[12] + column) for column in local_up]
+    own_grads = list(local_down.values()) + list(local_up.values())
+    stacked_at, stack = [early(column) for column in stacked], list(stacked.values())
+
+    def kernel(gq, gk, gv, wq, wk, wv, x_ref, gf_ref, skip_ref, hid, lsk, hbm_w, wm, gains, gain, dtab, utab, cond, act_ref,
+               *refs):
         wide_refs, refs = refs[: len(wide)], refs[len(wide) :]
-        local_refs, refs = refs[: len(local)], refs[len(local) :]
+        own_refs, refs = refs[: len(own_grads)], refs[len(own_grads) :]
         stack_refs, refs = refs[: len(stack)], refs[len(stack) :]
-        (out_h, out_l, out_a, out_b, out_c, w, buf_h, buf_l, low, table, swap_out, swap_in, partial_ref, from_left,
-         from_right, stage_right, stage_left, summed, slots, other_out, other_in, shifts, shift_in, act_out, act_in, g_act,
-         wsem, osem, ssem, rsem, dsend, drecv, msend, mrecv, *sems) = refs
+        (out_h, out_l, out_a, out_b, out_c, w, buf_h, buf_l, low, g_ref, qkv_a, bq, bk, bv, partial_g, left_g, right_g,
+         sr_g, sl_g, table, late, swap_out, swap_in, partial_e, left_e, right_e, sr_e, sl_e, summed, late_out, late_in,
+         partial_l, slots_l, slots, other_out, other_in, shifts, shift_in, act_out, act_in, g_act, g_sum,
+         wsem, osem, ssem, rsem, dsend, drecv, msend, mrecv, zsend, zrecv, *sems) = refs
         me = lax.axis_index("tensor")
         core = lax.axis_index("ctx")
         dp = lax.axis_index("dp")
         peer = {"ctx": 1 - core}
-        line = Line(me, count, *sems)
+        grad_line = Line(me, count, *sems[:4])
+        early_line = Line(me, count, *sems[4:])
         peers = [{"dp": xor_place(dp, number)} for number in (1, 2, 3)]
+        z_peers = [{"tensor": xor_place(me, number)} for number in range(1, count)]
         load = pltpu.make_async_copy(hbm_w, w, wsem)
         load.start()
-        greet(line_partners(me, count) + [(core >= 0, peer)] + [(core >= 0, device) for device in peers])
-
-        g_shift = jnp.sum(g_ref[...], axis=0, keepdims=True)
-        shift_in[0] = g_shift
-        swap_shift = push(shift_in.at[0], shift_in.at[1], ssem.at[2], rsem.at[2], peer)
-        swap_shift.start()
-        act = act_ref[dp, :, :width]
-        act_low = act.astype(BF)
-        mod_u = dot_nt(act_low, down_of(dtab, 1))
-        once = jnp.where(me == 0, 1.0, 0.0)
-        shift_u = dot_nt(g_shift.astype(BF), up_of(utab, 1))
-        mod_a = jnp.concatenate([shift_u * once, jnp.zeros((7, RANK), F32)], axis=0).astype(BF)
-        mod_b = jnp.concatenate([mod_u * once, jnp.zeros((7, RANK), F32)], axis=0).astype(BF)
-        act_pad = jnp.concatenate([act_low.astype(F32), jnp.zeros((7, width), F32)], axis=0).astype(BF)
-        shift_pad = jnp.concatenate([g_shift, jnp.zeros((7, width), F32)], axis=0).astype(BF)
-
-        table[...] = jnp.zeros_like(table)
-        table[:, IN_AT[1] : IN_AT[2]] = dot_tn(mod_a, act_pad)
-        table[:, IN_AT[12] + OUT_AT[1] : IN_AT[12] + OUT_AT[2]] = dot_tn(mod_b, shift_pad)
-        for start, ref in zip(wide_at, wide_refs):
-            table[:, start : start + ref.shape[1]] = ref[...]
-        for start, ref in zip(stacked_at, stack_refs):
-            size = ref.shape[2]
-            for place in range(count):
-                table[:, start + place * size : start + (place + 1) * size] = ref[place]
-        for place in range(count):
-            @pl.when(me == place)
-            def _(place=place):
-                for start, ref in zip(local_at, local_refs):
-                    size = ref.shape[1]
-                    table[:, start + place * size : start + (place + 1) * size] = ref[...]
-
-        load.wait()
-
-        def skip_block(number, own):
+        greet([(core >= 0, device) for device in z_peers + peers + [peer]])
+        for number, target in enumerate((bq, bk, bv)):
+            qkv_a[number * RANK : (number + 1) * RANK, :] = down_of(dtab, 2 + number)
+            take_local(target, utab, OUT_AT[2 + number], me, count)
+        g_sum[...] = jnp.zeros_like(g_sum)
+        act_low = act_ref[dp, :, :width].astype(BF)
+
+        def compute(number):
+            @pl.when(number % each == 0)
+            def _():
+                rows = rows_of(number // each, block)
+                gu = jnp.concatenate(
+                    [dot_nt(gq[rows, :], bq[...]), dot_nt(gk[rows, :], bk[...]), dot_nt(gv[rows, :], bv[...])], axis=1
+                ).astype(BF)
+                y = dot_nt(gq[rows, :], wq[...]) + dot_nt(gk[rows, :], wk[...]) + dot_nt(gv[rows, :], wv[...])
+                y = (y + dot_nn(gu, qkv_a[...])).astype(BF)
+                for piece in range(each):
+                    partial_g[number + piece] = y[piece * chunk : (piece + 1) * chunk]
+
+        def finish(slot, total):
+            g_ref[rows_of(slot, chunk), :] = total
+
+        def skip_block(number):
             rows = rows_of(number, block)
             ga_in = g_ref[rows, :]
+            g_sum[...] += jnp.sum(ga_in, axis=0, keepdims=True)
             normal, inverse = stats(skip_ref[rows, :])
             g_low = (
                 gf_ref[number].astype(F32) + norm_backward(normal, inverse, ga_in * gain[0:1, :])
@@ -1985,14 +1975,14 @@
             gu = dot_nt(g_low, up_of(utab, 0)).astype(BF)
             a_left, a_right = dtab[:, :width], dtab[:, width : 2 * width]
 
-            @pl.when(own)
+            @pl.when(number == me)
             def _():
                 low_l = (left * gains[0:1, :]).astype(BF)
                 low_r = (right * gains[1:2, :]).astype(BF)
                 u = (dot_nt(low_l, a_left) + dot_nt(low_r, a_right)).astype(BF)
-                table[:, :width] = dot_tn(gu, low_l)
-                table[:, width : 2 * width] = dot_tn(gu, low_r)
-                table[:, IN_AT[12] : IN_AT[12] + width] = dot_tn(u, g_low)
+                late[:, :width] = dot_tn(gu, low_l)
+                late[:, width : 2 * width] = dot_tn(gu, low_r)
+                late[:, EARLY_A : EARLY_A + width] = dot_tn(u, g_low)
 
             for place in range(count):
                 low[:, place * span : (place + 1) * span] = dot_nn(g_low, w[place])
@@ -2008,34 +1998,46 @@
             pltpu.make_async_copy(buf_l.at[number], out_l.at[rows, :], osem.at[1, number]).start()
 
         swap = push(swap_out, swap_in, ssem.at[0], rsem.at[0], peer)
-        shift_sends = [
-            push(shifts.at[dp], shifts.at[dp], msend.at[0, number], mrecv.at[0, number], device)
-            for number, device in enumerate(peers)
-        ]
-        act_sends = [
-            push(act_out.at[xor_place(dp, number)], act_in.at[dp], msend.at[1, number - 1], mrecv.at[1, number - 1],
-                 peers[number - 1])
-            for number in (1, 2, 3)
-        ]
-
-        def step(number, carry):
-            place = lax.rem(me + number, count)
-            skip_block(place, number == 0)
-
-            @pl.when(number == 0)
-            def _():
+
+        def early_step(number):
+            line_scatter_step(early_line, number, partial_e, left_e, right_e, sr_e, sl_e)
+
+        def beside(number):
+            @pl.when(number == 1)
+            def _():
+                load.wait()
+                x = x_ref[...]
+                u = dot_nt(x, qkv_a[...]).astype(BF)
+                table[...] = jnp.zeros_like(table)
+                late[...] = jnp.zeros_like(late)
+                for start, ref in zip(wide_at, wide_refs):
+                    table[:, start : start + ref.shape[1]] = ref[...]
+                for start, ref in zip(stacked_at, stack_refs):
+                    size = ref.shape[2]
+                    for place in range(count):
+                        table[:, start + place * size : start + (place + 1) * size] = ref[place]
+                qkv_b = []
+                for which, (grad, factor) in enumerate(((gq, bq), (gk, bk), (gv, bv))):
+                    gu = dot_nt(grad[...], factor[...]).astype(BF)
+                    table[:, which * width : (which + 1) * width] = dot_tn(gu, x)
+                    qkv_b.append(dot_tn(u[:, which * RANK : (which + 1) * RANK], grad[...]))
+                for place in range(count):
+                    @pl.when(me == place)
+                    def _(place=place):
+                        for which, piece in enumerate(qkv_b):
+                            start = base + which * width + place * local
+                            table[:, start : start + local] = piece
+                        for start, ref in zip(local_at, own_refs):
+                            size = ref.shape[1]
+                            table[:, start + place * size : start + (place + 1) * size] = ref[...]
                 for which in range(2):
                     @pl.when(core == which)
                     def _(which=which):
-                        swap_out[...] = table[:, (1 - which) * half : (2 - which) * half].astype(BF)
+                        swap_out[...] = table[:, (1 - which) * half_e : (2 - which) * half_e].astype(BF)
 
                 swap.start()
-                swap_shift.wait()
-                shifts[dp] = shift_in[0] + shift_in[1]
-                for send in shift_sends:
-                    send.start()
-
-            @pl.when(number == 1)
+
+            @pl.when(number == 3)
             def _():
                 swap.wait()
                 for which in range(2):
@@ -2043,28 +2045,90 @@
                     def _(which=which):
                         for part in range(count):
                             at = slice(part * own_rows, (part + 1) * own_rows)
-                            mine = table[at, which * half : (which + 1) * half]
-                            partial_ref[part] = (mine + swap_in[at, :].astype(F32)).astype(BF)
-
-                for other in (1, 2, 3):
-                    source = shifts.at[xor_place(dp, other)]
-                    push(source, source, msend.at[0, other - 1], mrecv.at[0, other - 1], peers[other - 1]).wait_recv()
-                every = jnp.concatenate([shifts[sequence] for sequence in range(4)], axis=0).astype(BF)
-                products = dot_nt(every, wm[...])
-                for sequence in range(4):
-                    act_out[sequence] = products[sequence : sequence + 1]
-                for send in act_sends:
-                    send.start()
-
-            @pl.when((number >= 1) & (number < count))
-            def _():
-                line_scatter_step(line, number - 1, partial_ref, from_left, from_right, stage_right, stage_left)
-
-            return carry
-
-        lax.fori_loop(0, count, step, 0)
-        line_scatter_finish(line, partial_ref, from_left, from_right, stage_right, stage_left, summed)
-        slots[dp] = summed[...].astype(BF)
+                            mine = table[at, which * half_e : (which + 1) * half_e]
+                            partial_e[part] = (mine + swap_in[at, :].astype(F32)).astype(BF)
+
+            @pl.when((number >= steps) & (number < steps + count - 1))
+            def _():
+                early_step(number - steps)
+
+        def after(slot):
+            @pl.when(slot % each == each - 1)
+            def _():
+                skip_block(slot // each)
+
+        line_reduce_all(
+            grad_line, steps, compute, partial_g, left_g, right_g, sr_g, sl_g, finish, beside, after
+        )
+
+        g_shift = g_sum[...]
+        shift_in[0] = g_shift
+        swap_shift = push(shift_in.at[0], shift_in.at[1], ssem.at[2], rsem.at[2], peer)
+        swap_shift.start()
+        mod_u = dot_nt(act_low, down_of(dtab, 1))
+        once = jnp.where(me == 0, 1.0, 0.0)
+        shift_u = dot_nt(g_shift.astype(BF), up_of(utab, 1))
+        zeros_u, zeros_w = jnp.zeros((7, RANK), F32), jnp.zeros((7, width), F32)
+        mod_a = jnp.concatenate([shift_u * once, zeros_u], axis=0).astype(BF)
+        mod_b = jnp.concatenate([mod_u * once, zeros_u], axis=0).astype(BF)
+        act_pad = jnp.concatenate([act_low.astype(F32), zeros_w], axis=0).astype(BF)
+        shift_pad = jnp.concatenate([g_shift, zeros_w], axis=0).astype(BF)
+        late[:, IN_AT[1] : IN_AT[2]] = dot_tn(mod_a, act_pad)
+        late[:, EARLY_A + OUT_AT[1] : EARLY_A + OUT_AT[2]] = dot_tn(mod_b, shift_pad)
+        for which in range(2):
+            @pl.when(core == which)
+            def _(which=which):
+                late_out[...] = late[:, (1 - which) * half_l : (2 - which) * half_l].astype(BF)
+
+        swap_late = push(late_out, late_in, ssem.at[1], rsem.at[1], peer)
+        swap_late.start()
+        swap_shift.wait()
+        shifts[dp] = shift_in[0] + shift_in[1]
+        shift_sends = [
+            push(shifts.at[dp], shifts.at[dp], msend.at[0, number], mrecv.at[0, number], device)
+            for number, device in enumerate(peers)
+        ]
+        for send in shift_sends:
+            send.start()
+        swap_late.wait()
+        for which in range(2):
+            @pl.when(core == which)
+            def _(which=which):
+                for part in range(count):
+                    at = slice(part * own_rows, (part + 1) * own_rows)
+                    mine = late[at, which * half_l : (which + 1) * half_l]
+                    partial_l[part] = (mine + late_in[at, :].astype(F32)).astype(BF)
+
+        late_sends = [
+            push(partial_l.at[xor_place(me, number + 1)], slots_l.at[me], zsend.at[number], zrecv.at[number], device)
+            for number, device in enumerate(z_peers)
+        ]
+        for send in late_sends:
+            send.start()
+        slots_l[me] = partial_l[me]
+        for number in (1, 2, 3):
+            source = shifts.at[xor_place(dp, number)]
+            push(source, source, msend.at[0, number - 1], mrecv.at[0, number - 1], peers[number - 1]).wait_recv()
+        every = jnp.concatenate([shifts[sequence] for sequence in range(4)], axis=0).astype(BF)
+        products = dot_nt(every, wm[...])
+        for sequence in range(4):
+            act_out[sequence] = products[sequence : sequence + 1]
+        act_sends = [
+            push(act_out.at[xor_place(dp, number)], act_in.at[dp], msend.at[1, number - 1], mrecv.at[1, number - 1],
+                 peers[number - 1])
+            for number in (1, 2, 3)
+        ]
+        for send in act_sends:
+            send.start()
+        line_scatter_finish(early_line, partial_e, left_e, right_e, sr_e, sl_e, summed)
+        slots[dp, :, :half_e] = summed[...].astype(BF)
+        for number in range(count - 1):
+            arrived = slots_l.at[xor_place(me, number + 1)]
+            push(arrived, arrived, zsend.at[number], zrecv.at[number], z_peers[number]).wait_recv()
+        late_sum = slots_l[0].astype(F32)
+        for place in range(1, count):
+            late_sum = late_sum + slots_l[place].astype(F32)
+        slots[dp, :, half_e:] = late_sum.astype(BF)
         sends = [
             push(slots.at[dp], slots.at[dp], dsend.at[number], drecv.at[number], device)
             for number, device in enumerate(peers)
@@ -2090,14 +2154,14 @@
 
         def total(which):
             slot = (dp * 2 + which).astype(F32)
-            result = jnp.zeros((own_rows, half), F32)
+            result = jnp.zeros((own_rows, half_e + half_l), F32)
             for sequence in range(4):
                 chosen = jnp.where(act_ref[sequence, :, width : width + 1] == slot, 1.0, 0.0)
                 result = result + slots[sequence].astype(F32) * chosen
             return result
 
         other_out[...] = total(1 - core).astype(BF)
-        last = push(other_out, other_in, ssem.at[1], rsem.at[1], peer)
+        last = push(other_out, other_in, ssem.at[3], rsem.at[3], peer)
         last.start()
         mine = total(core)
         last.wait_recv()
@@ -2106,13 +2170,15 @@
             @pl.when(core == which)
             def _(which=which):
                 both = (mine, other) if which == 0 else (other, mine)
-                cut = IN_AT[12]
-                whole = jnp.concatenate(both, axis=1)
-                out_a[...] = whole[:, :cut]
-                out_b[...] = whole[:, cut:columns]
+                first = jnp.concatenate([piece[:, :half_e] for piece in both], axis=1)
+                second = jnp.concatenate([piece[:, half_e:] for piece in both], axis=1)
+                out_a[:, :EARLY_A] = second[:, :EARLY_A]
+                out_a[:, EARLY_A:] = first[:, :base]
+                out_b[:, :EARLY_B] = second[:, EARLY_A:LATE]
+                out_b[:, EARLY_B:] = first[:, base:EARLY]
 
         last.wait_send()
-        for send in sends + shift_sends + act_sends:
+        for send in sends + shift_sends + act_sends + late_sends:
             send.wait_send()
 
         def drain(number, carry):
@@ -2123,12 +2189,14 @@
 
         lax.fori_loop(0, count, drain, 0)
 
-    part = (own_rows, half)
+    part_e = (own_rows, half_e)
+    part_l = (own_rows, half_l)
+    part = (own_rows, half_e + half_l)
     return call(
         kernel,
-        [(array, True) for array in (g_attn, g_first, skip_out, hidden, long_skip)]
+        [(array, True) for array in (*grads, *projections, attn_in, g_first, skip_out, hidden, long_skip)]
         + [(weight, False)]
-        + [(array, True) for array in (mod_weight, gain_halves, gain_rows, *tables, condition, act_all, *wide, *local,
+        + [(array, True) for array in (mod_weight, gain_halves, gain_rows, *tables, condition, act_all, *wide, *own_grads,
                                        *stack)],
         [
             ((tokens, width), F32, False),
@@ -2142,15 +2210,19 @@
             vmem(count, block, width, dtype=F32),
             vmem(count, block, width, dtype=F32),
             vmem(block, 2 * width, dtype=F32),
-            vmem(RANK, 2 * half, dtype=F32),
-            vmem(RANK, half),
-            vmem(RANK, half),
+            vmem(tokens, width, dtype=F32),
+            vmem(3 * RANK, width),
+            vmem(RANK, local), vmem(RANK, local), vmem(RANK, local),
         ]
-        + [vmem(count, *part) for _ in range(5)]
-        + [vmem(*part, dtype=F32), vmem(4, *part), vmem(*part), vmem(*part)]
+        + [vmem(steps, chunk, width) for _ in range(5)]
+        + [vmem(RANK, 2 * half_e, dtype=F32), vmem(RANK, 2 * half_l, dtype=F32), vmem(RANK, half_e), vmem(RANK, half_e)]
+        + [vmem(count, *part_e) for _ in range(5)]
+        + [vmem(*part_e, dtype=F32), vmem(RANK, half_l), vmem(RANK, half_l), vmem(count, *part_l), vmem(count, *part_l)]
+        + [vmem(4, *part), vmem(*part), vmem(*part)]
         + [vmem(4, 1, width, dtype=F32), vmem(2, 1, width, dtype=F32), vmem(4, 1, mod_rows, dtype=F32),
-           vmem(4, 1, mod_rows, dtype=F32), vmem(1, width, dtype=F32)]
-        + [dma(), dma(2, count), dma(3), dma(3), dma(3), dma(3), dma(2, 3), dma(2, 3)] + [dma(count) for _ in range(4)],
+           vmem(4, 1, mod_rows, dtype=F32), vmem(1, width, dtype=F32), vmem(1, width, dtype=F32)]
+        + [dma(), dma(2, count), dma(4), dma(4), dma(3), dma(3), dma(2, 3), dma(2, 3), dma(count), dma(count)]
+        + [dma(steps) for _ in range(4)] + [dma(count) for _ in range(4)],
         collective=5,
         cost=cost_of(4 * tokens * width * width, 30e6),
     )
@@ -2208,35 +2280,29 @@
         "dn": feedforward_down_weight.T,
     }
     (skip_out, attn_in, query, keys, values, low, logs, inv_q, inv_k, summed, act_all, text_kv, wq, wk, wv, wo, wcq, wco,
-     wup, wdn) = front(
+     wup) = front(
         count, heads, condition, sequence_adapter_index, hidden, long_skip, text, weights, shift_modulation_weight,
         gain_halves, norm_gain_rows, tables,
     )
-    first, second, cross_in, mlp_in, cquery, cinv, clogs, clow, cu, skip_half = cross_forward(
-        count, heads, summed, skip_out, wcq, wco, weights["skip"], text_kv, norm_gain_rows, tables
-    )
-    g_mlp_in, down_part, g_up_a, g_up_b, g_down_a, g_down_b, skip_all = feed_forward(
-        count, mlp_in, cot, second, wup, wdn, skip_half, tables
-    )
-    block_out = lax.psum(down_part, "tensor")
-    g_first, g_cq_a, g_cq_b, g_ck_a, g_ck_b, g_cv_a, g_cv_b, g_co_a, g_co_b = cross_backward(
-        count, heads, g_mlp_in, cot, first, second, cross_in, cquery, cinv, clogs, clow, cu, text, wcq, wco, text_kv,
-        norm_gain_rows, tables,
-    )
-    g_attn, g_first_all, g_qkv_a, g_q_b, g_k_b, g_v_b, g_o_a, g_o_b = attention_backward(
-        count, heads, g_first, attn_in, query, keys, values, low, logs, inv_q, inv_k, (wq, wk, wv, wo), tables
-    )
+    (g_first, block_sum, g_cq_a, g_cq_b, g_ck_a, g_ck_b, g_cv_a, g_cv_b, g_co_a, g_co_b, g_up_a, g_up_b, g_down_a, g_down_b,
+     skip_all) = middle(
+        count, heads, summed, skip_out, wcq, wco, wup, weights["dn"], weights["skip"], text_kv, text, cot, norm_gain_rows,
+        tables,
+    )
+    gq, gk, gv, g_first_all, block_all, g_o_a, g_o_b = attention_backward(
+        count, heads, g_first, block_sum, query, keys, values, low, logs, inv_q, inv_k, wo, tables
+    )
+    block_out = block_all.reshape(hidden.shape)
     base = IN_AT[12]
     hidden_grad, skip_grad, grad_down, grad_up, g_condition = back_end(
-        count, g_attn, g_first_all, skip_out, hidden, long_skip, skip_all, shift_modulation_weight, gain_halves,
-        norm_gain_rows, tables, condition, act_all,
+        count, (gq, gk, gv), (wq, wk, wv), attn_in, g_first_all, skip_out, hidden, long_skip, skip_all,
+        shift_modulation_weight, gain_halves, norm_gain_rows, tables, condition, act_all,
         {
             IN_AT[6]: g_cq_a, IN_AT[7]: g_ck_a, IN_AT[8]: g_cv_a, IN_AT[10]: g_up_a,
-            IN_AT[2]: g_qkv_a[:RANK], IN_AT[3]: g_qkv_a[RANK : 2 * RANK], IN_AT[4]: g_qkv_a[2 * RANK :],
             base + OUT_AT[5]: g_o_b, base + OUT_AT[9]: g_co_b, base + OUT_AT[11]: g_down_b,
         },
         {IN_AT[5]: g_o_a, IN_AT[11]: g_down_a},
-        {OUT_AT[2]: g_q_b, OUT_AT[3]: g_k_b, OUT_AT[4]: g_v_b, OUT_AT[10]: g_up_b},
+        {OUT_AT[10]: g_up_b},
         {
             IN_AT[9]: g_co_a, base + OUT_AT[6]: g_cq_b, base + OUT_AT[7]: g_ck_b, base + OUT_AT[8]: g_cv_b,
         },

time: 503 us -> 420 us (0.83)
  Pallas kernels: 457 us -> 391 us
  between operations: 15.3 us -> 1.88 us
    pallas_call x6 -> x4, Pallas kernels: 457 us -> 391 us  [call(): pl.pallas_call(kernel, out_shape=[jax.ShapeDtypeStruct(shape, dtype) for...]
  transfers between devices with their start and end apart: 1 -> 0, of which waited for: 0 -> 0; matrix products, arithmetic and copies ran while one was open for 1% -> 0% of each run, Pallas kernels for 37% -> 0%
where the time goes in v4:
time: 420 us; the launch traced here: 413 us
  Pallas kernels  391 us (93%)
  local copies, waits for them, and re-layouts  19.7 us (5%)
    pallas_call x4, Pallas kernels, call(): pl.pallas_call(kernel, out_shape=[jax.ShapeDtypeStruct(shape, dtype) for...  391 us
    unnamed x18, local copies, waits for them, and re-layouts  9.83 us

profile of v4, /device:TPU:0, one launch (start us, length us, event | category | flops | bytes accessed | tf_op | source)
XLA Modules:
  0.0 412.6 jit_solution(10733691100797669271)
XLA Ops:
  0.6 0.0 copy-start.2
  0.6 0.0 copy-start.5
  0.7 0.0 copy-start.3
  1.4 0.0 copy-start.4
  1.4 2.1 dynamic-slice_bitcast_fusion.dtab
  3.5 2.0 dynamic-slice_bitcast_fusion.1.utab
  5.4 0.0 copy-done.2
  5.4 1.1 copy.28
  6.5 0.0 copy-done.5
  6.5 0.6 reshape.22.halves.gains
  7.1 0.0 copy-done.3
  7.1 0.9 copy.29
  8.0 0.0 copy-done.4
  8.0 0.9 copy.30
  8.9 132.2 %shard_map.253 = (f32[512,1408]{1,0:T(8,128)}, bf16[512,1408]{1,0:T(8,128)(2,1)}, bf16[4,512,88]{2,1,0:T(8,128)(2,1)}, bf16[2,4,512,88]{3,2,1,0:T(8,128)(2,1)}, ...) custom-call(bf16[352,704]{1,0:T(8,128)(2,1)} %bitcast.28, ...), custom_call_target="tpu_custom_call" | custom-call | flops 2030043136 | bytes 60000000 | tf_op jit(solution)/shard_map/pallas_call | solution.py:923
  141.1 111.5 %shard_map.254 = (bf16[128,1408]{1,0:T(8,128)(2,1)}, bf16[128,1408]{1,0:T(8,128)(2,1)}, f32[16,1408]{1,0:T(8,128)}, f32[4,16,352]{2,1,0:T(8,128)}, f32[16,1024]{...) custom-call(f32[128,1408]{1,0:T(8,128)} %get-tuple-element.52.sum_re, ...), custom_call_target="tpu_custom_call" | custom-call | flops 13287555072 | bytes 60000000 | tf_op jit(solution)/shard_map/pallas_call | solution.py:923
  252.6 61.2 %shard_map.255 = (bf16[512,352]{1,0:T(8,128)(2,1)}, bf16[512,352]{1,0:T(8,128)(2,1)}, bf16[512,352]{1,0:T(8,128)(2,1)}, bf16[4,128,1408]{2,1,0:T(8,128)(2,1)}, b...) custom-call(bf16[128,1408]{1,0:T(8,128)(2,1)} %get-tuple-element.58.g_ref, ...), custom_call_target="tpu_custom_call" | custom-call | flops 4060086272 | bytes 60000000 | tf_op jit(solution)/shard_map/pallas_call | solution.py:923
  313.8 86.2 %shard_map.256 = (f32[512,1408]{1,0:T(8,128)}, f32[512,1408]{1,0:T(8,128)}, f32[4,22272]{1,0:T(4,128)}, f32[4,21632]{1,0:T(4,128)}, f32[1,1408]{1,0:T(1,128)}) custom-call(bf16[512,352]{1,0:T(8,128)(2,1)} %get-tuple-element.69.gq, bf16[512,352]{1,0:T(8,128)(2,1)} %get-tuple-element.70.gk, bf16[512,352]{1,0:T(8,128)(2,1)} %get-tuple-element.71.gv, ...), custom_call_target="tpu_custom_call" | custom-call | flops 4060086272 | bytes 30000000 | tf_op jit(solution)/shard_map/pallas_call | solution.py:923
  400.0 0.0 copy-start.1
  400.0 2.0 reshape.23
  402.0 1.8 reshape.24
  403.8 1.3 constant_dynamic-slice_fusion
  405.1 2.6 copy.35
  407.7 0.0 copy-done.1
  407.7 0.0 copy-start
  407.7 1.6 copy.36
  409.3 1.3 copy-done
  410.6 1.6 copy.37
Async XLA Ops:
  0.6 4.8 %copy-start.2 = (bf16[704,352]{1,0:T(8,128)(2,1)S(1)}, bf16[704,352]{1,0:T(8,128)(2,1)}, u32[]{:S(2)}) copy-start(bf16[704,352]{1,0:T(8,128)(2,1)} %param.27) | copy-start | bytes 1486852
  0.6 5.9 %copy-start.5 = (f32[2816]{0:T(1024)S(1)}, f32[2816]{0:T(1024)}, u32[]{:S(2)}) copy-start(f32[2816]{0:T(1024)} %param.39) | copy-start | bytes 33796
  0.7 6.5 %copy-start.3 = (bf16[352,352]{1,0:T(8,128)(2,1)S(1)}, bf16[352,352]{1,0:T(8,128)(2,1)}, u32[]{:S(2)}) copy-start(bf16[352,352]{1,0:T(8,128)(2,1)} %param.32) | copy-start | bytes 743428
  1.4 6.6 %copy-start.4 = (bf16[352,352]{1,0:T(8,128)(2,1)S(1)}, bf16[352,352]{1,0:T(8,128)(2,1)}, u32[]{:S(2)}) copy-start(bf16[352,352]{1,0:T(8,128)(2,1)} %param.36) | copy-start | bytes 743428
  400.0 7.7 %copy-start.1 = (f32[512,1408]{1,0:T(8,128)S(1)}, f32[512,1408]{1,0:T(8,128)}, u32[]{:S(2)}) copy-start(f32[512,1408]{1,0:T(8,128)} %get-tuple-element.93) | copy-start | bytes 8650756
  407.7 2.9 copy-start
